TPU v7x, 256 devices: a whole 4x4x8 slice. The times are simulated.
256 devices in a mesh: seq: 64 (over x, z, core), head: 4 (over y).
Axes of the slice: x: 4, y: 4, z: 8, core: 2. Of those that a mesh axis runs over, the one named last changes fastest.
Arguments:
- queries: bfloat16 [16384, 4096], P('seq', 'head'), may hold values from -4 to 4
- key_rows: bfloat16 [16384, 4096], P('seq', 'head'), may hold values from -4 to 4
- value_rows: bfloat16 [16384, 4096], P('seq', 'head'), may hold values from -28 to 28
- norm_gain: float32 [4096], P('head'), may hold values from 0.1 to 1.9
- out_grad: bfloat16 [16384, 4096], P('seq', 'head'), may hold values from -4 to 4
Outputs:
- normed: bfloat16 [16384, 4096], P('seq', 'head')
- query_grad: bfloat16 [16384, 4096], P('seq', 'head')
- key_grad: bfloat16 [16384, 4096], P('seq', 'head')
- value_grad: bfloat16 [16384, 4096], P('seq', 'head')
All inputs are finite; a program needn't handle non-finite values.
Results may differ from a plain program's by a relative error of at most 0.0017.
The roundings to bfloat16 on the way count: a program that leaves them out, or rounds other values in their place, can miss the bound.
Values sent between devices are 32-bit elements; how exact they have to be, the bound alone decides.
No kernel may reach another device: no remote copies, remote signals or barrier semaphores. Data moves between devices by JAX's collectives and lax.ppermute only.
A program may use at most 192 MiB of HBM per device.

v0:
```python
import functools

import jax
import jax.numpy as jnp
from jax import lax
from jax.experimental import pallas as pl
from jax.experimental.pallas import tpu as pltpu
from jax.sharding import Mesh
from jax.sharding import PartitionSpec as P

HEADS = 32
HEAD_DIM = 128
CORES = 2
ROWS = 16

highest = lax.Precision.HIGHEST


def feature(values):
    return jnp.where(values > 0, values + 1.0, jnp.exp(jnp.minimum(values, 0.0)))


def feature_slope(values):
    return jnp.where(values > 0, jnp.ones_like(values), jnp.exp(jnp.minimum(values, 0.0)))


def swap_cores(array):
    return lax.ppermute(array, "core", [(0, 1), (1, 0)])


def to_wire(state, row, chips):
    half = state.shape[0] // CORES
    state = state.reshape(CORES, chips, ROWS, HEAD_DIM)
    row = row.reshape(CORES, half, 1, 1, HEAD_DIM)
    row = jnp.pad(row, ((0, 0), (0, 0), (0, chips // half - 1), (0, 0), (0, 0)))
    return jnp.concatenate([state, row.reshape(CORES, chips, 1, HEAD_DIM)], axis=2)


def from_wire(wire, heads):
    chips = wire.shape[1]
    state = wire[:, :, :ROWS].reshape(heads, HEAD_DIM, HEAD_DIM)
    row = wire[:, :, ROWS].reshape(heads, (chips * CORES) // heads, HEAD_DIM)[:, 0]
    return state, row


def chip_sums_kernel(backward, spread, sums):
    chips = spread.shape[0]
    total = jnp.zeros(spread.shape[1:], jnp.float32)
    for step in range(chips):
        chip = chips - 1 - step if backward else step
        sums[chip] = total
        if step < chips - 1:
            total = total + spread[chip]


def chip_sums(spread, backward):
    return pl.pallas_call(
        functools.partial(chip_sums_kernel, backward),
        out_shape=jax.ShapeDtypeStruct(spread.shape, jnp.float32),
        name="chip_sums",
    )(spread)


def scan_states(state, row, backward):
    chips = lax.axis_size("chip")
    core = lax.axis_index("core")
    heads = state.shape[0]
    mine = to_wire(state, row, chips)
    other = swap_cores(mine)
    pair = lax.dynamic_index_in_dim(mine + other, core, 0, False)
    spread = lax.all_to_all(pair, "chip", 0, 0)
    kept = lax.all_to_all(chip_sums(spread, backward), "chip", 0, 0)
    got = swap_cores(kept)
    first = jnp.where(core == 0, kept, got)
    second = jnp.where(core == 0, got, kept)
    adds = (core == 0) if backward else (core == 1)
    out = jnp.stack([first, second]) + jnp.where(adds, other, 0.0)
    return from_wire(out, heads)


def heads_major(array, heads_here):
    return array.reshape(array.shape[0], heads_here, HEAD_DIM).transpose(1, 0, 2)


def tokens_major(array):
    return array.transpose(1, 0, 2).reshape(array.shape[1], -1)


def body(queries, key_rows, value_rows, norm_gain, out_grad):
    width = HEADS * HEAD_DIM
    tokens = queries.shape[0]
    heads_here = norm_gain.shape[0] // HEAD_DIM
    query_raw = heads_major(queries, heads_here).astype(jnp.float32)
    key_raw = heads_major(key_rows, heads_here).astype(jnp.float32)
    query_feat = feature(query_raw).astype(jnp.bfloat16)
    key_feat = feature(key_raw).astype(jnp.bfloat16)
    value_in = heads_major(value_rows, heads_here)
    query32 = query_feat.astype(jnp.float32)
    key32 = key_feat.astype(jnp.float32)
    value32 = value_in.astype(jnp.float32)
    rows = lax.broadcasted_iota(jnp.int32, (tokens, tokens), 0)
    cols = lax.broadcasted_iota(jnp.int32, (tokens, tokens), 1)
    mask = (rows >= cols)[None]
    scores = jnp.einsum("hte,hse->hts", query_feat, key_feat, preferred_element_type=jnp.float32)
    scores = jnp.where(mask, scores, 0.0)
    scores_low = scores.astype(jnp.bfloat16)
    block_kv = jnp.einsum("hse,hsf->hef", key_feat, value_in, preferred_element_type=jnp.float32)
    block_ks = jnp.sum(key32, axis=1)
    prefix_kv, prefix_ks = scan_states(block_kv, block_ks, False)
    numer = jnp.einsum("hte,hef->htf", query32, prefix_kv, precision=highest)
    numer = numer + jnp.einsum(
        "hts,hsf->htf", scores_low, value_in, preferred_element_type=jnp.float32
    )
    denom = jnp.einsum("hte,he->ht", query32, prefix_ks, precision=highest) + jnp.sum(
        scores, axis=2
    )
    attn = numer / denom[:, :, None]
    gain = norm_gain.reshape(heads_here, 1, HEAD_DIM)
    grad_in = gain * heads_major(out_grad, heads_here).astype(jnp.float32)
    sum_squares, cross = lax.psum(
        (jnp.sum(attn * attn, axis=(0, 2)), jnp.sum(attn * grad_in, axis=(0, 2))), "head"
    )
    inv_rms = lax.rsqrt(sum_squares / width + 1e-06)[None, :, None]
    normed = tokens_major((gain * attn * inv_rms).astype(jnp.bfloat16))
    d_attn = inv_rms * grad_in - attn * inv_rms**3 * (cross / width)[None, :, None]
    d_numer = d_attn / denom[:, :, None]
    d_denom = -jnp.sum(d_attn * attn, axis=2) / denom
    numer_low = d_numer.astype(jnp.bfloat16)
    mixed = jnp.einsum("htf,hsf->hts", numer_low, value_in, preferred_element_type=jnp.float32)
    mixed = jnp.where(mask, mixed + d_denom[:, :, None], 0.0)
    mixed_low = mixed.astype(jnp.bfloat16)
    block_g = jnp.einsum("hte,htf->hef", query_feat, numer_low, preferred_element_type=jnp.float32)
    block_gz = jnp.einsum("hte,ht->he", query32, d_denom, precision=highest)
    suffix_g, suffix_gz = scan_states(block_g, block_gz, True)
    q_grad = jnp.einsum("htf,hef->hte", d_numer, prefix_kv, precision=highest)
    q_grad = q_grad + d_denom[:, :, None] * prefix_ks[:, None, :]
    q_grad = q_grad + jnp.einsum(
        "hts,hse->hte", mixed_low, key_feat, preferred_element_type=jnp.float32
    )
    k_grad = (
        jnp.einsum("hsf,hef->hse", value32, suffix_g, precision=highest) + suffix_gz[:, None, :]
    )
    k_grad = k_grad + jnp.einsum(
        "hts,hte->hse", mixed_low, query_feat, preferred_element_type=jnp.float32
    )
    v_grad = jnp.einsum("hse,hef->hsf", key32, suffix_g, precision=highest)
    v_grad = v_grad + jnp.einsum(
        "hts,htf->hsf", scores_low, numer_low, preferred_element_type=jnp.float32
    )
    query_grad = tokens_major((q_grad * feature_slope(query_raw)).astype(jnp.bfloat16))
    key_grad = tokens_major((k_grad * feature_slope(key_raw)).astype(jnp.bfloat16))
    value_grad = tokens_major(v_grad.astype(jnp.bfloat16))
    return (normed, query_grad, key_grad, value_grad)


def solution(mesh):
    devices = mesh.devices
    fine = Mesh(
        devices.reshape(devices.shape[0] // CORES, CORES, devices.shape[1]),
        ("chip", "core", "head"),
    )
    rows = P(("chip", "core"), "head")
    return jax.shard_map(
        body,
        mesh=fine,
        in_specs=(rows, rows, rows, P("head"), rows),
        out_specs=(rows, rows, rows, rows),
        check_vma=False,
    )
```

profile of v0, /device:TPU:1, one launch (start us, length us, event | category | flops | bytes accessed | tf_op | source)
XLA Modules:
  0.0 136.6 jit_solution(6912634050140473162)
XLA Ops:
  0.6 2.4 %fusion.16 = (f32[256,1024]{1,0:T(8,128)}, bf16[32,8,8,128]{3,2,1,0:T(8,128)(2,1)S(1)}, bf16[32,8,8,128]{3,1,2,0:T(8,128)(2,1)S(1)}) fusion(bf16[256,1024]{1,0:T(8,128)(2,1)} %param.6), kind=kLoop, calls=%fused_computation.31 | loop fusion | flops 1835008 | bytes 2621440 | tf_op jit(solution)/shard_map/jit(_where)/select_n | solution.py:24
  3.2 1.3 copy-done
  5.1 3.3 %collective-permute-start = (f32[2,32,17,128]{3,1,2,0:T(8,128)S(1)}, f32[2,32,17,128]{3,1,2,0:T(8,128)S(1)}, u32[]{:S(2)}, u32[]{:S(2)}) collective-permute-start(f32[2,32,17,128]{3,1,2,0:T(8,128)S(1)} %pad_maximum_fusion), channel_id=1, source_target_pairs={{0,4},{4,0},{1,5},{5,1},{2,6},{6,2},{3,7},{7,3},{8,12},{12,8},{9,1... | collective-permute-start | bytes 1671176 | tf_op jit(solution)/shard_map/ppermute | solution.py:28
  8.4 1.6 %collective-permute-done = f32[2,32,17,128]{3,1,2,0:T(8,128)S(1)} collective-permute-done((f32[2,32,17,128]{3,1,2,0:T(8,128)S(1)}, f32[2,32,17,128]{3,1,2,0:T(8,128)S(1)}, u32[]{:S(2)}, u32[]{:S(2)}) %collective-permute-start) | collective-permute-done | bytes 557088 | tf_op jit(solution)/shard_map/ppermute | solution.py:28
  10.2 21.0 %all_to_all.20.spread = f32[32,17,128]{2,1,0:T(8,128)} all-to-all(f32[32,17,128]{2,1,0:T(8,128)S(1)} %bitcast.183), channel_id=1, replica_groups=mesh['chip'=32,'core'=2,'head'=4] {'chip'}, dimensions={0} | all-to-all | bytes 557056 | tf_op jit(solution)/shard_map/all_to_all | solution.py:71
  31.2 1.8 %chip_sums.2 = f32[32,17,128]{2,1,0:T(8,128)} custom-call(f32[32,17,128]{2,1,0:T(8,128)} %all_to_all.20.spread), custom_call_target="tpu_custom_call" | custom-call | tf_op jit(solution)/shard_map/chip_sums/pallas_call | solution.py:57
  33.1 7.6 %all-to-all-start.1 = ((f32[32,17,128]{2,1,0:T(8,128)}), f32[32,17,128]{2,1,0:T(8,128)S(1)}, u32[]{:S(2)}, u32[]{:S(2)}) async-start(f32[32,17,128]{2,1,0:T(8,128)} %chip_sums.2), calls=%async_computation.1 | async-start | bytes 786432 | tf_op jit(solution)/shard_map/all_to_all | solution.py:72
  40.9 2.3 %fusion.12 = (f32[256,1024]{1,0:T(8,128)}, bf16[256,1024]{1,0:T(8,128)(2,1)S(1)}) fusion(bf16[256,1024]{1,0:T(8,128)(2,1)} %param.5), kind=kLoop, calls=%fused_computation.27 | loop fusion | flops 1835008 | bytes 2097152 | tf_op jit(solution)/shard_map/jit(_where)/select_n | solution.py:24
  43.5 0.6 iota_compare_fusion
  44.2 7.3 %all-to-all-done.1 = f32[32,17,128]{2,1,0:T(8,128)S(1)} async-done(((f32[32,17,128]{2,1,0:T(8,128)}), f32[32,17,128]{2,1,0:T(8,128)S(1)}, u32[]{:S(2)}, u32[]{:S(2)}) %all-to-all-start.1) | async-done | bytes 278560 | tf_op jit(solution)/shard_map/all_to_all | solution.py:72
  51.5 4.6 %collective-permute-start.1 = (f32[32,17,128]{2,1,0:T(8,128)S(1)}, f32[32,17,128]{2,1,0:T(8,128)S(1)}, u32[]{:S(2)}, u32[]{:S(2)}) collective-permute-start(f32[32,17,128]{2,1,0:T(8,128)S(1)} %all-to-all-done.1), channel_id=1, source_target_pairs={{0,4},{4,0},{1,5},{5,1},{2,6},{6,2},{3,7},{7,3},{8,12},{12,8},{9,1... | collective-permute-start | bytes 835592 | tf_op jit(solution)/shard_map/ppermute | solution.py:28
  56.1 1.3 select_reduce_fusion
  57.5 1.3 copy-done.16
  58.8 0.4 maximum_add_fusion
  59.9 0.6 fusion.51
  60.7 1.6 %fusion.18 = (f32[256]{0:T(256)S(1)}, f32[256]{0:T(256)S(1)}, f32[8,256,128]{1,2,0:T(8,128)}) fusion(f32[256,8,128]{0,2,1:T(8,128)S(1)} %bitcast.165, f32[8,128]{1,0:T(8,128)S(1)} %bitcast.191, f32[8,256]{1,0:T(8,128)S(1)} %bitcast_add_fusion, f32[8,256,128]{1,2,0:T(8,128)S(1)} %fusion.51, bf16[8,256,128]{2,0,1:T(8,128)(2,1)S(1)} %bitcast.184, ...), kind=kOutput, calls=%fused_computation.35 | convolution fusion | flops 136576512 | bytes 4798464 | tf_op jit(solution)/shard_map/hts,hsf->htf/dot_general | solution.py:111
  62.2 8.7 %all-reduce.2 = (f32[256]{0:T(256)S(1)}, f32[256]{0:T(256)S(1)}) all-reduce(f32[256]{0:T(256)S(1)} %get-tuple-element.13, f32[256]{0:T(256)S(1)} %get-tuple-element.12), channel_id=1, replica_groups=mesh['chip'=32,'core'=2,'head'=4] {'head'}, use_global_device_ids=true, to_apply=%region_3.4 | all-reduce | flops 512 | bytes 4096 | tf_op jit(solution)/shard_map/psum | solution.py:120
  71.0 1.7 %multiply_reduce_fusion = (f32[8,256]{1,0:T(8,128)S(1)}, f32[8,256,128]{1,2,0:T(8,128)S(1)}) fusion(f32[256,8,128]{0,2,1:T(8,128)S(1)} %bitcast.166, f32[256]{0:T(256)S(1)} %get-tuple-element.32, f32[256]{0:T(256)S(1)} %get-tuple-element.27, f32[256]{0:T(256)S(1)} %get-tuple-element.28, f32[8,128]{1,0:T(8,128)S(1)} %bitcast.192, ...), kind=kLoop, calls=%fused_computation.40 | loop fusion | flops 3143680 | bytes 4217856 | tf_op jit(solution)/shard_map/reduce_sum | solution.py:127
  73.3 0.5 fusion.40
  73.8 0.9 pad_maximum_fusion.1
  74.7 2.0 %collective-permute-start.2 = (f32[2,32,17,128]{3,1,2,0:T(8,128)}, f32[2,32,17,128]{3,1,2,0:T(8,128)S(1)}, u32[]{:S(2)}, u32[]{:S(2)}) collective-permute-start(f32[2,32,17,128]{3,1,2,0:T(8,128)} %pad_maximum_fusion.1), channel_id=1, source_target_pairs={{0,4},{4,0},{1,5},{5,1},{2,6},{6,2},{3,7},{7,3},{8,12},{12,8},{9,1... | collective-permute-start | bytes 1671176 | tf_op jit(solution)/shard_map/ppermute | solution.py:28
  76.7 2.5 %copy.52 = f32[256,1024]{0,1:T(8,128)} copy(f32[256,1024]{1,0:T(8,128)} %get-tuple-element.25) | data formatting | bytes 2097152 | tf_op jit(solution)/shard_map/jit(_where)/select_n | solution.py:24
  79.2 2.5 %copy.58 = f32[256,1024]{0,1:T(8,128)} copy(f32[256,1024]{1,0:T(8,128)} %get-tuple-element.22) | data formatting | bytes 2097152 | tf_op jit(solution)/shard_map/jit(_where)/select_n | solution.py:24
  81.8 0.8 copy-done.13
  82.6 0.9 copy.137
  83.6 4.9 %all-to-all-start.2 = ((f32[32,17,128]{2,1,0:T(8,128)}), f32[32,17,128]{2,1,0:T(8,128)S(1)}, u32[]{:S(2)}, u32[]{:S(2)}) async-start(f32[32,17,128]{2,1,0:T(8,128)} %bitcast.182), calls=%async_computation.2 | async-start | bytes 786432 | tf_op jit(solution)/shard_map/all_to_all | solution.py:71
  88.5 1.7 %fusion.21 = bf16[256,8,128]{0,2,1:T(8,128)(2,1)} fusion(f32[8,256,128]{1,2,0:T(8,128)S(1)} %copy-done.7, f32[256]{0:T(256)} %copy-done.26, f32[256,8]{0,1:T(8,128)S(1)} %bitcast.185, f32[8,128]{1,0:T(8,128)} %bitcast.190), kind=kLoop, calls=%fused_computation.39 | loop fusion | flops 1048576 | bytes 1586176 | tf_op jit(solution)/shard_map/convert_element_type | solution.py:124
  90.2 0.8 slice.26
  90.9 2.0 %copy.61 = bf16[256,1024]{1,0:T(8,128)(2,1)} copy(bf16[256,1024]{0,1:T(8,128)(2,1)} %bitcast.178) | data formatting | bytes 1048576
  93.0 1.5 %select_convert_fusion = bf16[8,256,256]{1,2,0:T(8,128)(2,1)} fusion(f32[8,256]{1,0:T(8,128)S(1)} %copy-done.24, pred[256,256]{0,1:T(8,128)(4,1)S(1)} %copy-done.20, f32[8,256,128]{1,2,0:T(8,128)S(1)} %get-tuple-element.17, bf16[256,1024]{1,0:T(8,128)(2,1)S(1)} %copy-done), kind=kOutput, calls=%fused_computation | convolution fusion | flops 136052736 | bytes 2695168 | tf_op jit(solution)/shard_map/htf,hsf->hts/dot_general | solution.py:129
  94.5 6.2 %all-to-all-done.2.spread = f32[32,17,128]{2,1,0:T(8,128)S(1)} async-done(((f32[32,17,128]{2,1,0:T(8,128)}), f32[32,17,128]{2,1,0:T(8,128)S(1)}, u32[]{:S(2)}, u32[]{:S(2)}) %all-to-all-start.2) | async-done | bytes 278560 | tf_op jit(solution)/shard_map/all_to_all | solution.py:71
  100.7 0.7 copy-done.12
  101.4 1.8 %chip_sums.3 = f32[32,17,128]{2,1,0:T(8,128)} custom-call(f32[32,17,128]{2,1,0:T(8,128)} %copy-done.12), custom_call_target="tpu_custom_call" | custom-call | tf_op jit(solution)/shard_map/chip_sums/pallas_call | solution.py:57
  103.2 7.5 %all-to-all-start.3 = ((f32[32,17,128]{2,1,0:T(8,128)}), f32[32,17,128]{2,1,0:T(8,128)S(1)}, u32[]{:S(2)}, u32[]{:S(2)}) async-start(f32[32,17,128]{2,1,0:T(8,128)} %chip_sums.3), calls=%async_computation.3 | async-start | bytes 786432 | tf_op jit(solution)/shard_map/all_to_all | solution.py:72
  110.8 1.1 fusion.5
  112.5 1.1 fusion.7
  113.6 2.1 %copy.62 = bf16[256,1024]{1,0:T(8,128)(2,1)} copy(bf16[256,1024]{0,1:T(8,128)(2,1)} %bitcast.181) | data formatting | bytes 1048576
  115.7 6.1 %all-to-all-done.3 = f32[32,17,128]{2,1,0:T(8,128)S(1)} async-done(((f32[32,17,128]{2,1,0:T(8,128)}), f32[32,17,128]{2,1,0:T(8,128)S(1)}, u32[]{:S(2)}, u32[]{:S(2)}) %all-to-all-start.3) | async-done | bytes 278560 | tf_op jit(solution)/shard_map/all_to_all | solution.py:72
  121.9 4.2 %collective-permute-start.3 = (f32[32,17,128]{2,1,0:T(8,128)S(1)}, f32[32,17,128]{2,1,0:T(8,128)S(1)}, u32[]{:S(2)}, u32[]{:S(2)}) collective-permute-start(f32[32,17,128]{2,1,0:T(8,128)S(1)} %all-to-all-done.3), channel_id=1, source_target_pairs={{0,4},{4,0},{1,5},{5,1},{2,6},{6,2},{3,7},{7,3},{8,12},{12,8},{9,1... | collective-permute-start | bytes 835592 | tf_op jit(solution)/shard_map/ppermute | solution.py:28
  126.1 0.5 convolution_bitcast_fusion
  126.6 0.9 collective-permute-done.3
  128.1 0.9 copy-done.2
  129.1 0.6 fusion.24
  129.7 0.6 copy-done.8
  130.3 1.5 %fusion.8 = bf16[256,8,128]{0,2,1:T(8,128)(2,1)} fusion(f32[256,8,128]{0,2,1:T(8,128)S(1)} %bitcast.174, f32[256,8,128]{0,2,1:T(8,128)S(1)} %convolution_bitcast_fusion, f32[8,128,128]{2,1,0:T(8,128)S(1)} %bitcast.173, f32[8,128]{1,0:T(8,128)S(1)} %bitcast.196, bf16[256,1024]{1,0:T(8,128)(2,1)S(1)} %copy-done), kind=kOutput, calls=%fused_computation.23 | convolution fusion | flops 403701760 | bytes 3674112 | tf_op jit(solution)/shard_map/hsf,hef->hse/dot_general | solution.py:141
  131.8 2.1 %copy.63 = bf16[256,1024]{1,0:T(8,128)(2,1)} copy(bf16[256,1024]{0,1:T(8,128)(2,1)} %bitcast.179) | data formatting | bytes 1048576
  133.9 1.7 %fusion.6 = bf16[8,256,128]{1,2,0:T(8,128)(2,1)S(1)} fusion(f32[8,256,128]{1,2,0:T(8,128)S(1)} %fusion.24, bf16[8,256,256]{1,2,0:T(8,128)(2,1)} %copy-done.17, pred[256,256]{0,1:T(8,128)(4,1)S(1)} %copy-done.21, f32[8,256,128]{1,2,0:T(8,128)S(1)} %get-tuple-element.17), kind=kOutput, calls=%fused_computation.21 | convolution fusion | flops 135528448 | bytes 3735552 | tf_op jit(solution)/shard_map/hts,htf->hsf/dot_general | solution.py:147
  135.6 1.0 copy.64
  (78 shorter events, 4.2 us)
Async XLA Ops:
  3.0 53.1 %copy-start.1 = (bf16[32,8,8,128]{3,2,1,0:T(8,128)(2,1)}, bf16[32,8,8,128]{3,2,1,0:T(8,128)(2,1)S(1)}, u32[]{:S(2)}) copy-start(bf16[32,8,8,128]{3,2,1,0:T(8,128)(2,1)S(1)} %get-tuple-element.23) | copy-start | bytes 1572868
  3.0 1.4 %copy-start = (bf16[256,1024]{1,0:T(8,128)(2,1)S(1)}, bf16[256,1024]{1,0:T(8,128)(2,1)}, u32[]{:S(2)}) copy-start(bf16[256,1024]{1,0:T(8,128)(2,1)} %param.7) | copy-start | bytes 1572868
  3.2 1.8 %copy-start.5 = (bf16[32,8,8,128]{3,2,1,0:T(8,128)(2,1)}, bf16[32,8,8,128]{3,2,1,0:T(8,128)(2,1)S(1)}, u32[]{:S(2)}) copy-start(bf16[32,8,8,128]{3,2,1,0:T(8,128)(2,1)S(1)} %copy.93) | copy-start | bytes 1572868
  5.1 4.9 %collective-permute-start = (f32[2,32,17,128]{3,1,2,0:T(8,128)S(1)}, f32[2,32,17,128]{3,1,2,0:T(8,128)S(1)}, u32[]{:S(2)}, u32[]{:S(2)}) collective-permute-start(f32[2,32,17,128]{3,1,2,0:T(8,128)S(1)} %pad_maximum_fusion), channel_id=1, source_target_pairs={{0,4},{4,0},{1,5},{5,1},{2,6},{6,2},{3,7},{7,3},{8,12},{12,8},{9,1... | collective-permute-start | bytes 1671176 | tf_op jit(solution)/shard_map/ppermute | solution.py:28
  10.0 21.2 %copy-start.15 = (f32[2,32,17,128]{3,1,2,0:T(8,128)}, f32[2,32,17,128]{3,1,2,0:T(8,128)S(1)}, u32[]{:S(2)}) copy-start(f32[2,32,17,128]{3,1,2,0:T(8,128)S(1)} %collective-permute-done) | copy-start | bytes 1671172
  31.2 9.4 %copy-start.18 = (bf16[256,1024]{1,0:T(8,128)(2,1)S(1)}, bf16[256,1024]{1,0:T(8,128)(2,1)}, u32[]{:S(2)}) copy-start(bf16[256,1024]{1,0:T(8,128)(2,1)} %param.9) | copy-start | bytes 1572868
  33.1 18.4 %all-to-all-start.1 = ((f32[32,17,128]{2,1,0:T(8,128)}), f32[32,17,128]{2,1,0:T(8,128)S(1)}, u32[]{:S(2)}, u32[]{:S(2)}) async-start(f32[32,17,128]{2,1,0:T(8,128)} %chip_sums.2), calls=%async_computation.1 | async-start | bytes 786432 | tf_op jit(solution)/shard_map/all_to_all | solution.py:72
  51.5 6.0 %collective-permute-start.1 = (f32[32,17,128]{2,1,0:T(8,128)S(1)}, f32[32,17,128]{2,1,0:T(8,128)S(1)}, u32[]{:S(2)}, u32[]{:S(2)}) collective-permute-start(f32[32,17,128]{2,1,0:T(8,128)S(1)} %all-to-all-done.1), channel_id=1, source_target_pairs={{0,4},{4,0},{1,5},{5,1},{2,6},{6,2},{3,7},{7,3},{8,12},{12,8},{9,1... | collective-permute-start | bytes 835592 | tf_op jit(solution)/shard_map/ppermute | solution.py:28
  57.4 3.1 %copy-start.17 = (bf16[8,256,256]{1,2,0:T(8,128)(2,1)}, bf16[8,256,256]{1,2,0:T(8,128)(2,1)S(1)}, u32[]{:S(2)}) copy-start(bf16[8,256,256]{1,2,0:T(8,128)(2,1)S(1)} %get-tuple-element.30) | copy-start | bytes 3145732
  57.4 1.4 %copy-start.16 = (f32[2,32,17,128]{3,1,2,0:T(8,128)S(1)}, f32[2,32,17,128]{3,1,2,0:T(8,128)}, u32[]{:S(2)}) copy-start(f32[2,32,17,128]{3,1,2,0:T(8,128)} %copy-done.15) | copy-start | bytes 1671172
  59.2 0.6 copy-start.22
  59.3 1.2 copy-start.3
  59.8 0.8 copy-start.19
  59.9 0.8 copy-start.25
  71.0 1.7 %copy-start.26 = (f32[256]{0:T(256)}, f32[256]{0:T(256)S(1)}, u32[]{:S(2)}) copy-start(f32[256]{0:T(256)S(1)} %get-tuple-element.28) | copy-start | bytes 3076
  72.7 0.6 copy-start.23
  74.7 7.1 %collective-permute-start.2 = (f32[2,32,17,128]{3,1,2,0:T(8,128)}, f32[2,32,17,128]{3,1,2,0:T(8,128)S(1)}, u32[]{:S(2)}, u32[]{:S(2)}) collective-permute-start(f32[2,32,17,128]{3,1,2,0:T(8,128)} %pad_maximum_fusion.1), channel_id=1, source_target_pairs={{0,4},{4,0},{1,5},{5,1},{2,6},{6,2},{3,7},{7,3},{8,12},{12,8},{9,1... | collective-permute-start | bytes 1671176 | tf_op jit(solution)/shard_map/ppermute | solution.py:28
  81.8 0.8 copy-start.13
  82.6 5.8 %copy-start.7 = (f32[8,256,128]{1,2,0:T(8,128)S(1)}, f32[8,256,128]{1,2,0:T(8,128)}, u32[]{:S(2)}) copy-start(f32[8,256,128]{1,2,0:T(8,128)} %get-tuple-element.31) | copy-start | bytes 3145732
  83.6 17.1 %all-to-all-start.2 = ((f32[32,17,128]{2,1,0:T(8,128)}), f32[32,17,128]{2,1,0:T(8,128)S(1)}, u32[]{:S(2)}, u32[]{:S(2)}) async-start(f32[32,17,128]{2,1,0:T(8,128)} %bitcast.182), calls=%async_computation.2 | async-start | bytes 786432 | tf_op jit(solution)/shard_map/all_to_all | solution.py:71
  90.2 2.8 %copy-start.20 = (pred[256,256]{0,1:T(8,128)(4,1)S(1)}, pred[256,256]{0,1:T(8,128)(4,1)}, u32[]{:S(2)}) copy-start(pred[256,256]{0,1:T(8,128)(4,1)} %iota_compare_fusion) | copy-start | bytes 196612
  90.2 2.8 %copy-start.24 = (f32[8,256]{1,0:T(8,128)S(1)}, f32[8,256]{1,0:T(8,128)}, u32[]{:S(2)}) copy-start(f32[8,256]{1,0:T(8,128)} %copy-done.23) | copy-start | bytes 24580
  94.5 16.3 %copy-start.4 = (f32[2,32,16,128]{3,2,1,0:T(8,128)S(1)}, f32[2,32,16,128]{3,2,1,0:T(8,128)}, u32[]{:S(2)}) copy-start(f32[2,32,16,128]{3,2,1,0:T(8,128)} %copy-done.3) | copy-start | bytes 1572868
  100.7 0.7 copy-start.12
  103.2 18.7 %all-to-all-start.3 = ((f32[32,17,128]{2,1,0:T(8,128)}), f32[32,17,128]{2,1,0:T(8,128)S(1)}, u32[]{:S(2)}, u32[]{:S(2)}) async-start(f32[32,17,128]{2,1,0:T(8,128)} %chip_sums.3), calls=%async_computation.3 | async-start | bytes 786432 | tf_op jit(solution)/shard_map/all_to_all | solution.py:72
  110.7 1.1 copy-start.6
  110.8 1.4 %copy-start.9 = (f32[256,1024]{0,1:T(8,128)S(1)}, f32[256,1024]{0,1:T(8,128)}, u32[]{:S(2)}) copy-start(f32[256,1024]{0,1:T(8,128)} %copy.52) | copy-start | bytes 3145732
  110.8 1.7 %copy-start.10 = (bf16[8,256,256]{1,2,0:T(8,128)(2,1)S(1)}, bf16[8,256,256]{1,2,0:T(8,128)(2,1)}, u32[]{:S(2)}) copy-start(bf16[8,256,256]{1,2,0:T(8,128)(2,1)} %select_convert_fusion) | copy-start | bytes 3145732
  113.6 12.5 %copy-start.11 = (bf16[8,256,256]{1,2,0:T(8,128)(2,1)S(1)}, bf16[8,256,256]{1,2,0:T(8,128)(2,1)}, u32[]{:S(2)}) copy-start(bf16[8,256,256]{1,2,0:T(8,128)(2,1)} %select_convert_fusion) | copy-start | bytes 3145732
  121.9 5.6 %collective-permute-start.3 = (f32[32,17,128]{2,1,0:T(8,128)S(1)}, f32[32,17,128]{2,1,0:T(8,128)S(1)}, u32[]{:S(2)}, u32[]{:S(2)}) collective-permute-start(f32[32,17,128]{2,1,0:T(8,128)S(1)} %all-to-all-done.3), channel_id=1, source_target_pairs={{0,4},{4,0},{1,5},{5,1},{2,6},{6,2},{3,7},{7,3},{8,12},{12,8},{9,1... | collective-permute-start | bytes 835592 | tf_op jit(solution)/shard_map/ppermute | solution.py:28
  126.6 1.1 copy-start.14
  128.0 1.0 copy-start.2
  129.1 1.2 copy-start.8
  131.8 2.1 %copy-start.21 = (pred[256,256]{0,1:T(8,128)(4,1)S(1)}, pred[256,256]{0,1:T(8,128)(4,1)}, u32[]{:S(2)}) copy-start(pred[256,256]{0,1:T(8,128)(4,1)} %iota_compare_fusion) | copy-start | bytes 196612
where the time goes:
time: 138 us; the launch traced here: 137 us
  starting transfers between devices  34.2 us (25%)
  blocking collectives  29.7 us (22%)
  local copies, waits for them, and re-layouts  22.2 us (16%)
  waiting for transfers between devices  22.2 us (16%)
  matrix products  12.9 us (9%)
  other arithmetic  10.8 us (8%)
  Pallas kernels  3.61 us (3%)
    all_to_all x1, blocking collectives, scan_states(): spread = lax.all_to_all(pair, 'chip', 0, 0)  21 us
    all_to_all x2, starting transfers between devices, scan_states(): kept = lax.all_to_all(chip_sums(spread, backward), 'chip', 0, 0)  15.1 us
    unnamed x60, local copies, waits for them, and re-layouts  14.4 us
    ppermute x4, starting transfers between devices, swap_cores(): return lax.ppermute(array, 'core', [(0, 1), (1, 0)])  14.2 us
    all_to_all x2, waiting for transfers between devices, scan_states(): kept = lax.all_to_all(chip_sums(spread, backward), 'chip', 0, 0)  13.5 us
    psum x1, blocking collectives, body(): lax.psum((jnp.sum(attn * attn, axis=(0, 2)), jnp.sum(attn * grad_in, axis...  8.7 us
    all_to_all x1, waiting for transfers between devices, scan_states(): spread = lax.all_to_all(pair, 'chip', 0, 0)  6.19 us
    select_n x2, local copies, waits for them, and re-layouts, feature_slope(): jnp.where(values > 0, jnp.ones_like(values), jnp.exp(jnp.minimum(values,...  5.07 us
  transfers between devices with their start and end apart: 7, of which 6 were waited for; matrix products, arithmetic and copies ran while one was open for 15% of the time, Pallas kernels for 0%

commit v1 on v0

v1 whole, which is shorter than its diff:
```python
import functools

import jax
import jax.numpy as jnp
from jax import lax
from jax.experimental import pallas as pl
from jax.experimental.pallas import tpu as pltpu
from jax.sharding import Mesh
from jax.sharding import PartitionSpec as P

HEADS = 32
HEAD_DIM = 128
CORES = 2
ROWS = 16
BLOCK = 256
BLOCKS = HEAD_DIM // ROWS

f32 = jnp.float32
bf16 = jnp.bfloat16
highest = lax.Precision.HIGHEST


def feature(values):
    return jnp.where(values > 0, values + 1.0, jnp.exp(jnp.minimum(values, 0.0)))


def feature_slope(values):
    return jnp.where(values > 0, jnp.ones_like(values), jnp.exp(jnp.minimum(values, 0.0)))


def dot(left, right, left_dim, right_dim, precision=None):
    return lax.dot_general(
        left,
        right,
        (((left_dim,), (right_dim,)), ((), ())),
        precision=precision,
        preferred_element_type=f32,
    )


def split(values):
    high = values.astype(bf16)
    return high, (values - high.astype(f32)).astype(bf16)


def head_columns(side, place, heads_side):
    return pl.ds(pl.multiple_of((side * heads_side + place) * HEAD_DIM, HEAD_DIM), HEAD_DIM)


def put_state(wire, place, state, row):
    first = place * BLOCKS
    wire[first : first + BLOCKS, 0:ROWS, :] = state.reshape(BLOCKS, ROWS, HEAD_DIM)
    wire[first : first + 1, ROWS : ROWS + 1, :] = row.reshape(1, 1, HEAD_DIM)


def clear_rows(wire):
    wire[:, ROWS : ROWS + 1, :] = jnp.zeros((wire.shape[0], 1, HEAD_DIM), f32)


def get_state(wire, extra, adds, place):
    first = place * BLOCKS
    blocks = pl.ds(first, BLOCKS)
    state = wire[blocks, 0:ROWS, :] + jnp.where(adds, extra[blocks, 0:ROWS, :], 0.0)
    row = wire[first, ROWS : ROWS + 1, :] + jnp.where(adds, extra[first, ROWS : ROWS + 1, :], 0.0)
    return state.reshape(HEAD_DIM, HEAD_DIM), row


def send_out(slots, target, slot, here, sem):
    copy = pltpu.make_async_copy(slots.at[slot], target.at[:, here], sem)
    copy.start()
    return copy


def causal(tokens):
    rows = lax.broadcasted_iota(jnp.int32, (tokens, tokens), 0)
    cols = lax.broadcasted_iota(jnp.int32, (tokens, tokens), 1)
    return rows >= cols


def head_order(core, heads_side):
    return [(side, place) for side in (1 - core, core) for place in range(heads_side)]


def states_kernel(core, keys, values, mine, theirs, key_slots, value_slots, sems):
    heads_side = keys.shape[1] // HEAD_DIM // CORES
    order = head_order(core[0], heads_side)
    copies = []
    for slot, (side, place) in enumerate(order):
        here = head_columns(side, place, heads_side)
        pair = (
            pltpu.make_async_copy(keys.at[:, here], key_slots.at[slot], sems.at[0, slot]),
            pltpu.make_async_copy(values.at[:, here], value_slots.at[slot], sems.at[1, slot]),
        )
        for copy in pair:
            copy.start()
        copies.append(pair)
    clear_rows(theirs)
    clear_rows(mine)
    for slot, (side, place) in enumerate(order):
        for copy in copies[slot]:
            copy.wait()
        key_feat = feature(key_slots[slot].astype(f32)).astype(bf16)
        row = jnp.sum(key_feat.astype(f32), axis=0, keepdims=True)
        wire = theirs if slot < heads_side else mine
        put_state(wire, place, dot(value_slots[slot], key_feat, 0, 0), row)


def inside_forward_kernel(queries, keys, values, query_out, key_out, low_out, numer, denom):
    tokens, width = queries.shape
    mask = causal(tokens)
    for head in range(width // HEAD_DIM):
        here = pl.ds(head * HEAD_DIM, HEAD_DIM)
        query_feat = feature(queries[:, here].astype(f32)).astype(bf16)
        key_feat = feature(keys[:, here].astype(f32)).astype(bf16)
        query_out[:, here] = query_feat
        key_out[:, here] = key_feat
        scores = jnp.where(mask, dot(query_feat, key_feat, 1, 1), 0.0)
        scores_low = scores.astype(bf16)
        low_out[:, pl.ds(head * tokens, tokens)] = scores_low
        numer[:, here] = dot(scores_low, values[:, here], 1, 0)
        total = jnp.sum(scores, axis=1, keepdims=True)
        denom[:, here] = jnp.broadcast_to(total, (tokens, HEAD_DIM))


def attention_kernel(
    core, query_feat, numer_in, denom_in, kept, got, extra, extra_got, gain, out_grad,
    attn_out, inverse_out, stats,
):
    tokens, width = query_feat.shape
    heads_side = width // HEAD_DIM // CORES
    adds = core[0] == 1
    squares = jnp.zeros((tokens, HEAD_DIM), f32)
    cross = jnp.zeros((tokens, HEAD_DIM), f32)
    for wire, more, side in ((kept, extra, core[0]), (got, extra_got, 1 - core[0])):
        for place in range(heads_side):
            here = head_columns(side, place, heads_side)
            state, row = get_state(wire, more, adds, place)
            both = jnp.concatenate([state, jnp.broadcast_to(row, state.shape)], axis=0)
            right = jnp.concatenate(split(both), axis=1)
            query = query_feat[:, here]
            product = dot(jnp.concatenate([query, query], axis=1), right, 1, 1)
            numer = numer_in[:, here] + product[:, :HEAD_DIM]
            inverse = 1.0 / (denom_in[:, here] + product[:, HEAD_DIM:])
            attn = numer * inverse
            grad_in = gain[:, here] * out_grad[:, here].astype(f32)
            squares = squares + attn * attn
            cross = cross + attn * grad_in
            attn_out[:, here] = attn
            inverse_out[:, here] = inverse
    ones = jnp.ones((8, HEAD_DIM), f32)
    which = lax.broadcasted_iota(jnp.int32, (8, tokens), 0)
    row_squares = dot(ones, squares, 1, 1, highest)
    row_cross = dot(ones, cross, 1, 1, highest)
    stats[...] = jnp.where(which == 0, row_squares, jnp.where(which == 1, row_cross, 0.0))


def token_scales(stats, width_all):
    tokens = stats.shape[1]
    squares = stats[0:1, :]
    cross = stats[1:2, :]
    scale = lax.rsqrt(squares / width_all + 1e-06)
    slope = scale * scale * scale * (cross / width_all)
    which = lax.broadcasted_iota(jnp.int32, (8, tokens), 0)
    rows = jnp.where(which == 0, scale, jnp.where(which == 1, slope, 0.0))
    pick = lax.broadcasted_iota(jnp.int32, (8, 2 * HEAD_DIM), 0) == (
        lax.broadcasted_iota(jnp.int32, (8, 2 * HEAD_DIM), 1) // HEAD_DIM
    )
    spread = dot(rows, pick.astype(f32), 0, 0, highest)
    return spread[:, :HEAD_DIM], spread[:, HEAD_DIM:]


def gradient_kernel(
    core, query_feat, attn_in, inverse_in, gain, out_grad, stats, numer_out, denom_out, mine, theirs
):
    width = query_feat.shape[1]
    heads_side = width // HEAD_DIM // CORES
    scale, slope = token_scales(stats[...], HEADS * HEAD_DIM)
    for wire, side in ((theirs, 1 - core[0]), (mine, core[0])):
        clear_rows(wire)
        for place in range(heads_side):
            here = head_columns(side, place, heads_side)
            attn = attn_in[:, here]
            inverse = inverse_in[:, here]
            grad_in = gain[:, here] * out_grad[:, here].astype(f32)
            d_attn = scale * grad_in - attn * slope
            d_numer = d_attn * inverse
            total = jnp.sum(d_attn * attn, axis=1, keepdims=True)
            d_denom = -total * inverse
            numer_out[:, here] = d_numer
            denom_out[:, here] = d_denom
            query = query_feat[:, here]
            row = jnp.sum(d_denom * query.astype(f32), axis=0, keepdims=True)
            put_state(wire, place, dot(d_numer.astype(bf16), query, 0, 0), row)


def inside_backward_kernel(
    core, queries, query_feat, key_feat, values, low, d_numer_in, d_denom_in, attn, gain, stats,
    kept, got, extra, extra_got, normed, query_grad, key_part, value_part,
    normed_slots, query_slots, sems,
):
    tokens, width = queries.shape
    copies = []
    heads_side = width // HEAD_DIM // CORES
    adds = core[0] == 1
    mask = causal(tokens)
    scale, _ = token_scales(stats[...], HEADS * HEAD_DIM)
    for wire, more, side in ((kept, extra, core[0]), (got, extra_got, 1 - core[0])):
        for place in range(heads_side):
            here = head_columns(side, place, heads_side)
            wide = pl.ds(pl.multiple_of((side * heads_side + place) * tokens, tokens), tokens)
            state, row = get_state(wire, more, adds, place)
            state_high, state_low = split(state)
            slot = len(copies) // 2
            normed_slots[slot] = (gain[:, here] * attn[:, here] * scale).astype(bf16)
            copies.append(send_out(normed_slots, normed, slot, here, sems.at[0, slot]))
            d_numer = d_numer_in[:, here]
            d_denom = d_denom_in[:, here]
            numer_low, numer_rest = split(d_numer)
            query = query_feat[:, here]
            key = key_feat[:, here]
            value = values[:, here]
            mixed = dot(numer_low, value, 1, 1) + jnp.concatenate([d_denom, d_denom], axis=1)
            mixed_low = jnp.where(mask, mixed, 0.0).astype(bf16)
            left = jnp.concatenate([numer_low, numer_low, numer_rest], axis=1)
            right = jnp.concatenate([state_high, state_low, state_high], axis=0)
            grad = dot(left, right, 1, 0) + d_denom * row + dot(mixed_low, key, 1, 0)
            query_raw = queries[:, here].astype(f32)
            query_slots[slot] = (grad * feature_slope(query_raw)).astype(bf16)
            copies.append(send_out(query_slots, query_grad, slot, here, sems.at[1, slot]))
            key_part[:, here] = dot(mixed_low, query, 0, 0)
            value_part[:, here] = dot(low[:, wide], numer_low, 0, 0)
    for copy in copies:
        copy.wait()


def outside_backward_kernel(
    core, keys, key_feat, values, key_part, value_part, kept, got, extra, extra_got,
    key_grad, value_grad, key_slots, value_slots, sems,
):
    width = keys.shape[1]
    copies = []
    heads_side = width // HEAD_DIM // CORES
    adds = core[0] == 0
    for wire, more, side in ((kept, extra, core[0]), (got, extra_got, 1 - core[0])):
        for place in range(heads_side):
            here = head_columns(side, place, heads_side)
            state, row = get_state(wire, more, adds, place)
            high, low = split(state)
            value = values[:, here]
            key = key_feat[:, here]
            grad = dot(
                jnp.concatenate([value, value], axis=1), jnp.concatenate([high, low], axis=0), 1, 0
            )
            grad = grad + row + key_part[:, here]
            key_raw = keys[:, here].astype(f32)
            slot = len(copies) // 2
            key_slots[slot] = (grad * feature_slope(key_raw)).astype(bf16)
            copies.append(send_out(key_slots, key_grad, slot, here, sems.at[0, slot]))
            grad = dot(
                jnp.concatenate([key, key], axis=1), jnp.concatenate([high, low], axis=1), 1, 1
            )
            value_slots[slot] = (grad + value_part[:, here]).astype(bf16)
            copies.append(send_out(value_slots, value_grad, slot, here, sems.at[1, slot]))
    for copy in copies:
        copy.wait()


def chip_sums_kernel(backward, spread, sums):
    chips = spread.shape[0]
    total = jnp.zeros(spread.shape[1:], f32)
    for step in range(chips):
        chip = chips - 1 - step if backward else step
        sums[chip] = total
        if step < chips - 1:
            total = total + spread[chip]


def shaped(shape, dtype):
    return jax.ShapeDtypeStruct(shape, dtype)


def call(kernel, name, out_shape, *operands, core=None, flops=0, hbm_in=(), hbm_out=(), slots=0):
    moved = sum(x.size * x.dtype.itemsize for x in operands)
    moved += sum(x.size * x.dtype.itemsize for x in jax.tree.leaves(out_shape))

    def spaces(count, hbm):
        kinds = [pltpu.HBM if place in hbm else pltpu.VMEM for place in range(count)]
        return [pl.BlockSpec(memory_space=kind) for kind in kinds]

    in_specs = spaces(len(operands), hbm_in)
    out_specs = spaces(len(jax.tree.leaves(out_shape)), hbm_out)
    scratch = []
    if slots:
        scratch = [pltpu.VMEM((slots, BLOCK, HEAD_DIM), bf16)] * 2
        scratch.append(pltpu.SemaphoreType.DMA((2, slots)))
    if core is not None:
        in_specs = [pl.BlockSpec(memory_space=pltpu.SMEM)] + in_specs
        operands = (core,) + operands
    return pl.pallas_call(
        kernel,
        out_shape=out_shape,
        in_specs=in_specs,
        out_specs=tuple(out_specs) if isinstance(out_shape, tuple) else out_specs[0],
        scratch_shapes=scratch,
        compiler_params=pltpu.CompilerParams(vmem_limit_bytes=16 << 20),
        cost_estimate=pl.CostEstimate(flops=flops, bytes_accessed=moved, transcendentals=0),
        name=name,
    )(*operands)


def swap_cores(array):
    return lax.ppermute(array, "core", [(0, 1), (1, 0)])


def chip_sums(spread, backward):
    kernel = functools.partial(chip_sums_kernel, backward)
    return call(kernel, "chip_sums", shaped(spread.shape, f32), spread)


def body(queries, key_rows, value_rows, norm_gain, out_grad):
    tokens, width = queries.shape
    heads = width // HEAD_DIM
    chips = lax.axis_size("chip")
    core = lax.axis_index("core").astype(jnp.int32).reshape(1)
    gain = norm_gain.reshape(1, width)
    wire = shaped((chips, ROWS + 1, HEAD_DIM), f32)
    narrow = shaped((tokens, width), bf16)
    full = shaped((tokens, width), f32)
    unit = 2 * tokens * HEAD_DIM * HEAD_DIM * heads

    mine, theirs = call(
        states_kernel,
        "states",
        (wire, wire),
        key_rows,
        value_rows,
        core=core,
        flops=unit,
        hbm_in=(0, 1),
        slots=heads,
    )
    theirs, mine, q_in, k_in, v_in = lax.optimization_barrier(
        (theirs, mine, queries, key_rows, value_rows)
    )
    extra = swap_cores(theirs)
    extra_got = swap_cores(mine)
    inside = call(
        inside_forward_kernel,
        "inside_forward",
        (narrow, narrow, shaped((tokens, heads * tokens), bf16), full, full),
        q_in,
        k_in,
        v_in,
        flops=4 * unit,
    )
    extra, extra_got, mine, inside = lax.optimization_barrier((extra, extra_got, mine, inside))
    query_feat, key_feat, low, numer_in, denom_in = inside
    spread = lax.all_to_all(mine + extra, "chip", 0, 0)
    kept = lax.all_to_all(chip_sums(spread, False), "chip", 0, 0)
    got = swap_cores(kept)
    prefix = (kept, got, extra, extra_got)
    attn, inverse, stats = call(
        attention_kernel,
        "attention",
        (full, full, shaped((8, tokens), f32)),
        query_feat,
        numer_in,
        denom_in,
        *prefix,
        gain,
        out_grad,
        core=core,
        flops=4 * unit,
    )
    stats = lax.psum(stats, "head")
    d_numer, d_denom, mine, theirs = call(
        gradient_kernel,
        "gradient",
        (full, full, wire, wire),
        query_feat,
        attn,
        inverse,
        gain,
        out_grad,
        stats,
        core=core,
        flops=unit,
    )
    theirs, mine, d_numer, d_denom = lax.optimization_barrier((theirs, mine, d_numer, d_denom))
    extra = swap_cores(theirs)
    extra_got = swap_cores(mine)
    inside = call(
        inside_backward_kernel,
        "inside_backward",
        (narrow, narrow, full, full),
        queries,
        query_feat,
        key_feat,
        value_rows,
        low,
        d_numer,
        d_denom,
        attn,
        gain,
        stats,
        *prefix,
        core=core,
        flops=11 * unit,
        hbm_out=(0, 1),
        slots=heads,
    )
    extra, extra_got, mine, inside = lax.optimization_barrier((extra, extra_got, mine, inside))
    normed, query_grad, key_part, value_part = inside
    spread = lax.all_to_all(mine + extra, "chip", 0, 0)
    kept = lax.all_to_all(chip_sums(spread, True), "chip", 0, 0)
    got = swap_cores(kept)
    key_grad, value_grad = call(
        outside_backward_kernel,
        "outside_backward",
        (narrow, narrow),
        key_rows,
        key_feat,
        value_rows,
        key_part,
        value_part,
        kept,
        got,
        extra,
        extra_got,
        core=core,
        flops=4 * unit,
        hbm_out=(0, 1),
        slots=heads,
    )
    return (normed, query_grad, key_grad, value_grad)


def solution(mesh):
    devices = mesh.devices
    fine = Mesh(
        devices.reshape(devices.shape[0] // CORES, CORES, devices.shape[1]),
        ("chip", "core", "head"),
    )
    rows = P(("chip", "core"), "head")
    return jax.shard_map(
        body,
        mesh=fine,
        in_specs=(rows, rows, rows, P("head"), rows),
        out_specs=(rows, rows, rows, rows),
        check_vma=False,
    )
```

time: 138 us -> 120 us (0.87)
  blocking collectives: 29.7 us -> 82.6 us
  waiting for transfers between devices: 22.2 us -> 2.71 us
  starting transfers between devices: 34.2 us -> 15.3 us
  local copies, waits for them, and re-layouts: 22.2 us -> 7.1 us
  matrix products: 12.9 us -> 0 us
  other arithmetic: 10.8 us -> 0.09 us
  Pallas kernels: 3.61 us -> 11.2 us
    all_to_all x1 -> x4, blocking collectives: 21 us -> 73.8 us  [the longest x2 37.3 us: body(): spread = lax.all_to_all(mine + extra, 'chip', 0, 0)]
    all_to_all x3 -> x0, starting transfers between devices: 20 us -> none  [the longest x2 15.1 us: scan_states(): kept = lax.all_to_all(chip_sums(spread, backward), 'chip', 0, 0)]
    all_to_all x3 -> x0, waiting for transfers between devices: 19.7 us -> none  [the longest x2 13.5 us: scan_states(): kept = lax.all_to_all(chip_sums(spread, backward), 'chip', 0, 0)]
    dot_general x14 -> x0, matrix products: 12.9 us -> none  [the longest x1 1.7 us: body(): jnp.einsum('hts,htf->hsf', scores_low, numer_low, preferred_element_type=...]
    pallas_call x2 -> x8, Pallas kernels: 3.61 us -> 11.2 us  [call(): pl.pallas_call(kernel, out_shape=out_shape, in_specs=in_specs, out_specs=...]
    unnamed x60 -> x38, local copies, waits for them, and re-layouts: 14.4 us -> 7.1 us
    select_n x2 -> x0, local copies, waits for them, and re-layouts: 5.07 us -> none  [feature_slope(): jnp.where(values > 0, jnp.ones_like(values), jnp.exp(jnp.minimum(values,...]
    select_n x2 -> x0, other arithmetic: 4.74 us -> none  [feature_slope(): jnp.where(values > 0, jnp.ones_like(values), jnp.exp(jnp.minimum(values,...]
  transfers between devices with their start and end apart: 7 -> 6, of which waited for: 6 -> 2; matrix products, arithmetic and copies ran while one was open for 15% -> 0% of each run, Pallas kernels for 0% -> 4%
where the time goes in v1:
time: 120 us
  blocking collectives  82.6 us (69%)
  starting transfers between devices  15.3 us (13%)
  Pallas kernels  11.2 us (9%)
  local copies, waits for them, and re-layouts  7.1 us (6%)
  waiting for transfers between devices  2.71 us (2%)
    all_to_all x2, blocking collectives, body(): spread = lax.all_to_all(mine + extra, 'chip', 0, 0)  37.3 us
    all_to_all x1, blocking collectives, body(): kept = lax.all_to_all(chip_sums(spread, False), 'chip', 0, 0)  18.3 us
    all_to_all x1, blocking collectives, body(): kept = lax.all_to_all(chip_sums(spread, True), 'chip', 0, 0)  18.2 us
    ppermute x6, starting transfers between devices, swap_cores(): return lax.ppermute(array, 'core', [(0, 1), (1, 0)])  15.3 us
    pallas_call x8, Pallas kernels, call(): pl.pallas_call(kernel, out_shape=out_shape, in_specs=in_specs, out_specs=...  11.2 us
    psum x1, blocking collectives, body(): stats = lax.psum(stats, 'head')  8.81 us
    unnamed x38, local copies, waits for them, and re-layouts  7.1 us
    ppermute x6, waiting for transfers between devices, swap_cores(): return lax.ppermute(array, 'core', [(0, 1), (1, 0)])  2.71 us
  transfers between devices with their start and end apart: 6, of which 2 were waited for; matrix products, arithmetic and copies ran while one was open for 0% of the time, Pallas kernels for 4%

profile of v1, /device:TPU:1, one launch (start us, length us, event | category | flops | bytes accessed | tf_op | source)
XLA Modules:
  0.0 119.9 jit_solution(8148066096487087554)
XLA Ops:
  0.6 0.0 copy-start
  0.6 1.0 copy-done
  1.7 1.0 copy-done.2
  2.7 2.1 %states.1 = (f32[32,17,128]{2,1,0:T(8,128)S(1)}, f32[32,17,128]{2,1,0:T(8,128)S(1)}) custom-call(s32[1]{0:T(128)} %bitcast.core, bf16[256,1024]{1,0:T(8,128)(2,1)S(1)} %copy-done.2, bf16[256,1024]{1,0:T(8,128)(2,1)S(1)} %copy-done), custom_call_target="tpu_custom_call" | custom-call | flops 67108864 | bytes 1605632 | tf_op jit(solution)/shard_map/states/pallas_call | solution.py:299
  4.8 3.3 %collective-permute-start = (f32[32,17,128]{2,1,0:T(8,128)S(1)}, f32[32,17,128]{2,1,0:T(8,128)S(1)}, u32[]{:S(2)}, u32[]{:S(2)}) collective-permute-start(f32[32,17,128]{2,1,0:T(8,128)S(1)} %get-tuple-element.50), channel_id=1, source_target_pairs={{0,4},{4,0},{1,5},{5,1},{2,6},{6,2},{3,7},{7,3},{8,12},{12,8},{9,1... | collective-permute-start | bytes 835592 | tf_op jit(solution)/shard_map/ppermute | solution.py:312
  8.2 0.1 collective-permute-start.1
  8.3 0.0 copy-done.1
  8.3 0.0 copy-done.3
  8.3 1.0 copy-done.4
  9.3 1.1 inside_forward.1
  10.4 0.0 copy-start.6
  10.4 0.0 copy-start.14
  10.4 0.0 collective-permute-done.extra
  10.4 0.0 collective-permute-done.1.extra_got
  10.4 0.0 copy-start.10
  10.5 0.7 copy-done.6
  11.2 20.8 %all_to_all.20.spread = f32[32,17,128]{2,1,0:T(8,128)S(1)} all-to-all(f32[32,17,128]{2,1,0:T(8,128)S(1)} %add.8), channel_id=1, replica_groups=mesh['chip'=32,'core'=2,'head'=4] {'chip'}, dimensions={0} | all-to-all | bytes 557056 | tf_op jit(solution)/shard_map/all_to_all | solution.py:358
  32.1 0.0 copy-done.14
  32.1 0.0 copy-start.8
  32.1 0.0 copy-start.18
  32.1 18.3 %all_to_all.21.kept = f32[32,17,128]{2,1,0:T(8,128)S(1)} all-to-all(f32[32,17,128]{2,1,0:T(8,128)S(1)} %chip_sums.2), channel_id=1, replica_groups=mesh['chip'=32,'core'=2,'head'=4] {'chip'}, dimensions={0} | all-to-all | bytes 557056 | tf_op jit(solution)/shard_map/all_to_all | solution.py:359
  50.4 4.6 %collective-permute-start.2 = (f32[32,17,128]{2,1,0:T(8,128)S(1)}, f32[32,17,128]{2,1,0:T(8,128)S(1)}, u32[]{:S(2)}, u32[]{:S(2)}) collective-permute-start(f32[32,17,128]{2,1,0:T(8,128)S(1)} %all_to_all.21.kept), channel_id=1, source_target_pairs={{0,4},{4,0},{1,5},{5,1},{2,6},{6,2},{3,7},{7,3},{8,12},{12,8},{9,1... | collective-permute-start | bytes 835592 | tf_op jit(solution)/shard_map/ppermute | solution.py:312
  55.1 1.3 %collective-permute-done.2.got = f32[32,17,128]{2,1,0:T(8,128)S(1)} collective-permute-done((f32[32,17,128]{2,1,0:T(8,128)S(1)}, f32[32,17,128]{2,1,0:T(8,128)S(1)}, u32[]{:S(2)}, u32[]{:S(2)}) %collective-permute-start.2) | collective-permute-done | bytes 278560 | tf_op jit(solution)/shard_map/ppermute | solution.py:312
  56.4 0.0 copy-done.10
  56.4 0.0 copy-done.8
  56.4 0.0 copy-done.18
  56.4 1.2 %attention.1 = (f32[256,1024]{1,0:T(8,128)S(1)}, f32[256,1024]{1,0:T(8,128)S(1)}, f32[8,256]{1,0:T(8,128)S(1)}) custom-call(s32[1]{0:T(128)} %bitcast.core, bf16[256,1024]{1,0:T(8,128)(2,1)S(1)} %get-tuple-element.60.query_feat, f32[256,1024]{1,0:T(8,128)S(1)} %get-tuple-element.61.numer_in, f32[256,1024]{1,0:T(8,128)S(1)} %get-tuple-element.62.denom_in, ...), custom_call_target="tpu_custom_call" | custom-call | flops 268435456 | bytes 6369280 | tf_op jit(solution)/shard_map/attention/pallas_call | solution.py:299
  57.6 0.0 copy-done.12
  57.6 1.0 copy-done.16
  58.6 8.8 %psum.7.stats = f32[8,256]{1,0:T(8,128)S(1)} all-reduce(f32[8,256]{1,0:T(8,128)S(1)} %get-tuple-element.68), channel_id=1, replica_groups=mesh['chip'=32,'core'=2,'head'=4] {'head'}, use_global_device_ids=true, to_apply=%region_0.0 | all-reduce | flops 2048 | bytes 16384 | tf_op jit(solution)/shard_map/psum | solution.py:375
  67.4 0.0 copy-start.9
  67.4 1.0 copy-done.9
  68.5 1.2 %copy-done.17 = f32[256,1024]{1,0:T(8,128)S(1)} copy-done((f32[256,1024]{1,0:T(8,128)S(1)}, f32[256,1024]{1,0:T(8,128)}, u32[]{:S(2)}) %copy-start.17) | copy-done | bytes 1048600
  69.7 0.0 copy-start.15
  69.7 1.6 %gradient.1 = (f32[256,1024]{1,0:T(8,128)S(1)}, f32[256,1024]{1,0:T(8,128)S(1)}, f32[32,17,128]{2,1,0:T(8,128)S(1)}, f32[32,17,128]{2,1,0:T(8,128)S(1)}) custom-call(s32[1]{0:T(128)} %bitcast.core, bf16[256,1024]{1,0:T(8,128)(2,1)S(1)} %get-tuple-element.60.query_feat, f32[256,1024]{1,0:T(8,128)S(1)} %get-tuple-element.66.attn_in.attn, ...), custom_call_target="tpu_custom_call" | custom-call | flops 67108864 | bytes 5812224 | tf_op jit(solution)/shard_map/gradient/pallas_call | solution.py:299
  71.4 2.5 %collective-permute-start.3 = (f32[32,17,128]{2,1,0:T(8,128)S(1)}, f32[32,17,128]{2,1,0:T(8,128)S(1)}, u32[]{:S(2)}, u32[]{:S(2)}) collective-permute-start(f32[32,17,128]{2,1,0:T(8,128)S(1)} %get-tuple-element.73), channel_id=1, source_target_pairs={{0,4},{4,0},{1,5},{5,1},{2,6},{6,2},{3,7},{7,3},{8,12},{12,8},{9,1... | collective-permute-start | bytes 835592 | tf_op jit(solution)/shard_map/ppermute | solution.py:312
  73.8 0.1 collective-permute-start.4
  73.9 0.0 copy-done.5
  73.9 0.0 copy-done.13
  73.9 0.0 copy-done.15
  74.0 3.6 %inside_backward.1 = (bf16[256,1024]{1,0:T(8,128)(2,1)}, bf16[256,1024]{1,0:T(8,128)(2,1)}, f32[256,1024]{1,0:T(8,128)S(1)}, f32[256,1024]{1,0:T(8,128)S(1)}) custom-call(s32[1]{0:T(128)} %bitcast.core, bf16[256,1024]{1,0:T(8,128)(2,1)S(1)} %copy-done.5, bf16[256,1024]{1,0:T(8,128)(2,1)S(1)} %get-tuple-element.60.query_feat, ...), custom_call_target="tpu_custom_call" | custom-call | flops 738197504 | bytes 10563584 | tf_op jit(solution)/shard_map/inside_backward/pallas_call | solution.py:299
  77.5 0.0 collective-permute-done.3.extra
  77.5 0.0 collective-permute-done.4.extra_got
  77.6 16.4 %all_to_all.22.spread = f32[32,17,128]{2,1,0:T(8,128)S(1)} all-to-all(f32[32,17,128]{2,1,0:T(8,128)S(1)} %add.9), channel_id=1, replica_groups=mesh['chip'=32,'core'=2,'head'=4] {'chip'}, dimensions={0} | all-to-all | bytes 557056 | tf_op jit(solution)/shard_map/all_to_all | solution.py:414
  94.1 18.2 %all_to_all.23.kept = f32[32,17,128]{2,1,0:T(8,128)S(1)} all-to-all(f32[32,17,128]{2,1,0:T(8,128)S(1)} %chip_sums.3), channel_id=1, replica_groups=mesh['chip'=32,'core'=2,'head'=4] {'chip'}, dimensions={0} | all-to-all | bytes 557056 | tf_op jit(solution)/shard_map/all_to_all | solution.py:415
  112.3 4.6 %collective-permute-start.5 = (f32[32,17,128]{2,1,0:T(8,128)S(1)}, f32[32,17,128]{2,1,0:T(8,128)S(1)}, u32[]{:S(2)}, u32[]{:S(2)}) collective-permute-start(f32[32,17,128]{2,1,0:T(8,128)S(1)} %all_to_all.23.kept), channel_id=1, source_target_pairs={{0,4},{4,0},{1,5},{5,1},{2,6},{6,2},{3,7},{7,3},{8,12},{12,8},{9,1... | collective-permute-start | bytes 835592 | tf_op jit(solution)/shard_map/ppermute | solution.py:312
  116.9 1.3 %collective-permute-done.5.got = f32[32,17,128]{2,1,0:T(8,128)S(1)} collective-permute-done((f32[32,17,128]{2,1,0:T(8,128)S(1)}, f32[32,17,128]{2,1,0:T(8,128)S(1)}, u32[]{:S(2)}, u32[]{:S(2)}) %collective-permute-start.5) | collective-permute-done | bytes 278560 | tf_op jit(solution)/shard_map/ppermute | solution.py:312
  118.3 1.6 %outside_backward.1 = (bf16[256,1024]{1,0:T(8,128)(2,1)}, bf16[256,1024]{1,0:T(8,128)(2,1)}) custom-call(s32[1]{0:T(128)} %bitcast.core, bf16[256,1024]{1,0:T(8,128)(2,1)S(1)} %copy-done.3, bf16[256,1024]{1,0:T(8,128)(2,1)S(1)} %copy-done.7, bf16[256,1024]{1,0:T(8,128)(2,1)S(1)} %copy-done.1, f32[256,1024]{1,0:T(8,128)S(1)} %get-tuple-element.85.key_part, ...), custom_call_target="tpu_custom_call" | custom-call | flops 268435456 | bytes 5832704 | tf_op jit(solution)/shard_map/outside_backward/pallas_call | solution.py:299
  (17 shorter events, 0.2 us)
Async XLA Ops:
  0.6 1.0 copy-start
  1.7 1.0 copy-start.2
  2.7 5.5 %copy-start.1 = (bf16[256,1024]{1,0:T(8,128)(2,1)S(1)}, bf16[256,1024]{1,0:T(8,128)(2,1)}, u32[]{:S(2)}) copy-start(bf16[256,1024]{1,0:T(8,128)(2,1)} %values.6) | copy-start | bytes 1572868
  2.7 5.5 %copy-start.3 = (bf16[256,1024]{1,0:T(8,128)(2,1)S(1)}, bf16[256,1024]{1,0:T(8,128)(2,1)}, u32[]{:S(2)}) copy-start(bf16[256,1024]{1,0:T(8,128)(2,1)} %keys.4) | copy-start | bytes 1572868
  4.8 5.6 %collective-permute-start = (f32[32,17,128]{2,1,0:T(8,128)S(1)}, f32[32,17,128]{2,1,0:T(8,128)S(1)}, u32[]{:S(2)}, u32[]{:S(2)}) collective-permute-start(f32[32,17,128]{2,1,0:T(8,128)S(1)} %get-tuple-element.50), channel_id=1, source_target_pairs={{0,4},{4,0},{1,5},{5,1},{2,6},{6,2},{3,7},{7,3},{8,12},{12,8},{9,1... | collective-permute-start | bytes 835592 | tf_op jit(solution)/shard_map/ppermute | solution.py:312
  8.2 2.2 %collective-permute-start.1 = (f32[32,17,128]{2,1,0:T(8,128)S(1)}, f32[32,17,128]{2,1,0:T(8,128)S(1)}, u32[]{:S(2)}, u32[]{:S(2)}) collective-permute-start(f32[32,17,128]{2,1,0:T(8,128)S(1)} %get-tuple-element.63), channel_id=1, source_target_pairs={{0,4},{4,0},{1,5},{5,1},{2,6},{6,2},{3,7},{7,3},{8,12},{12,8},{9,1... | collective-permute-start | bytes 835592 | tf_op jit(solution)/shard_map/ppermute | solution.py:312
  8.3 1.0 copy-start.4
  10.4 0.8 copy-start.6
  10.4 21.7 %copy-start.14 = (bf16[256,2048]{1,0:T(8,128)(2,1)}, bf16[256,2048]{1,0:T(8,128)(2,1)S(1)}, u32[]{:S(2)}) copy-start(bf16[256,2048]{1,0:T(8,128)(2,1)S(1)} %get-tuple-element.76.low) | copy-start | bytes 3145732
  10.4 46.0 %copy-start.10 = (f32[32,17,128]{2,1,0:T(8,128)}, f32[32,17,128]{2,1,0:T(8,128)S(1)}, u32[]{:S(2)}) copy-start(f32[32,17,128]{2,1,0:T(8,128)S(1)} %collective-permute-done.1.extra_got) | copy-start | bytes 835588
  32.1 24.3 %copy-start.8 = (bf16[256,1024]{1,0:T(8,128)(2,1)S(1)}, bf16[256,1024]{1,0:T(8,128)(2,1)}, u32[]{:S(2)}) copy-start(bf16[256,1024]{1,0:T(8,128)(2,1)} %out_grad.3) | copy-start | bytes 1572868
  32.1 24.3 %copy-start.18 = (f32[1024]{0:T(1024)S(1)}, f32[1024]{0:T(1024)}, u32[]{:S(2)}) copy-start(f32[1024]{0:T(1024)} %param.8) | copy-start | bytes 12292
  50.4 6.0 %collective-permute-start.2 = (f32[32,17,128]{2,1,0:T(8,128)S(1)}, f32[32,17,128]{2,1,0:T(8,128)S(1)}, u32[]{:S(2)}, u32[]{:S(2)}) collective-permute-start(f32[32,17,128]{2,1,0:T(8,128)S(1)} %all_to_all.21.kept), channel_id=1, source_target_pairs={{0,4},{4,0},{1,5},{5,1},{2,6},{6,2},{3,7},{7,3},{8,12},{12,8},{9,1... | collective-permute-start | bytes 835592 | tf_op jit(solution)/shard_map/ppermute | solution.py:312
  56.4 1.2 %copy-start.12 = (f32[32,17,128]{2,1,0:T(8,128)}, f32[32,17,128]{2,1,0:T(8,128)S(1)}, u32[]{:S(2)}) copy-start(f32[32,17,128]{2,1,0:T(8,128)S(1)} %collective-permute-done.2.got) | copy-start | bytes 835588
  57.6 1.0 copy-start.16
  67.4 1.0 copy-start.9
  68.5 1.2 %copy-start.17 = (f32[256,1024]{1,0:T(8,128)S(1)}, f32[256,1024]{1,0:T(8,128)}, u32[]{:S(2)}) copy-start(f32[256,1024]{1,0:T(8,128)} %copy-done.16) | copy-start | bytes 3145732
  69.7 4.2 %copy-start.5 = (bf16[256,1024]{1,0:T(8,128)(2,1)S(1)}, bf16[256,1024]{1,0:T(8,128)(2,1)}, u32[]{:S(2)}) copy-start(bf16[256,1024]{1,0:T(8,128)(2,1)} %queries.2) | copy-start | bytes 1572868
  69.7 4.2 %copy-start.7 = (bf16[256,1024]{1,0:T(8,128)(2,1)S(1)}, bf16[256,1024]{1,0:T(8,128)(2,1)}, u32[]{:S(2)}) copy-start(bf16[256,1024]{1,0:T(8,128)(2,1)} %copy-done.6) | copy-start | bytes 1572868
  69.7 4.2 %copy-start.11 = (f32[32,17,128]{2,1,0:T(8,128)S(1)}, f32[32,17,128]{2,1,0:T(8,128)}, u32[]{:S(2)}) copy-start(f32[32,17,128]{2,1,0:T(8,128)} %copy-done.10) | copy-start | bytes 835588
  69.7 4.2 %copy-start.13 = (f32[32,17,128]{2,1,0:T(8,128)S(1)}, f32[32,17,128]{2,1,0:T(8,128)}, u32[]{:S(2)}) copy-start(f32[32,17,128]{2,1,0:T(8,128)} %copy-done.12) | copy-start | bytes 835588
  69.7 4.2 %copy-start.15 = (bf16[256,2048]{1,0:T(8,128)(2,1)S(1)}, bf16[256,2048]{1,0:T(8,128)(2,1)}, u32[]{:S(2)}) copy-start(bf16[256,2048]{1,0:T(8,128)(2,1)} %copy-done.14) | copy-start | bytes 3145732
  71.4 6.2 %collective-permute-start.3 = (f32[32,17,128]{2,1,0:T(8,128)S(1)}, f32[32,17,128]{2,1,0:T(8,128)S(1)}, u32[]{:S(2)}, u32[]{:S(2)}) collective-permute-start(f32[32,17,128]{2,1,0:T(8,128)S(1)} %get-tuple-element.73), channel_id=1, source_target_pairs={{0,4},{4,0},{1,5},{5,1},{2,6},{6,2},{3,7},{7,3},{8,12},{12,8},{9,1... | collective-permute-start | bytes 835592 | tf_op jit(solution)/shard_map/ppermute | solution.py:312
  73.8 3.7 %collective-permute-start.4 = (f32[32,17,128]{2,1,0:T(8,128)S(1)}, f32[32,17,128]{2,1,0:T(8,128)S(1)}, u32[]{:S(2)}, u32[]{:S(2)}) collective-permute-start(f32[32,17,128]{2,1,0:T(8,128)S(1)} %get-tuple-element.87), channel_id=1, source_target_pairs={{0,4},{4,0},{1,5},{5,1},{2,6},{6,2},{3,7},{7,3},{8,12},{12,8},{9,1... | collective-permute-start | bytes 835592 | tf_op jit(solution)/shard_map/ppermute | solution.py:312
  112.3 6.0 %collective-permute-start.5 = (f32[32,17,128]{2,1,0:T(8,128)S(1)}, f32[32,17,128]{2,1,0:T(8,128)S(1)}, u32[]{:S(2)}, u32[]{:S(2)}) collective-permute-start(f32[32,17,128]{2,1,0:T(8,128)S(1)} %all_to_all.23.kept), channel_id=1, source_target_pairs={{0,4},{4,0},{1,5},{5,1},{2,6},{6,2},{3,7},{7,3},{8,12},{12,8},{9,1... | collective-permute-start | bytes 835592 | tf_op jit(solution)/shard_map/ppermute | solution.py:312

commit v2 on v1

--- a/solution.py
+++ b/solution.py
@@ -11,7 +11,8 @@
 HEADS = 32
 HEAD_DIM = 128
 CORES = 2
-ROWS = 16
+SIDE = 4
+ROWS = 64
 BLOCK = 256
 BLOCKS = HEAD_DIM // ROWS
 
@@ -170,11 +171,14 @@
 
 
 def gradient_kernel(
-    core, query_feat, attn_in, inverse_in, gain, out_grad, stats, numer_out, denom_out, mine, theirs
+    core, query_feat, attn_in, inverse_in, gain, out_grad, stats, stats_a, stats_b, stats_c,
+    numer_out, denom_out, mine, theirs, stats_out,
 ):
     width = query_feat.shape[1]
     heads_side = width // HEAD_DIM // CORES
-    scale, slope = token_scales(stats[...], HEADS * HEAD_DIM)
+    total = (stats[...] + stats_a[...]) + (stats_b[...] + stats_c[...])
+    stats_out[...] = total
+    scale, slope = token_scales(total, HEADS * HEAD_DIM)
     for wire, side in ((theirs, 1 - core[0]), (mine, core[0])):
         clear_rows(wire)
         for place in range(heads_side):
@@ -265,9 +269,20 @@
         copy.wait()
 
 
-def chip_sums_kernel(backward, spread, sums):
+def row_total_kernel(spread, total):
+    value = spread[0]
+    for chip in range(1, spread.shape[0]):
+        value = value + spread[chip]
+    total[...] = value
+
+
+def chip_sums_kernel(backward, row, spread, *rest):
+    *others, sums = rest
     chips = spread.shape[0]
     total = jnp.zeros(spread.shape[1:], f32)
+    for step, other in enumerate(others, 1):
+        inside = row[0] + step < SIDE if backward else row[0] >= step
+        total = total + jnp.where(inside, other[...], 0.0)
     for step in range(chips):
         chip = chips - 1 - step if backward else step
         sums[chip] = total
@@ -312,18 +327,31 @@
     return lax.ppermute(array, "core", [(0, 1), (1, 0)])
 
 
-def chip_sums(spread, backward):
+def shifted(array, axis, step):
+    size = lax.axis_size(axis)
+    return lax.ppermute(array, axis, [(i, (i + step) % size) for i in range(size)])
+
+
+def scan_chips(pair, row, backward, inside):
+    spread = lax.all_to_all(pair, "z", 0, 0)
+    total = call(row_total_kernel, "row_total", shaped(spread.shape[1:], f32), spread)
+    sign = -1 if backward else 1
+    others = [shifted(total, "x", sign * step) for step in range(1, SIDE)]
+    total, done = lax.optimization_barrier((total, inside[1:]))
+    done = inside[0](*done)
+    others, spread, done = lax.optimization_barrier((others, spread, done))
     kernel = functools.partial(chip_sums_kernel, backward)
-    return call(kernel, "chip_sums", shaped(spread.shape, f32), spread)
+    sums = call(kernel, "chip_sums", shaped(spread.shape, f32), spread, *others, core=row)
+    return lax.all_to_all(sums, "z", 0, 0), done
 
 
 def body(queries, key_rows, value_rows, norm_gain, out_grad):
     tokens, width = queries.shape
     heads = width // HEAD_DIM
-    chips = lax.axis_size("chip")
     core = lax.axis_index("core").astype(jnp.int32).reshape(1)
+    row = lax.axis_index("x").astype(jnp.int32).reshape(1)
     gain = norm_gain.reshape(1, width)
-    wire = shaped((chips, ROWS + 1, HEAD_DIM), f32)
+    wire = shaped((lax.axis_size("z"), ROWS + 1, HEAD_DIM), f32)
     narrow = shaped((tokens, width), bf16)
     full = shaped((tokens, width), f32)
     unit = 2 * tokens * HEAD_DIM * HEAD_DIM * heads
@@ -339,24 +367,23 @@
         hbm_in=(0, 1),
         slots=heads,
     )
-    theirs, mine, q_in, k_in, v_in = lax.optimization_barrier(
-        (theirs, mine, queries, key_rows, value_rows)
-    )
     extra = swap_cores(theirs)
     extra_got = swap_cores(mine)
-    inside = call(
-        inside_forward_kernel,
-        "inside_forward",
-        (narrow, narrow, shaped((tokens, heads * tokens), bf16), full, full),
-        q_in,
-        k_in,
-        v_in,
-        flops=4 * unit,
-    )
-    extra, extra_got, mine, inside = lax.optimization_barrier((extra, extra_got, mine, inside))
+    extra, extra_got, mine = lax.optimization_barrier((extra, extra_got, mine))
+
+    def inside_forward(*operands):
+        return call(
+            inside_forward_kernel,
+            "inside_forward",
+            (narrow, narrow, shaped((tokens, heads * tokens), bf16), full, full),
+            *operands,
+            flops=4 * unit,
+        )
+
+    kept, inside = scan_chips(
+        mine + extra, row, False, (inside_forward, queries, key_rows, value_rows)
+    )
     query_feat, key_feat, low, numer_in, denom_in = inside
-    spread = lax.all_to_all(mine + extra, "chip", 0, 0)
-    kept = lax.all_to_all(chip_sums(spread, False), "chip", 0, 0)
     got = swap_cores(kept)
     prefix = (kept, got, extra, extra_got)
     attn, inverse, stats = call(
@@ -372,47 +399,40 @@
         core=core,
         flops=4 * unit,
     )
-    stats = lax.psum(stats, "head")
-    d_numer, d_denom, mine, theirs = call(
+    stats_from = [shifted(stats, "head", step) for step in (2, 1, 3)]
+    d_numer, d_denom, mine, theirs, stats = call(
         gradient_kernel,
         "gradient",
-        (full, full, wire, wire),
+        (full, full, wire, wire, shaped((8, tokens), f32)),
         query_feat,
         attn,
         inverse,
         gain,
         out_grad,
         stats,
+        *stats_from,
         core=core,
         flops=unit,
     )
-    theirs, mine, d_numer, d_denom = lax.optimization_barrier((theirs, mine, d_numer, d_denom))
     extra = swap_cores(theirs)
     extra_got = swap_cores(mine)
-    inside = call(
-        inside_backward_kernel,
-        "inside_backward",
-        (narrow, narrow, full, full),
-        queries,
-        query_feat,
-        key_feat,
-        value_rows,
-        low,
-        d_numer,
-        d_denom,
-        attn,
-        gain,
-        stats,
-        *prefix,
-        core=core,
-        flops=11 * unit,
-        hbm_out=(0, 1),
-        slots=heads,
-    )
-    extra, extra_got, mine, inside = lax.optimization_barrier((extra, extra_got, mine, inside))
+    extra, extra_got, mine = lax.optimization_barrier((extra, extra_got, mine))
+
+    def inside_backward(*operands):
+        return call(
+            inside_backward_kernel,
+            "inside_backward",
+            (narrow, narrow, full, full),
+            *operands,
+            core=core,
+            flops=11 * unit,
+            hbm_out=(0, 1),
+            slots=heads,
+        )
+
+    operands = (queries, query_feat, key_feat, value_rows, low, d_numer, d_denom, attn, gain, stats)
+    kept, inside = scan_chips(mine + extra, row, True, (inside_backward,) + operands + prefix)
     normed, query_grad, key_part, value_part = inside
-    spread = lax.all_to_all(mine + extra, "chip", 0, 0)
-    kept = lax.all_to_all(chip_sums(spread, True), "chip", 0, 0)
     got = swap_cores(kept)
     key_grad, value_grad = call(
         outside_backward_kernel,
@@ -438,10 +458,10 @@
 def solution(mesh):
     devices = mesh.devices
     fine = Mesh(
-        devices.reshape(devices.shape[0] // CORES, CORES, devices.shape[1]),
-        ("chip", "core", "head"),
-    )
-    rows = P(("chip", "core"), "head")
+        devices.reshape(SIDE, devices.shape[0] // (SIDE * CORES), CORES, devices.shape[1]),
+        ("x", "z", "core", "head"),
+    )
+    rows = P(("x", "z", "core"), "head")
     return jax.shard_map(
         body,
         mesh=fine,

time: 120 us -> 108 us (0.900)
  blocking collectives: 82.6 us -> 58.7 us
  starting transfers between devices: 15.3 us -> 24 us
  waiting for transfers between devices: 2.71 us -> 10.3 us
  local copies, waits for them, and re-layouts: 7.1 us -> 2.1 us
    all_to_all x4, blocking collectives: 73.8 us -> 58.7 us  [the longest x2 33.8 us: scan_chips(): spread = lax.all_to_all(pair, 'z', 0, 0)]
    ppermute x0 -> x9, starting transfers between devices: none -> 11.5 us  [shifted(): lax.ppermute(array, axis, [(i, (i + step) % size) for i in range(size)])]
    psum x1 -> x0, blocking collectives: 8.81 us -> none  [body(): stats = lax.psum(stats, 'head')]
    unnamed x38 -> x14, local copies, waits for them, and re-layouts: 7.1 us -> 2.1 us
    ppermute x0 -> x9, waiting for transfers between devices: none -> 4.87 us  [shifted(): lax.ppermute(array, axis, [(i, (i + step) % size) for i in range(size)])]
    ppermute x6, waiting for transfers between devices: 2.71 us -> 5.48 us  [swap_cores(): return lax.ppermute(array, 'core', [(0, 1), (1, 0)])]
    ppermute x6, starting transfers between devices: 15.3 us -> 12.6 us  [swap_cores(): return lax.ppermute(array, 'core', [(0, 1), (1, 0)])]
    pallas_call x8 -> x10, Pallas kernels: 11.2 us -> 11.2 us  [call(): pl.pallas_call(kernel, out_shape=out_shape, in_specs=in_specs, out_specs=...]
  transfers between devices with their start and end apart: 6 -> 15, of which waited for: 2 -> 10; matrix products, arithmetic and copies ran while one was open for 0% -> 0% of each run, Pallas kernels for 4% -> 4%
where the time goes in v2:
time: 108 us; the launch traced here: 107 us
  blocking collectives  58.7 us (54%)
  starting transfers between devices  24 us (22%)
  Pallas kernels  11.2 us (10%)
  waiting for transfers between devices  10.3 us (10%)
  local copies, waits for them, and re-layouts  2.1 us (2%)
    all_to_all x2, blocking collectives, scan_chips(): spread = lax.all_to_all(pair, 'z', 0, 0)  33.8 us
    all_to_all x2, blocking collectives, scan_chips(): return (lax.all_to_all(sums, 'z', 0, 0), done)  25 us
    ppermute x6, starting transfers between devices, swap_cores(): return lax.ppermute(array, 'core', [(0, 1), (1, 0)])  12.6 us
    ppermute x9, starting transfers between devices, shifted(): lax.ppermute(array, axis, [(i, (i + step) % size) for i in range(size)])  11.5 us
    pallas_call x10, Pallas kernels, call(): pl.pallas_call(kernel, out_shape=out_shape, in_specs=in_specs, out_specs=...  11.2 us
    ppermute x6, waiting for transfers between devices, swap_cores(): return lax.ppermute(array, 'core', [(0, 1), (1, 0)])  5.48 us
    ppermute x9, waiting for transfers between devices, shifted(): lax.ppermute(array, axis, [(i, (i + step) % size) for i in range(size)])  4.87 us
  transfers between devices with their start and end apart: 15, of which 10 were waited for; matrix products, arithmetic and copies ran while one was open for 0% of the time, Pallas kernels for 4%

profile of v2, /device:TPU:1, one launch (start us, length us, event | category | flops | bytes accessed | tf_op | source)
XLA Modules:
  0.0 107.5 jit_solution(7097462475207020846)
XLA Ops:
  0.6 0.0 copy-start
  0.6 1.0 copy-done
  1.7 1.0 copy-done.2
  2.7 2.1 %states.1 = (f32[8,65,128]{2,1,0:T(8,128)S(1)}, f32[8,65,128]{2,1,0:T(8,128)S(1)}) custom-call(s32[1]{0:T(128)} %bitcast.core, bf16[256,1024]{1,0:T(8,128)(2,1)S(1)} %copy-done.2, bf16[256,1024]{1,0:T(8,128)(2,1)S(1)} %copy-done), custom_call_target="tpu_custom_call" | custom-call | flops 67108864 | bytes 1581056 | tf_op jit(solution)/shard_map/states/pallas_call | solution.py:314
  4.8 3.3 %collective-permute-start = (f32[8,65,128]{2,1,0:T(8,128)S(1)}, f32[8,65,128]{2,1,0:T(8,128)S(1)}, u32[]{:S(2)}, u32[]{:S(2)}) collective-permute-start(f32[8,65,128]{2,1,0:T(8,128)S(1)} %get-tuple-element.65), channel_id=1, source_target_pairs={{0,4},{4,0},{1,5},{5,1},{2,6},{6,2},{3,7},{7,3},{8,12},{12,8},{9,1... | collective-permute-start | bytes 798728 | tf_op jit(solution)/shard_map/ppermute | solution.py:327
  8.1 0.1 collective-permute-start.1
  8.2 1.1 %collective-permute-done.extra = f32[8,65,128]{2,1,0:T(8,128)S(1)} collective-permute-done((f32[8,65,128]{2,1,0:T(8,128)S(1)}, f32[8,65,128]{2,1,0:T(8,128)S(1)}, u32[]{:S(2)}, u32[]{:S(2)}) %collective-permute-start) | collective-permute-done | bytes 266272 | tf_op jit(solution)/shard_map/ppermute | solution.py:327
  9.4 0.4 collective-permute-done.1.extra_got
  9.8 0.0 copy-start.1
  9.8 18.6 %all_to_all.20.spread = f32[8,65,128]{2,1,0:T(8,128)S(1)} all-to-all(f32[8,65,128]{2,1,0:T(8,128)S(1)} %add.6), channel_id=1, replica_groups=mesh['x'=4,'z'=8,'core'=2,'head'=4] {'z'}, dimensions={0} | all-to-all | bytes 532480 | tf_op jit(solution)/shard_map/all_to_all | solution.py:336
  28.4 2.6 %collective-permute-start.4 = (f32[65,128]{1,0:T(8,128)S(1)}, f32[65,128]{1,0:T(8,128)S(1)}, u32[]{:S(2)}, u32[]{:S(2)}) collective-permute-start(f32[65,128]{1,0:T(8,128)S(1)} %row_total.2), channel_id=1, source_target_pairs={{0,192},{64,0},{128,64},{192,128},{1,193},{65,1},{129,65},{193,129... | collective-permute-start | bytes 99848 | tf_op jit(solution)/shard_map/ppermute | solution.py:332
  31.0 0.5 collective-permute-start.3
  31.5 0.6 collective-permute-start.2
  32.1 0.0 copy-done.3
  32.1 0.0 copy-done.4
  32.1 1.1 inside_forward.1
  33.2 0.0 collective-permute-done.4.rest_2_
  33.2 2.1 %collective-permute-done.3.rest_1_ = f32[65,128]{1,0:T(8,128)S(1)} collective-permute-done((f32[65,128]{1,0:T(8,128)S(1)}, f32[65,128]{1,0:T(8,128)S(1)}, u32[]{:S(2)}, u32[]{:S(2)}) %collective-permute-start.3) | collective-permute-done | bytes 33312 | tf_op jit(solution)/shard_map/ppermute | solution.py:332
  35.3 0.4 collective-permute-done.2.rest_0_
  35.7 0.0 copy-start.6
  35.7 12.2 %all_to_all.21.kept = f32[8,65,128]{2,1,0:T(8,128)S(1)} all-to-all(f32[8,65,128]{2,1,0:T(8,128)S(1)} %chip_sums.2), channel_id=1, replica_groups=mesh['x'=4,'z'=8,'core'=2,'head'=4] {'z'}, dimensions={0} | all-to-all | bytes 532480 | tf_op jit(solution)/shard_map/all_to_all | solution.py:345
  47.9 4.0 %collective-permute-start.5 = (f32[8,65,128]{2,1,0:T(8,128)S(1)}, f32[8,65,128]{2,1,0:T(8,128)S(1)}, u32[]{:S(2)}, u32[]{:S(2)}) collective-permute-start(f32[8,65,128]{2,1,0:T(8,128)S(1)} %all_to_all.21.kept), channel_id=1, source_target_pairs={{0,4},{4,0},{1,5},{5,1},{2,6},{6,2},{3,7},{7,3},{8,12},{12,8},{9,1... | collective-permute-start | bytes 798728 | tf_op jit(solution)/shard_map/ppermute | solution.py:327
  52.0 1.2 %collective-permute-done.5.got = f32[8,65,128]{2,1,0:T(8,128)S(1)} collective-permute-done((f32[8,65,128]{2,1,0:T(8,128)S(1)}, f32[8,65,128]{2,1,0:T(8,128)S(1)}, u32[]{:S(2)}, u32[]{:S(2)}) %collective-permute-start.5) | collective-permute-done | bytes 266272 | tf_op jit(solution)/shard_map/ppermute | solution.py:327
  53.2 0.0 copy-done.6
  53.2 1.2 %attention.1 = (f32[256,1024]{1,0:T(8,128)S(1)}, f32[256,1024]{1,0:T(8,128)S(1)}, f32[8,256]{1,0:T(8,128)S(1)}) custom-call(s32[1]{0:T(128)} %bitcast.core, bf16[256,1024]{1,0:T(8,128)(2,1)S(1)} %get-tuple-element.98.query_feat, f32[256,1024]{1,0:T(8,128)S(1)} %get-tuple-element.78.numer_in, f32[256,1024]{1,0:T(8,128)S(1)} %get-tuple-element.79.denom_in, ...), custom_call_target="tpu_custom_call" | custom-call | flops 268435456 | bytes 6320128 | tf_op jit(solution)/shard_map/attention/pallas_call | solution.py:314
  54.4 2.8 %collective-permute-start.8 = (f32[8,256]{1,0:T(8,128)S(1)}, f32[8,256]{1,0:T(8,128)S(1)}, u32[]{:S(2)}, u32[]{:S(2)}) collective-permute-start(f32[8,256]{1,0:T(8,128)S(1)} %get-tuple-element.87.stats), channel_id=1, source_target_pairs={{0,3},{1,0},{2,1},{3,2},{4,7},{5,4},{6,5},{7,6},{8,11},{9,8},{10,9... | collective-permute-start | bytes 24584 | tf_op jit(solution)/shard_map/ppermute | solution.py:332
  57.1 0.0 collective-permute-start.7
  57.1 1.6 %collective-permute-start.6 = (f32[8,256]{1,0:T(8,128)S(1)}, f32[8,256]{1,0:T(8,128)S(1)}, u32[]{:S(2)}, u32[]{:S(2)}) collective-permute-start(f32[8,256]{1,0:T(8,128)S(1)} %get-tuple-element.87.stats), channel_id=1, source_target_pairs={{0,2},{1,3},{2,0},{3,1},{4,6},{5,7},{6,4},{7,5},{8,10},{9,11},{10,... | collective-permute-start | bytes 24584 | tf_op jit(solution)/shard_map/ppermute | solution.py:332
  58.8 0.0 collective-permute-done.8.stats_c
  58.8 2.1 %collective-permute-done.7.stats_b = f32[8,256]{1,0:T(8,128)S(1)} collective-permute-done((f32[8,256]{1,0:T(8,128)S(1)}, f32[8,256]{1,0:T(8,128)S(1)}, u32[]{:S(2)}, u32[]{:S(2)}) %collective-permute-start.7) | collective-permute-done | bytes 8224 | tf_op jit(solution)/shard_map/ppermute | solution.py:332
  60.8 0.3 collective-permute-done.6.stats_a
  61.1 1.7 %gradient.1 = (f32[256,1024]{1,0:T(8,128)S(1)}, f32[256,1024]{1,0:T(8,128)S(1)}, f32[8,65,128]{2,1,0:T(8,128)S(1)}, f32[8,65,128]{2,1,0:T(8,128)S(1)}, f32[8,256]{1,0:T(8,128)S(1)}) custom-call(s32[1]{0:T(128)} %bitcast.core, bf16[256,1024]{1,0:T(8,128)(2,1)S(1)} %get-tuple-element.98.query_feat, f32[256,1024]{1,0:T(8,128)S(1)} %get-tuple-element.104.attn_in.attn, ...), custom_call_target="tpu_custom_call" | custom-call | flops 67108864 | bytes 5820416 | tf_op jit(solution)/shard_map/gradient/pallas_call | solution.py:314
  62.8 1.9 %collective-permute-start.9 = (f32[8,65,128]{2,1,0:T(8,128)S(1)}, f32[8,65,128]{2,1,0:T(8,128)S(1)}, u32[]{:S(2)}, u32[]{:S(2)}) collective-permute-start(f32[8,65,128]{2,1,0:T(8,128)S(1)} %get-tuple-element.88), channel_id=1, source_target_pairs={{0,4},{4,0},{1,5},{5,1},{2,6},{6,2},{3,7},{7,3},{8,12},{12,8},{9,1... | collective-permute-start | bytes 798728 | tf_op jit(solution)/shard_map/ppermute | solution.py:327
  64.7 0.1 collective-permute-start.10
  64.8 1.1 %collective-permute-done.9.extra = f32[8,65,128]{2,1,0:T(8,128)S(1)} collective-permute-done((f32[8,65,128]{2,1,0:T(8,128)S(1)}, f32[8,65,128]{2,1,0:T(8,128)S(1)}, u32[]{:S(2)}, u32[]{:S(2)}) %collective-permute-start.9) | collective-permute-done | bytes 266272 | tf_op jit(solution)/shard_map/ppermute | solution.py:327
  65.9 0.4 collective-permute-done.10.extra_got
  66.3 15.2 %all_to_all.22.spread = f32[8,65,128]{2,1,0:T(8,128)S(1)} all-to-all(f32[8,65,128]{2,1,0:T(8,128)S(1)} %add.7), channel_id=1, replica_groups=mesh['x'=4,'z'=8,'core'=2,'head'=4] {'z'}, dimensions={0} | all-to-all | bytes 532480 | tf_op jit(solution)/shard_map/all_to_all | solution.py:336
  81.6 0.1 collective-permute-start.13
  81.7 1.3 %collective-permute-start.12 = (f32[65,128]{1,0:T(8,128)S(1)}, f32[65,128]{1,0:T(8,128)S(1)}, u32[]{:S(2)}, u32[]{:S(2)}) collective-permute-start(f32[65,128]{1,0:T(8,128)S(1)} %row_total.3), channel_id=1, source_target_pairs={{0,128},{64,192},{128,0},{192,64},{1,129},{65,193},{129,1},{193,65... | collective-permute-start | bytes 99848 | tf_op jit(solution)/shard_map/ppermute | solution.py:332
  83.0 2.0 %collective-permute-start.11 = (f32[65,128]{1,0:T(8,128)S(1)}, f32[65,128]{1,0:T(8,128)S(1)}, u32[]{:S(2)}, u32[]{:S(2)}) collective-permute-start(f32[65,128]{1,0:T(8,128)S(1)} %row_total.3), channel_id=1, source_target_pairs={{0,192},{64,0},{128,64},{192,128},{1,193},{65,1},{129,65},{193,129... | collective-permute-start | bytes 99848 | tf_op jit(solution)/shard_map/ppermute | solution.py:332
  85.0 3.5 %inside_backward.1 = (bf16[256,1024]{1,0:T(8,128)(2,1)}, bf16[256,1024]{1,0:T(8,128)(2,1)}, f32[256,1024]{1,0:T(8,128)S(1)}, f32[256,1024]{1,0:T(8,128)S(1)}) custom-call(s32[1]{0:T(128)} %bitcast.core, bf16[256,1024]{1,0:T(8,128)(2,1)S(1)} %copy-done.4, bf16[256,1024]{1,0:T(8,128)(2,1)S(1)} %get-tuple-element.98.query_feat, ...), custom_call_target="tpu_custom_call" | custom-call | flops 738197504 | bytes 10514432 | tf_op jit(solution)/shard_map/inside_backward/pallas_call | solution.py:314
  88.5 0.0 collective-permute-done.13.rest_2_
  88.5 0.0 collective-permute-done.12.rest_1_
  88.5 0.0 collective-permute-done.11.rest_0_
  88.6 12.8 %all_to_all.23.kept = f32[8,65,128]{2,1,0:T(8,128)S(1)} all-to-all(f32[8,65,128]{2,1,0:T(8,128)S(1)} %chip_sums.3), channel_id=1, replica_groups=mesh['x'=4,'z'=8,'core'=2,'head'=4] {'z'}, dimensions={0} | all-to-all | bytes 532480 | tf_op jit(solution)/shard_map/all_to_all | solution.py:345
  101.4 3.1 %collective-permute-start.14 = (f32[8,65,128]{2,1,0:T(8,128)S(1)}, f32[8,65,128]{2,1,0:T(8,128)S(1)}, u32[]{:S(2)}, u32[]{:S(2)}) collective-permute-start(f32[8,65,128]{2,1,0:T(8,128)S(1)} %all_to_all.23.kept), channel_id=1, source_target_pairs={{0,4},{4,0},{1,5},{5,1},{2,6},{6,2},{3,7},{7,3},{8,12},{12,8},{9,1... | collective-permute-start | bytes 798728 | tf_op jit(solution)/shard_map/ppermute | solution.py:327
  104.5 1.2 %collective-permute-done.14.got = f32[8,65,128]{2,1,0:T(8,128)S(1)} collective-permute-done((f32[8,65,128]{2,1,0:T(8,128)S(1)}, f32[8,65,128]{2,1,0:T(8,128)S(1)}, u32[]{:S(2)}, u32[]{:S(2)}) %collective-permute-start.14) | collective-permute-done | bytes 266272 | tf_op jit(solution)/shard_map/ppermute | solution.py:327
  105.7 1.6 %outside_backward.1 = (bf16[256,1024]{1,0:T(8,128)(2,1)}, bf16[256,1024]{1,0:T(8,128)(2,1)}) custom-call(s32[1]{0:T(128)} %bitcast.core, bf16[256,1024]{1,0:T(8,128)(2,1)S(1)} %copy-done.3, bf16[256,1024]{1,0:T(8,128)(2,1)S(1)} %get-tuple-element.99.key_feat, bf16[256,1024]{1,0:T(8,128)(2,1)S(1)} %copy-done.1, f32[256,1024]{1,0:T(8,128)S(1)} %get-tuple-element.117.key_part, ...), custom_call_target="tpu_custom_call" | custom-call | flops 268435456 | bytes 5783552 | tf_op jit(solution)/shard_map/outside_backward/pallas_call | solution.py:314
  (12 shorter events, 0.2 us)
Async XLA Ops:
  0.6 1.0 copy-start
  1.7 1.0 copy-start.2
  4.8 4.5 %collective-permute-start = (f32[8,65,128]{2,1,0:T(8,128)S(1)}, f32[8,65,128]{2,1,0:T(8,128)S(1)}, u32[]{:S(2)}, u32[]{:S(2)}) collective-permute-start(f32[8,65,128]{2,1,0:T(8,128)S(1)} %get-tuple-element.65), channel_id=1, source_target_pairs={{0,4},{4,0},{1,5},{5,1},{2,6},{6,2},{3,7},{7,3},{8,12},{12,8},{9,1... | collective-permute-start | bytes 798728 | tf_op jit(solution)/shard_map/ppermute | solution.py:327
  8.1 1.6 %collective-permute-start.1 = (f32[8,65,128]{2,1,0:T(8,128)S(1)}, f32[8,65,128]{2,1,0:T(8,128)S(1)}, u32[]{:S(2)}, u32[]{:S(2)}) collective-permute-start(f32[8,65,128]{2,1,0:T(8,128)S(1)} %get-tuple-element.67), channel_id=1, source_target_pairs={{0,4},{4,0},{1,5},{5,1},{2,6},{6,2},{3,7},{7,3},{8,12},{12,8},{9,1... | collective-permute-start | bytes 798728 | tf_op jit(solution)/shard_map/ppermute | solution.py:327
  9.8 22.3 %copy-start.3 = (bf16[256,1024]{1,0:T(8,128)(2,1)S(1)}, bf16[256,1024]{1,0:T(8,128)(2,1)}, u32[]{:S(2)}) copy-start(bf16[256,1024]{1,0:T(8,128)(2,1)} %keys.4) | copy-start | bytes 1572868
  9.8 22.3 %copy-start.4 = (bf16[256,1024]{1,0:T(8,128)(2,1)S(1)}, bf16[256,1024]{1,0:T(8,128)(2,1)}, u32[]{:S(2)}) copy-start(bf16[256,1024]{1,0:T(8,128)(2,1)} %queries.1) | copy-start | bytes 1572868
  9.8 22.3 %copy-start.1 = (bf16[256,1024]{1,0:T(8,128)(2,1)S(1)}, bf16[256,1024]{1,0:T(8,128)(2,1)}, u32[]{:S(2)}) copy-start(bf16[256,1024]{1,0:T(8,128)(2,1)} %values.5) | copy-start | bytes 1572868
  28.4 4.8 %collective-permute-start.4 = (f32[65,128]{1,0:T(8,128)S(1)}, f32[65,128]{1,0:T(8,128)S(1)}, u32[]{:S(2)}, u32[]{:S(2)}) collective-permute-start(f32[65,128]{1,0:T(8,128)S(1)} %row_total.2), channel_id=1, source_target_pairs={{0,192},{64,0},{128,64},{192,128},{1,193},{65,1},{129,65},{193,129... | collective-permute-start | bytes 99848 | tf_op jit(solution)/shard_map/ppermute | solution.py:332
  31.0 4.3 %collective-permute-start.3 = (f32[65,128]{1,0:T(8,128)S(1)}, f32[65,128]{1,0:T(8,128)S(1)}, u32[]{:S(2)}, u32[]{:S(2)}) collective-permute-start(f32[65,128]{1,0:T(8,128)S(1)} %row_total.2), channel_id=1, source_target_pairs={{0,128},{64,192},{128,0},{192,64},{1,129},{65,193},{129,1},{193,65... | collective-permute-start | bytes 99848 | tf_op jit(solution)/shard_map/ppermute | solution.py:332
  31.5 4.2 %collective-permute-start.2 = (f32[65,128]{1,0:T(8,128)S(1)}, f32[65,128]{1,0:T(8,128)S(1)}, u32[]{:S(2)}, u32[]{:S(2)}) collective-permute-start(f32[65,128]{1,0:T(8,128)S(1)} %row_total.2), channel_id=1, source_target_pairs={{0,64},{64,128},{128,192},{192,0},{1,65},{65,129},{129,193},{193,1... | collective-permute-start | bytes 99848 | tf_op jit(solution)/shard_map/ppermute | solution.py:332
  35.7 17.5 %copy-start.5 = (bf16[256,1024]{1,0:T(8,128)(2,1)S(1)}, bf16[256,1024]{1,0:T(8,128)(2,1)}, u32[]{:S(2)}) copy-start(bf16[256,1024]{1,0:T(8,128)(2,1)} %out_grad.3) | copy-start | bytes 1572868
  35.7 17.4 %copy-start.6 = (f32[1024]{0:T(1024)S(1)}, f32[1024]{0:T(1024)}, u32[]{:S(2)}) copy-start(f32[1024]{0:T(1024)} %param.8) | copy-start | bytes 12292
  47.9 5.2 %collective-permute-start.5 = (f32[8,65,128]{2,1,0:T(8,128)S(1)}, f32[8,65,128]{2,1,0:T(8,128)S(1)}, u32[]{:S(2)}, u32[]{:S(2)}) collective-permute-start(f32[8,65,128]{2,1,0:T(8,128)S(1)} %all_to_all.21.kept), channel_id=1, source_target_pairs={{0,4},{4,0},{1,5},{5,1},{2,6},{6,2},{3,7},{7,3},{8,12},{12,8},{9,1... | collective-permute-start | bytes 798728 | tf_op jit(solution)/shard_map/ppermute | solution.py:327
  54.4 4.4 %collective-permute-start.8 = (f32[8,256]{1,0:T(8,128)S(1)}, f32[8,256]{1,0:T(8,128)S(1)}, u32[]{:S(2)}, u32[]{:S(2)}) collective-permute-start(f32[8,256]{1,0:T(8,128)S(1)} %get-tuple-element.87.stats), channel_id=1, source_target_pairs={{0,3},{1,0},{2,1},{3,2},{4,7},{5,4},{6,5},{7,6},{8,11},{9,8},{10,9... | collective-permute-start | bytes 24584 | tf_op jit(solution)/shard_map/ppermute | solution.py:332
  57.1 3.7 %collective-permute-start.7 = (f32[8,256]{1,0:T(8,128)S(1)}, f32[8,256]{1,0:T(8,128)S(1)}, u32[]{:S(2)}, u32[]{:S(2)}) collective-permute-start(f32[8,256]{1,0:T(8,128)S(1)} %get-tuple-element.87.stats), channel_id=1, source_target_pairs={{0,1},{1,2},{2,3},{3,0},{4,5},{5,6},{6,7},{7,4},{8,9},{9,10},{10,1... | collective-permute-start | bytes 24584 | tf_op jit(solution)/shard_map/ppermute | solution.py:332
  57.1 4.0 %collective-permute-start.6 = (f32[8,256]{1,0:T(8,128)S(1)}, f32[8,256]{1,0:T(8,128)S(1)}, u32[]{:S(2)}, u32[]{:S(2)}) collective-permute-start(f32[8,256]{1,0:T(8,128)S(1)} %get-tuple-element.87.stats), channel_id=1, source_target_pairs={{0,2},{1,3},{2,0},{3,1},{4,6},{5,7},{6,4},{7,5},{8,10},{9,11},{10,... | collective-permute-start | bytes 24584 | tf_op jit(solution)/shard_map/ppermute | solution.py:332
  62.8 3.1 %collective-permute-start.9 = (f32[8,65,128]{2,1,0:T(8,128)S(1)}, f32[8,65,128]{2,1,0:T(8,128)S(1)}, u32[]{:S(2)}, u32[]{:S(2)}) collective-permute-start(f32[8,65,128]{2,1,0:T(8,128)S(1)} %get-tuple-element.88), channel_id=1, source_target_pairs={{0,4},{4,0},{1,5},{5,1},{2,6},{6,2},{3,7},{7,3},{8,12},{12,8},{9,1... | collective-permute-start | bytes 798728 | tf_op jit(solution)/shard_map/ppermute | solution.py:327
  64.7 1.6 %collective-permute-start.10 = (f32[8,65,128]{2,1,0:T(8,128)S(1)}, f32[8,65,128]{2,1,0:T(8,128)S(1)}, u32[]{:S(2)}, u32[]{:S(2)}) collective-permute-start(f32[8,65,128]{2,1,0:T(8,128)S(1)} %get-tuple-element.90), channel_id=1, source_target_pairs={{0,4},{4,0},{1,5},{5,1},{2,6},{6,2},{3,7},{7,3},{8,12},{12,8},{9,1... | collective-permute-start | bytes 798728 | tf_op jit(solution)/shard_map/ppermute | solution.py:327
  81.6 6.9 %collective-permute-start.13 = (f32[65,128]{1,0:T(8,128)S(1)}, f32[65,128]{1,0:T(8,128)S(1)}, u32[]{:S(2)}, u32[]{:S(2)}) collective-permute-start(f32[65,128]{1,0:T(8,128)S(1)} %row_total.3), channel_id=1, source_target_pairs={{0,64},{64,128},{128,192},{192,0},{1,65},{65,129},{129,193},{193,1... | collective-permute-start | bytes 99848 | tf_op jit(solution)/shard_map/ppermute | solution.py:332
  81.7 6.9 %collective-permute-start.12 = (f32[65,128]{1,0:T(8,128)S(1)}, f32[65,128]{1,0:T(8,128)S(1)}, u32[]{:S(2)}, u32[]{:S(2)}) collective-permute-start(f32[65,128]{1,0:T(8,128)S(1)} %row_total.3), channel_id=1, source_target_pairs={{0,128},{64,192},{128,0},{192,64},{1,129},{65,193},{129,1},{193,65... | collective-permute-start | bytes 99848 | tf_op jit(solution)/shard_map/ppermute | solution.py:332
  83.0 5.5 %collective-permute-start.11 = (f32[65,128]{1,0:T(8,128)S(1)}, f32[65,128]{1,0:T(8,128)S(1)}, u32[]{:S(2)}, u32[]{:S(2)}) collective-permute-start(f32[65,128]{1,0:T(8,128)S(1)} %row_total.3), channel_id=1, source_target_pairs={{0,192},{64,0},{128,64},{192,128},{1,193},{65,1},{129,65},{193,129... | collective-permute-start | bytes 99848 | tf_op jit(solution)/shard_map/ppermute | solution.py:332
  101.4 4.4 %collective-permute-start.14 = (f32[8,65,128]{2,1,0:T(8,128)S(1)}, f32[8,65,128]{2,1,0:T(8,128)S(1)}, u32[]{:S(2)}, u32[]{:S(2)}) collective-permute-start(f32[8,65,128]{2,1,0:T(8,128)S(1)} %all_to_all.23.kept), channel_id=1, source_target_pairs={{0,4},{4,0},{1,5},{5,1},{2,6},{6,2},{3,7},{7,3},{8,12},{12,8},{9,1... | collective-permute-start | bytes 798728 | tf_op jit(solution)/shard_map/ppermute | solution.py:327

commit v3 on v0

v3 whole, which is shorter than its diff:
```python
import functools

import jax
import jax.numpy as jnp
from jax import lax
from jax.experimental import pallas as pl
from jax.experimental.pallas import tpu as pltpu
from jax.sharding import Mesh
from jax.sharding import PartitionSpec as P

HEADS = 32
HEAD_DIM = 128
CORES = 2
TOP = 2
ROWS = 32
BLOCK = 256
BLOCKS = HEAD_DIM // ROWS

f32 = jnp.float32
bf16 = jnp.bfloat16


def feature(values):
    return jnp.where(values > 0, values + 1.0, jnp.exp(jnp.minimum(values, 0.0)))


def feature_slope(values):
    return jnp.where(values > 0, jnp.ones_like(values), jnp.exp(jnp.minimum(values, 0.0)))


def dot(left, right, left_dim, right_dim):
    return lax.dot_general(
        left,
        right,
        (((left_dim,), (right_dim,)), ((), ())),
        preferred_element_type=f32,
    )


def split(values):
    high = values.astype(bf16)
    return high, (values - high.astype(f32)).astype(bf16)


def side_of(core, own):
    return core[0] if own else 1 - core[0]


def parts_of(values, axis):
    high, rest = split(values)
    middle = values - high.astype(f32)
    low = (middle - rest.astype(f32)).astype(bf16)
    return jnp.concatenate([high, rest, low], axis=axis)


def head_columns(side, place, heads_side):
    return pl.ds(pl.multiple_of((side * heads_side + place) * HEAD_DIM, HEAD_DIM), HEAD_DIM)


def columns(place, size=HEAD_DIM):
    return pl.ds(place * size, size)


def put_state(wire, place, state, row):
    first = place * BLOCKS
    wire[first : first + BLOCKS, 0:ROWS, :] = state.reshape(BLOCKS, ROWS, HEAD_DIM)
    wire[first : first + 1, ROWS : ROWS + 1, :] = row.reshape(1, 1, HEAD_DIM)


def clear_rows(wire):
    wire[:, ROWS : ROWS + 1, :] = jnp.zeros((wire.shape[0], 1, HEAD_DIM), f32)


def get_state(wire, extra, adds, place):
    first = place * BLOCKS
    blocks = pl.ds(first, BLOCKS)
    state = wire[blocks, 0:ROWS, :] + jnp.where(adds, extra[blocks, 0:ROWS, :], 0.0)
    row = wire[first, ROWS : ROWS + 1, :] + jnp.where(adds, extra[first, ROWS : ROWS + 1, :], 0.0)
    return state.reshape(HEAD_DIM, HEAD_DIM), row


def send_out(slots, target, slot, here, sem):
    copy = pltpu.make_async_copy(slots.at[slot], target.at[:, here], sem)
    copy.start()
    return copy


def causal(tokens):
    rows = lax.broadcasted_iota(jnp.int32, (tokens, tokens), 0)
    cols = lax.broadcasted_iota(jnp.int32, (tokens, tokens), 1)
    return rows >= cols


def key_features_kernel(core, keys, key_own, key_other):
    heads_side = keys.shape[1] // HEAD_DIM // CORES
    for target, own in ((key_other, False), (key_own, True)):
        for place in range(heads_side):
            here = head_columns(side_of(core, own), place, heads_side)
            target[:, columns(place)] = feature(keys[:, here].astype(f32)).astype(bf16)


def states_kernel(own, core, key_feat, values, wire):
    heads_side = key_feat.shape[1] // HEAD_DIM
    clear_rows(wire)
    for place in range(heads_side):
        here = head_columns(side_of(core, own), place, heads_side)
        key = key_feat[:, columns(place)]
        row = jnp.sum(key.astype(f32), axis=0, keepdims=True)
        put_state(wire, place, dot(values[:, here], key, 0, 0), row)


def inside_forward_kernel(own, core, queries, values, key_feat, query_out, low_out, numer, denom):
    tokens = queries.shape[0]
    heads_side = key_feat.shape[1] // HEAD_DIM
    mask = causal(tokens)
    for place in range(heads_side):
        here = head_columns(side_of(core, own), place, heads_side)
        there = columns(place)
        query_feat = feature(queries[:, here].astype(f32)).astype(bf16)
        query_out[:, there] = query_feat
        scores = jnp.where(mask, dot(query_feat, key_feat[:, there], 1, 1), 0.0)
        scores_low = scores.astype(bf16)
        low_out[:, columns(place, tokens)] = scores_low
        numer[:, there] = dot(scores_low, values[:, here], 1, 0)
        total = jnp.sum(scores, axis=1, keepdims=True)
        denom[:, there] = jnp.broadcast_to(total, (tokens, HEAD_DIM))


def attention_kernel(own, core, query_feat, numer_in, denom_in, wire, extra, gain, out_grad, *rest):
    tokens, width = query_feat.shape
    heads_side = width // HEAD_DIM
    adds = core[0] == 1
    if own:
        attn_out, inverse_out, squares_out, cross_out = rest
        squares = jnp.zeros((tokens, HEAD_DIM), f32)
        cross = jnp.zeros((tokens, HEAD_DIM), f32)
    else:
        squares_in, cross_in, attn_out, inverse_out, stats = rest
        squares = squares_in[...]
        cross = cross_in[...]
    for place in range(heads_side):
        here = head_columns(side_of(core, own), place, heads_side)
        there = columns(place)
        state, row = get_state(wire, extra, adds, place)
        both = jnp.concatenate([state, jnp.broadcast_to(row, state.shape)], axis=0)
        right = jnp.concatenate(split(both), axis=1)
        query = query_feat[:, there]
        product = dot(jnp.concatenate([query, query], axis=1), right, 1, 1)
        numer = numer_in[:, there] + product[:, :HEAD_DIM]
        inverse = 1.0 / (denom_in[:, there] + product[:, HEAD_DIM:])
        attn = numer * inverse
        grad_in = gain[:, here] * out_grad[:, here].astype(f32)
        squares = squares + attn * attn
        cross = cross + attn * grad_in
        attn_out[:, there] = attn
        inverse_out[:, there] = inverse
    if own:
        squares_out[...] = squares
        cross_out[...] = cross
    else:
        ones = jnp.ones((8, 3 * HEAD_DIM), bf16)
        which = lax.broadcasted_iota(jnp.int32, (8, tokens), 0)
        row_squares = dot(ones, parts_of(squares, 1), 1, 1)
        row_cross = dot(ones, parts_of(cross, 1), 1, 1)
        stats[...] = jnp.where(which == 0, row_squares, jnp.where(which == 1, row_cross, 0.0))


def token_scales(stats, width_all):
    tokens = stats.shape[1]
    squares = stats[0:1, :]
    cross = stats[1:2, :]
    scale = lax.rsqrt(squares / width_all + 1e-06)
    slope = scale * scale * scale * (cross / width_all)
    which = lax.broadcasted_iota(jnp.int32, (8, tokens), 0)
    rows = jnp.where(which == 0, scale, jnp.where(which == 1, slope, 0.0))
    pick = lax.broadcasted_iota(jnp.int32, (24, 2 * HEAD_DIM), 0) % 8 == (
        lax.broadcasted_iota(jnp.int32, (24, 2 * HEAD_DIM), 1) // HEAD_DIM
    )
    spread = dot(parts_of(rows, 0), pick.astype(f32).astype(bf16), 0, 0)
    return spread[:, :HEAD_DIM], spread[:, HEAD_DIM:]


def gradient_kernel(own, core, query_feat, attn_in, inverse_in, gain, out_grad, *rest):
    width = query_feat.shape[1]
    heads_side = width // HEAD_DIM
    if own:
        scale_in, slope_in, numer_out, denom_out, wire = rest
        scale = scale_in[...]
        slope = slope_in[...]
    else:
        parts, (numer_out, denom_out, wire, scale_out, slope_out) = rest[:-5], rest[-5:]
        total = (parts[0][...] + parts[1][...]) + (parts[2][...] + parts[3][...])
        scale, slope = token_scales(total, HEADS * HEAD_DIM)
        scale_out[...] = scale
        slope_out[...] = slope
    clear_rows(wire)
    for place in range(heads_side):
        here = head_columns(side_of(core, own), place, heads_side)
        there = columns(place)
        attn = attn_in[:, there]
        inverse = inverse_in[:, there]
        grad_in = gain[:, here] * out_grad[:, here].astype(f32)
        d_attn = scale * grad_in - attn * slope
        d_numer = d_attn * inverse
        total = jnp.sum(d_attn * attn, axis=1, keepdims=True)
        d_denom = -total * inverse
        numer_out[:, there] = d_numer
        denom_out[:, there] = d_denom
        query = query_feat[:, there]
        row = jnp.sum(d_denom * query.astype(f32), axis=0, keepdims=True)
        put_state(wire, place, dot(d_numer.astype(bf16), query, 0, 0), row)


def early_backward_kernel(core, gain, scale_in, *refs):
    halves, normed, parts = (refs[:3], refs[3:6]), refs[6], refs[7:9]
    normed_slots, _, sems = refs[9:]
    tokens, width_side = refs[0].shape
    heads_side = width_side // HEAD_DIM
    scale = scale_in[...]
    copies = []
    for half, own in enumerate((True, False)):
        attn, low, d_numer_in = halves[half]
        for place in range(heads_side):
            here = head_columns(side_of(core, own), place, heads_side)
            there = columns(place)
            slot = half * heads_side + place
            normed_slots[slot] = (gain[:, here] * attn[:, there] * scale).astype(bf16)
            copies.append(send_out(normed_slots, normed, slot, here, sems.at[0, slot]))
    for half in range(CORES):
        attn, low, d_numer_in = halves[half]
        for place in range(heads_side):
            there = columns(place)
            numer_low = d_numer_in[:, there].astype(bf16)
            parts[half][:, there] = dot(low[:, columns(place, tokens)], numer_low, 0, 0)
    for copy in copies:
        copy.wait()


def inside_backward_kernel(core, queries, values, *refs):
    halves, refs = (refs[:6], refs[6:12]), refs[12:]
    query_grad, parts, (query_slots, _, sems) = refs[0], refs[1:3], refs[3:]
    tokens, width = queries.shape
    heads_side = width // HEAD_DIM // CORES
    adds = core[0] == 1
    mask = causal(tokens)
    copies = []
    for half, own in enumerate((True, False)):
        query_feat, key_feat, d_numer_in, d_denom_in, wire, extra = halves[half]
        for place in range(heads_side):
            here = head_columns(side_of(core, own), place, heads_side)
            there = columns(place)
            slot = half * heads_side + place
            state, row = get_state(wire, extra, adds, place)
            state_high, state_low = split(state)
            d_denom = d_denom_in[:, there]
            numer_low, numer_rest = split(d_numer_in[:, there])
            key = key_feat[:, there]
            mixed = dot(numer_low, values[:, here], 1, 1)
            mixed = mixed + jnp.concatenate([d_denom, d_denom], axis=1)
            mixed_low = jnp.where(mask, mixed, 0.0).astype(bf16)
            left = jnp.concatenate([numer_low, numer_low, numer_rest], axis=1)
            right = jnp.concatenate([state_high, state_low, state_high], axis=0)
            grad = dot(left, right, 1, 0) + d_denom * row + dot(mixed_low, key, 1, 0)
            query_raw = queries[:, here].astype(f32)
            query_slots[slot] = (grad * feature_slope(query_raw)).astype(bf16)
            copies.append(send_out(query_slots, query_grad, slot, here, sems.at[0, slot]))
            parts[half][:, there] = dot(mixed_low, query_feat[:, there], 0, 0)
    for copy in copies:
        copy.wait()


def outside_backward_kernel(own, core, keys, values, key_feat, key_part, value_part, wire, extra, *rest):
    key_grad, value_grad, key_slots, value_slots, sems = rest[-5:]
    heads_side = key_feat.shape[1] // HEAD_DIM
    adds = core[0] == 0
    copies = []
    for place in range(heads_side):
        here = head_columns(side_of(core, own), place, heads_side)
        there = columns(place)
        state, row = get_state(wire, extra, adds, place)
        high, low = split(state)
        value = values[:, here]
        key = key_feat[:, there]
        grad = dot(
            jnp.concatenate([value, value], axis=1), jnp.concatenate([high, low], axis=0), 1, 0
        )
        grad = grad + row + key_part[:, there]
        key_raw = keys[:, here].astype(f32)
        key_slots[place] = (grad * feature_slope(key_raw)).astype(bf16)
        copies.append(send_out(key_slots, key_grad, place, here, sems.at[0, place]))
        grad = dot(
            jnp.concatenate([key, key], axis=1), jnp.concatenate([high, low], axis=1), 1, 1
        )
        value_slots[place] = (grad + value_part[:, there]).astype(bf16)
        copies.append(send_out(value_slots, value_grad, place, here, sems.at[1, place]))
    for copy in copies:
        copy.wait()


def group_total_kernel(spread, total):
    value = spread[0]
    for chip in range(1, spread.shape[0]):
        value = value + spread[chip]
    total[...] = value


def chip_sums_kernel(backward, top, spread, other, sums):
    chips = spread.shape[0]
    inside = top[0] == (0 if backward else TOP - 1)
    total = jnp.where(inside, other[...], 0.0)
    for step in range(chips):
        chip = chips - 1 - step if backward else step
        sums[chip] = total
        if step < chips - 1:
            total = total + spread[chip]


def shaped(shape, dtype):
    return jax.ShapeDtypeStruct(shape, dtype)


def call(
    kernel, name, out_shape, *operands, core=None, flops=0, hbm_in=(), hbm_out=(), slots=0,
    vmem=16, aliases=None,
):
    moved = sum(x.size * x.dtype.itemsize for x in operands)
    moved += sum(x.size * x.dtype.itemsize for x in jax.tree.leaves(out_shape))

    def spaces(count, hbm):
        kinds = [pltpu.HBM if place in hbm else pltpu.VMEM for place in range(count)]
        return [pl.BlockSpec(memory_space=kind) for kind in kinds]

    in_specs = spaces(len(operands), hbm_in)
    out_specs = spaces(len(jax.tree.leaves(out_shape)), hbm_out)
    scratch = []
    if slots:
        scratch = [pltpu.VMEM((slots, BLOCK, HEAD_DIM), bf16)] * 2
        scratch.append(pltpu.SemaphoreType.DMA((2, slots)))
    if core is not None:
        in_specs = [pl.BlockSpec(memory_space=pltpu.SMEM)] + in_specs
        operands = (core,) + operands
    return pl.pallas_call(
        kernel,
        out_shape=out_shape,
        in_specs=in_specs,
        out_specs=tuple(out_specs) if isinstance(out_shape, tuple) else out_specs[0],
        scratch_shapes=scratch,
        input_output_aliases=aliases or {},
        compiler_params=pltpu.CompilerParams(vmem_limit_bytes=vmem << 20),
        cost_estimate=pl.CostEstimate(flops=flops, bytes_accessed=moved, transcendentals=0),
        name=name,
    )(*operands)


def swap(array, axis):
    return lax.ppermute(array, axis, [(0, 1), (1, 0)])


def shifted(array, axis, step):
    size = lax.axis_size(axis)
    return lax.ppermute(array, axis, [(i, (i + step) % size) for i in range(size)])


def after(first, *later):
    return lax.optimization_barrier((first, later))


def scan_chips(pair, top, backward, inside=None, operands=()):
    spread = lax.all_to_all(pair, "chip", 0, 0)
    total = call(group_total_kernel, "group_total", shaped(spread.shape[1:], f32), spread)
    done = ()
    if inside is None:
        other = swap(total, "top")
    else:
        total, operands = after(total, *operands)
        other = swap(total, "top")
        done = inside(*operands)
    other, spread, done = lax.optimization_barrier((other, spread, done))
    kernel = functools.partial(chip_sums_kernel, backward)
    sums = call(kernel, "chip_sums", shaped(spread.shape, f32), spread, other, core=top)
    return lax.all_to_all(sums, "chip", 0, 0), done


def body(queries, key_rows, value_rows, norm_gain, out_grad):
    tokens, width = queries.shape
    heads = width // HEAD_DIM
    heads_side = heads // CORES
    core = lax.axis_index("core").astype(jnp.int32).reshape(1)
    top = lax.axis_index("top").astype(jnp.int32).reshape(1)
    core, top = lax.optimization_barrier((core, top))
    gain = norm_gain.reshape(1, width)
    wire = shaped((lax.axis_size("chip"), ROWS + 1, HEAD_DIM), f32)
    narrow = shaped((tokens, width), bf16)
    half_low = shaped((tokens, width // CORES), bf16)
    half = shaped((tokens, width // CORES), f32)
    square = shaped((tokens, heads_side * tokens), bf16)
    lanes = shaped((tokens, HEAD_DIM), f32)
    stats_shape = shaped((8, tokens), f32)
    unit = tokens * HEAD_DIM * HEAD_DIM * heads

    def side_call(kernel, name, own, *args, **named):
        kernel = functools.partial(kernel, own)
        return call(kernel, name + ("_own" if own else "_other"), *args, core=core, **named)

    key_own, key_other = call(
        key_features_kernel, "key_features", (half_low, half_low), key_rows, core=core
    )
    theirs = side_call(states_kernel, "states", False, wire, key_other, value_rows, flops=unit)
    theirs, (key_own,) = after(theirs, key_own)
    extra = swap(theirs, "core")
    mine = side_call(states_kernel, "states", True, wire, key_own, value_rows, flops=unit)
    mine, (key_own, queries_in) = after(mine, key_own, queries)
    extra_got = swap(mine, "core")
    halves = (half_low, square, half, half)
    inside = side_call(
        inside_forward_kernel, "inside_forward", True, halves, queries_in, value_rows, key_own,
        flops=4 * unit,
    )
    extra, extra_got, mine, inside = lax.optimization_barrier((extra, extra_got, mine, inside))
    query_own, low_own, numer, denom = inside
    kept, _ = scan_chips(mine + extra, top, False)
    kept, (queries_in, key_other) = after(kept, queries, key_other)
    got = swap(kept, "core")
    query_other, low_other, numer_other, denom_other = side_call(
        inside_forward_kernel, "inside_forward", False, halves, queries_in, value_rows, key_other,
        flops=4 * unit,
    )
    attn_own, inverse_own, squares, cross = side_call(
        attention_kernel, "attention", True, (half, half, lanes, lanes),
        query_own, numer, denom, kept, extra, gain, out_grad, flops=4 * unit,
    )
    attn_other, inverse_other, stats = side_call(
        attention_kernel, "attention", False, (half, half, stats_shape),
        query_other, numer_other, denom_other, got, extra_got, gain, out_grad, squares, cross,
        flops=4 * unit,
    )
    prefix_own = (kept, extra)
    prefix_other = (got, extra_got)
    stats_from = [shifted(stats, "head", step) for step in (2, 1, 3)]
    d_numer_other, d_denom_other, theirs, scale, slope = side_call(
        gradient_kernel, "gradient", False, (half, half, wire, lanes, lanes),
        query_other, attn_other, inverse_other, gain, out_grad, stats, *stats_from, flops=unit,
    )
    theirs, (scale, slope) = after(theirs, scale, slope)
    extra = swap(theirs, "core")
    d_numer_own, d_denom_own, mine = side_call(
        gradient_kernel, "gradient", True, (half, half, wire),
        query_own, attn_own, inverse_own, gain, out_grad, scale, slope, flops=unit,
    )

    mine, (scale,) = after(mine, scale)
    extra_got = swap(mine, "core")
    normed, value_part, value_part_other = call(
        early_backward_kernel, "early_backward", (narrow, half, half), gain, scale,
        attn_own, low_own, d_numer_own, attn_other, low_other, d_numer_other,
        core=core, flops=4 * unit, hbm_out=(0,), slots=heads,
    )
    extra, extra_got, mine, normed, value_part, value_part_other = lax.optimization_barrier(
        (extra, extra_got, mine, normed, value_part, value_part_other)
    )

    def inside_backward(*operands):
        return call(
            inside_backward_kernel, "inside_backward", (narrow, half, half),
            *operands, core=core, flops=18 * unit, hbm_out=(0,), slots=heads,
        )

    operands = (queries, value_rows)
    operands += (query_own, key_own, d_numer_own, d_denom_own) + prefix_own
    operands += (query_other, key_other, d_numer_other, d_denom_other) + prefix_other
    kept, inside = scan_chips(mine + extra, top, True, inside_backward, operands)
    query_grad, key_part, key_part_other = inside
    got = swap(kept, "core")
    last = dict(flops=4 * unit, hbm_out=(0, 1), slots=heads_side)
    key_grad, value_grad = side_call(
        outside_backward_kernel, "outside_backward", True, (narrow, narrow),
        key_rows, value_rows, key_own, key_part, value_part, kept, extra, **last,
    )
    key_grad, value_grad = side_call(
        outside_backward_kernel, "outside_backward", False, (narrow, narrow),
        key_rows, value_rows, key_other, key_part_other, value_part_other, got, extra_got,
        key_grad, value_grad, hbm_in=(7, 8), aliases={8: 0, 9: 1}, **last,
    )
    return (normed, query_grad, key_grad, value_grad)


def solution(mesh):
    devices = mesh.devices
    fine = Mesh(
        devices.reshape(TOP, devices.shape[0] // (TOP * CORES), CORES, devices.shape[1]),
        ("top", "chip", "core", "head"),
    )
    rows = P(("top", "chip", "core"), "head")
    return jax.shard_map(
        body,
        mesh=fine,
        in_specs=(rows, rows, rows, P("head"), rows),
        out_specs=(rows, rows, rows, rows),
        check_vma=False,
    )
```

time: 138 us -> 101 us (0.73)
  blocking collectives: 29.7 us -> 59.2 us
  local copies, waits for them, and re-layouts: 22.2 us -> 1.12 us
  waiting for transfers between devices: 22.2 us -> 5.45 us
  matrix products: 12.9 us -> 0 us
  starting transfers between devices: 34.2 us -> 22.8 us
  other arithmetic: 10.8 us -> 0.07 us
  Pallas kernels: 3.61 us -> 10.7 us
    all_to_all x1 -> x4, blocking collectives: 21 us -> 59.2 us  [the longest x2 31.8 us: scan_chips(): spread = lax.all_to_all(pair, 'chip', 0, 0)]
    all_to_all x3 -> x0, starting transfers between devices: 20 us -> none  [the longest x2 15.1 us: scan_states(): kept = lax.all_to_all(chip_sums(spread, backward), 'chip', 0, 0)]
    all_to_all x3 -> x0, waiting for transfers between devices: 19.7 us -> none  [the longest x2 13.5 us: scan_states(): kept = lax.all_to_all(chip_sums(spread, backward), 'chip', 0, 0)]
    unnamed x60 -> x12, local copies, waits for them, and re-layouts: 14.4 us -> 1.12 us
    dot_general x14 -> x0, matrix products: 12.9 us -> none  [the longest x1 1.7 us: body(): jnp.einsum('hts,htf->hsf', scores_low, numer_low, preferred_element_type=...]
    psum x1 -> x0, blocking collectives: 8.7 us -> none  [body(): lax.psum((jnp.sum(attn * attn, axis=(0, 2)), jnp.sum(attn * grad_in, axis...]
    ppermute x4 -> x11, starting transfers between devices: 14.2 us -> 22.8 us  [the longest x8 18.3 us: swap(): return lax.ppermute(array, axis, [(0, 1), (1, 0)])]
    pallas_call x2 -> x17, Pallas kernels: 3.61 us -> 10.7 us  [call(): pl.pallas_call(kernel, out_shape=out_shape, in_specs=in_specs, out_specs=...]
  transfers between devices with their start and end apart: 7 -> 11, of which waited for: 6 -> 8; matrix products, arithmetic and copies ran while one was open for 15% -> 0% of each run, Pallas kernels for 0% -> 7%
where the time goes in v3:
time: 101 us; the launch traced here: 100 us
  blocking collectives  59.2 us (59%)
  starting transfers between devices  22.8 us (23%)
  Pallas kernels  10.7 us (11%)
  waiting for transfers between devices  5.45 us (5%)
  local copies, waits for them, and re-layouts  1.12 us (1%)
    all_to_all x2, blocking collectives, scan_chips(): spread = lax.all_to_all(pair, 'chip', 0, 0)  31.8 us
    all_to_all x2, blocking collectives, scan_chips(): return (lax.all_to_all(sums, 'chip', 0, 0), done)  27.4 us
    ppermute x8, starting transfers between devices, swap(): return lax.ppermute(array, axis, [(0, 1), (1, 0)])  18.3 us
    pallas_call x17, Pallas kernels, call(): pl.pallas_call(kernel, out_shape=out_shape, in_specs=in_specs, out_specs=...  10.7 us
    ppermute x3, starting transfers between devices, shifted(): lax.ppermute(array, axis, [(i, (i + step) % size) for i in range(size)])  4.41 us
    ppermute x8, waiting for transfers between devices, swap(): return lax.ppermute(array, axis, [(0, 1), (1, 0)])  3.09 us
    ppermute x3, waiting for transfers between devices, shifted(): lax.ppermute(array, axis, [(i, (i + step) % size) for i in range(size)])  2.36 us
  transfers between devices with their start and end apart: 11, of which 8 were waited for; matrix products, arithmetic and copies ran while one was open for 0% of the time, Pallas kernels for 7%

profile of v3, /device:TPU:1, one launch (start us, length us, event | category | flops | bytes accessed | tf_op | source)
XLA Modules:
  0.0 100.3 jit_solution(9543990226239503665)
XLA Ops:
  0.6 0.0 copy-start
  0.6 0.0 copy-start.2
  0.7 1.1 %copy-done.2 = bf16[256,1024]{1,0:T(8,128)(2,1)S(1)} copy-done((bf16[256,1024]{1,0:T(8,128)(2,1)S(1)}, bf16[256,1024]{1,0:T(8,128)(2,1)}, u32[]{:S(2)}) %copy-start.2) | copy-done | bytes 524312
  1.7 0.3 key_features.1
  2.0 0.0 copy-done
  2.0 0.3 states_other.1
  2.3 0.0 copy-start.4
  2.3 0.3 states_own.1
  2.6 3.3 %collective-permute-start.1 = (f32[16,33,128]{2,1,0:T(8,128)S(1)}, f32[16,33,128]{2,1,0:T(8,128)S(1)}, u32[]{:S(2)}, u32[]{:S(2)}) collective-permute-start(f32[16,33,128]{2,1,0:T(8,128)S(1)} %states_own.1), channel_id=1, source_target_pairs={{0,4},{4,0},{1,5},{5,1},{2,6},{6,2},{3,7},{7,3},{8,12},{12,8},{9,1... | collective-permute-start | bytes 811016 | tf_op jit(solution)/shard_map/ppermute | solution.py:356
  6.0 0.1 collective-permute-start
  6.1 0.0 copy-done.4
  6.1 0.7 inside_forward_own.1
  6.7 0.5 collective-permute-done.1.extra.refs_11_
  7.2 0.5 collective-permute-done.extra.refs_5_
  7.7 17.5 %all_to_all.20.spread = f32[16,33,128]{2,1,0:T(8,128)S(1)} all-to-all(f32[16,33,128]{2,1,0:T(8,128)S(1)} %add.6), channel_id=1, replica_groups=mesh['top'=2,'chip'=16,'core'=2,'head'=4] {'chip'}, dimensions={0} | all-to-all | bytes 540672 | tf_op jit(solution)/shard_map/all_to_all | solution.py:369
  25.2 2.5 %collective-permute-start.2 = (f32[33,128]{1,0:T(8,128)S(1)}, f32[33,128]{1,0:T(8,128)S(1)}, u32[]{:S(2)}, u32[]{:S(2)}) collective-permute-start(f32[33,128]{1,0:T(8,128)S(1)} %group_total.2), channel_id=1, source_target_pairs={{0,128},{128,0},{1,129},{129,1},{2,130},{130,2},{3,131},{131,3},{4... | collective-permute-start | bytes 50696 | tf_op jit(solution)/shard_map/ppermute | solution.py:356
  27.8 1.7 %collective-permute-done.2.other = f32[33,128]{1,0:T(8,128)S(1)} collective-permute-done((f32[33,128]{1,0:T(8,128)S(1)}, f32[33,128]{1,0:T(8,128)S(1)}, u32[]{:S(2)}, u32[]{:S(2)}) %collective-permute-start.2) | collective-permute-done | bytes 16928 | tf_op jit(solution)/shard_map/ppermute | solution.py:356
  29.5 13.6 %all_to_all.21.wire.refs_4_ = f32[16,33,128]{2,1,0:T(8,128)S(1)} all-to-all(f32[16,33,128]{2,1,0:T(8,128)S(1)} %chip_sums.2), channel_id=1, replica_groups=mesh['top'=2,'chip'=16,'core'=2,'head'=4] {'chip'}, dimensions={0} | all-to-all | bytes 540672 | tf_op jit(solution)/shard_map/all_to_all | solution.py:381
  43.1 4.3 %collective-permute-start.3 = (f32[16,33,128]{2,1,0:T(8,128)S(1)}, f32[16,33,128]{2,1,0:T(8,128)S(1)}, u32[]{:S(2)}, u32[]{:S(2)}) collective-permute-start(f32[16,33,128]{2,1,0:T(8,128)S(1)} %all_to_all.21.wire.refs_4_), channel_id=1, source_target_pairs={{0,4},{4,0},{1,5},{5,1},{2,6},{6,2},{3,7},{7,3},{8,12},{12,8},{9,1... | collective-permute-start | bytes 811016 | tf_op jit(solution)/shard_map/ppermute | solution.py:356
  47.4 0.7 inside_forward_other.1
  48.1 0.0 copy-done.5
  48.1 0.4 attention_own.1
  48.5 0.2 collective-permute-done.3.wire.refs_10_
  48.6 0.6 attention_other.1
  49.2 2.8 %collective-permute-start.6 = (f32[8,256]{1,0:T(8,128)S(1)}, f32[8,256]{1,0:T(8,128)S(1)}, u32[]{:S(2)}, u32[]{:S(2)}) collective-permute-start(f32[8,256]{1,0:T(8,128)S(1)} %get-tuple-element.120.rest_0_), channel_id=1, source_target_pairs={{0,3},{1,0},{2,1},{3,2},{4,7},{5,4},{6,5},{7,6},{8,11},{9,8},{10,9... | collective-permute-start | bytes 24584 | tf_op jit(solution)/shard_map/ppermute | solution.py:361
  52.0 0.0 collective-permute-start.5
  52.0 1.6 %collective-permute-start.4 = (f32[8,256]{1,0:T(8,128)S(1)}, f32[8,256]{1,0:T(8,128)S(1)}, u32[]{:S(2)}, u32[]{:S(2)}) collective-permute-start(f32[8,256]{1,0:T(8,128)S(1)} %get-tuple-element.120.rest_0_), channel_id=1, source_target_pairs={{0,2},{1,3},{2,0},{3,1},{4,6},{5,7},{6,4},{7,5},{8,10},{9,11},{10,... | collective-permute-start | bytes 24584 | tf_op jit(solution)/shard_map/ppermute | solution.py:361
  53.6 0.0 collective-permute-done.6.rest_3_
  53.6 2.1 %collective-permute-done.5.rest_2_ = f32[8,256]{1,0:T(8,128)S(1)} collective-permute-done((f32[8,256]{1,0:T(8,128)S(1)}, f32[8,256]{1,0:T(8,128)S(1)}, u32[]{:S(2)}, u32[]{:S(2)}) %collective-permute-start.5) | collective-permute-done | bytes 8224 | tf_op jit(solution)/shard_map/ppermute | solution.py:361
  55.7 0.3 collective-permute-done.4.rest_1_
  56.0 0.7 gradient_other.1
  56.6 1.9 %collective-permute-start.7 = (f32[16,33,128]{2,1,0:T(8,128)S(1)}, f32[16,33,128]{2,1,0:T(8,128)S(1)}, u32[]{:S(2)}, u32[]{:S(2)}) collective-permute-start(f32[16,33,128]{2,1,0:T(8,128)S(1)} %get-tuple-element.124), channel_id=1, source_target_pairs={{0,4},{4,0},{1,5},{5,1},{2,6},{6,2},{3,7},{7,3},{8,12},{12,8},{9,1... | collective-permute-start | bytes 811016 | tf_op jit(solution)/shard_map/ppermute | solution.py:356
  58.5 0.4 gradient_own.1
  59.0 0.1 collective-permute-start.8
  59.1 1.4 %early_backward.1 = (bf16[256,1024]{1,0:T(8,128)(2,1)}, f32[256,512]{1,0:T(8,128)S(1)}, f32[256,512]{1,0:T(8,128)S(1)}) custom-call(s32[1]{0:T(128)} %bitcast.core, f32[1,1024]{1,0:T(1,128)S(1)} %bitcast.7, f32[256,128]{1,0:T(8,128)S(1)} %get-tuple-element.131.rest_0_.scale_in, f32[256,512]{1,0:T(8,128)S(1)} %get-tuple-element.125.attn_in.refs_0_, ...), custom_call_target="tpu_custom_call" | custom-call | flops 134217728 | bytes 4853760 | tf_op jit(solution)/shard_map/early_backward/pallas_call | solution.py:342
  60.5 0.0 collective-permute-done.7.extra
  60.5 0.2 collective-permute-done.8.extra
  60.7 14.3 %all_to_all.22.spread = f32[16,33,128]{2,1,0:T(8,128)S(1)} all-to-all(f32[16,33,128]{2,1,0:T(8,128)S(1)} %add.7), channel_id=1, replica_groups=mesh['top'=2,'chip'=16,'core'=2,'head'=4] {'chip'}, dimensions={0} | all-to-all | bytes 540672 | tf_op jit(solution)/shard_map/all_to_all | solution.py:369
  75.0 2.7 %collective-permute-start.9 = (f32[33,128]{1,0:T(8,128)S(1)}, f32[33,128]{1,0:T(8,128)S(1)}, u32[]{:S(2)}, u32[]{:S(2)}) collective-permute-start(f32[33,128]{1,0:T(8,128)S(1)} %group_total.3), channel_id=1, source_target_pairs={{0,128},{128,0},{1,129},{129,1},{2,130},{130,2},{3,131},{131,3},{4... | collective-permute-start | bytes 50696 | tf_op jit(solution)/shard_map/ppermute | solution.py:356
  77.8 2.7 %inside_backward.1 = (bf16[256,1024]{1,0:T(8,128)(2,1)}, f32[256,512]{1,0:T(8,128)S(1)}, f32[256,512]{1,0:T(8,128)S(1)}) custom-call(s32[1]{0:T(128)} %bitcast.core, bf16[256,1024]{1,0:T(8,128)(2,1)S(1)} %copy-done.4, bf16[256,1024]{1,0:T(8,128)(2,1)S(1)} %copy-done, bf16[256,512]{1,0:T(8,128)(2,1)S(1)} %get-tuple-element.147.query_feat.refs_0_, ...), custom_call_target="tpu_custom_call" | custom-call | flops 603979776 | bytes 6848512 | tf_op jit(solution)/shard_map/inside_backward/pallas_call | solution.py:342
  80.5 0.0 collective-permute-done.9.other
  80.5 0.0 copy-start.3
  80.5 13.8 %all_to_all.23.wire = f32[16,33,128]{2,1,0:T(8,128)S(1)} all-to-all(f32[16,33,128]{2,1,0:T(8,128)S(1)} %chip_sums.3), channel_id=1, replica_groups=mesh['top'=2,'chip'=16,'core'=2,'head'=4] {'chip'}, dimensions={0} | all-to-all | bytes 540672 | tf_op jit(solution)/shard_map/all_to_all | solution.py:381
  94.4 3.4 %collective-permute-start.10 = (f32[16,33,128]{2,1,0:T(8,128)S(1)}, f32[16,33,128]{2,1,0:T(8,128)S(1)}, u32[]{:S(2)}, u32[]{:S(2)}) collective-permute-start(f32[16,33,128]{2,1,0:T(8,128)S(1)} %all_to_all.23.wire), channel_id=1, source_target_pairs={{0,4},{4,0},{1,5},{5,1},{2,6},{6,2},{3,7},{7,3},{8,12},{12,8},{9,1... | collective-permute-start | bytes 811016 | tf_op jit(solution)/shard_map/ppermute | solution.py:356
  97.7 0.0 copy-done.3
  97.7 1.2 %outside_backward_own.1 = (bf16[256,1024]{1,0:T(8,128)(2,1)}, bf16[256,1024]{1,0:T(8,128)(2,1)}) custom-call(s32[1]{0:T(128)} %bitcast.core, bf16[256,1024]{1,0:T(8,128)(2,1)S(1)} %copy-done.3, bf16[256,1024]{1,0:T(8,128)(2,1)S(1)} %copy-done, bf16[256,512]{1,0:T(8,128)(2,1)S(1)} %get-tuple-element.148.key_feat.refs_1_, ...), custom_call_target="tpu_custom_call" | custom-call | flops 134217728 | bytes 3948544 | tf_op jit(solution)/shard_map/outside_backward_own/pallas_call | solution.py:342
  98.9 0.1 collective-permute-done.10.wire
  99.0 1.1 %outside_backward_other.1 = (bf16[256,1024]{1,0:T(8,128)(2,1)}, bf16[256,1024]{1,0:T(8,128)(2,1)}) custom-call(s32[1]{0:T(128)} %bitcast.core, bf16[256,1024]{1,0:T(8,128)(2,1)S(1)} %copy-done.3, bf16[256,1024]{1,0:T(8,128)(2,1)S(1)} %copy-done, ...), custom_call_target="tpu_custom_call", output_to_operand_aliasing={{0}: (8, {}), {1}: (9, {})} | custom-call | flops 134217728 | bytes 4997120 | tf_op jit(solution)/shard_map/outside_backward_other/pallas_call | solution.py:342
  (9 shorter events, 0.2 us)
Async XLA Ops:
  0.6 1.4 %copy-start = (bf16[256,1024]{1,0:T(8,128)(2,1)S(1)}, bf16[256,1024]{1,0:T(8,128)(2,1)}, u32[]{:S(2)}) copy-start(bf16[256,1024]{1,0:T(8,128)(2,1)} %values.12) | copy-start | bytes 1572868
  0.6 1.1 %copy-start.2 = (bf16[256,1024]{1,0:T(8,128)(2,1)S(1)}, bf16[256,1024]{1,0:T(8,128)(2,1)}, u32[]{:S(2)}) copy-start(bf16[256,1024]{1,0:T(8,128)(2,1)} %keys.5) | copy-start | bytes 1572868
  2.3 3.7 %copy-start.4 = (bf16[256,1024]{1,0:T(8,128)(2,1)S(1)}, bf16[256,1024]{1,0:T(8,128)(2,1)}, u32[]{:S(2)}) copy-start(bf16[256,1024]{1,0:T(8,128)(2,1)} %queries.2) | copy-start | bytes 1572868
  2.6 4.6 %collective-permute-start.1 = (f32[16,33,128]{2,1,0:T(8,128)S(1)}, f32[16,33,128]{2,1,0:T(8,128)S(1)}, u32[]{:S(2)}, u32[]{:S(2)}) collective-permute-start(f32[16,33,128]{2,1,0:T(8,128)S(1)} %states_own.1), channel_id=1, source_target_pairs={{0,4},{4,0},{1,5},{5,1},{2,6},{6,2},{3,7},{7,3},{8,12},{12,8},{9,1... | collective-permute-start | bytes 811016 | tf_op jit(solution)/shard_map/ppermute | solution.py:356
  6.0 1.7 %collective-permute-start = (f32[16,33,128]{2,1,0:T(8,128)S(1)}, f32[16,33,128]{2,1,0:T(8,128)S(1)}, u32[]{:S(2)}, u32[]{:S(2)}) collective-permute-start(f32[16,33,128]{2,1,0:T(8,128)S(1)} %states_other.1), channel_id=1, source_target_pairs={{0,4},{4,0},{1,5},{5,1},{2,6},{6,2},{3,7},{7,3},{8,12},{12,8},{9,1... | collective-permute-start | bytes 811016 | tf_op jit(solution)/shard_map/ppermute | solution.py:356
  25.2 4.2 %collective-permute-start.2 = (f32[33,128]{1,0:T(8,128)S(1)}, f32[33,128]{1,0:T(8,128)S(1)}, u32[]{:S(2)}, u32[]{:S(2)}) collective-permute-start(f32[33,128]{1,0:T(8,128)S(1)} %group_total.2), channel_id=1, source_target_pairs={{0,128},{128,0},{1,129},{129,1},{2,130},{130,2},{3,131},{131,3},{4... | collective-permute-start | bytes 50696 | tf_op jit(solution)/shard_map/ppermute | solution.py:356
  43.1 5.0 %copy-start.1 = (bf16[256,1024]{1,0:T(8,128)(2,1)S(1)}, bf16[256,1024]{1,0:T(8,128)(2,1)}, u32[]{:S(2)}) copy-start(bf16[256,1024]{1,0:T(8,128)(2,1)} %out_grad.7) | copy-start | bytes 1572868
  43.1 5.6 %collective-permute-start.3 = (f32[16,33,128]{2,1,0:T(8,128)S(1)}, f32[16,33,128]{2,1,0:T(8,128)S(1)}, u32[]{:S(2)}, u32[]{:S(2)}) collective-permute-start(f32[16,33,128]{2,1,0:T(8,128)S(1)} %all_to_all.21.wire.refs_4_), channel_id=1, source_target_pairs={{0,4},{4,0},{1,5},{5,1},{2,6},{6,2},{3,7},{7,3},{8,12},{12,8},{9,1... | collective-permute-start | bytes 811016 | tf_op jit(solution)/shard_map/ppermute | solution.py:356
  47.4 0.7 copy-start.5
  49.2 4.4 %collective-permute-start.6 = (f32[8,256]{1,0:T(8,128)S(1)}, f32[8,256]{1,0:T(8,128)S(1)}, u32[]{:S(2)}, u32[]{:S(2)}) collective-permute-start(f32[8,256]{1,0:T(8,128)S(1)} %get-tuple-element.120.rest_0_), channel_id=1, source_target_pairs={{0,3},{1,0},{2,1},{3,2},{4,7},{5,4},{6,5},{7,6},{8,11},{9,8},{10,9... | collective-permute-start | bytes 24584 | tf_op jit(solution)/shard_map/ppermute | solution.py:361
  52.0 3.7 %collective-permute-start.5 = (f32[8,256]{1,0:T(8,128)S(1)}, f32[8,256]{1,0:T(8,128)S(1)}, u32[]{:S(2)}, u32[]{:S(2)}) collective-permute-start(f32[8,256]{1,0:T(8,128)S(1)} %get-tuple-element.120.rest_0_), channel_id=1, source_target_pairs={{0,1},{1,2},{2,3},{3,0},{4,5},{5,6},{6,7},{7,4},{8,9},{9,10},{10,1... | collective-permute-start | bytes 24584 | tf_op jit(solution)/shard_map/ppermute | solution.py:361
  52.0 4.0 %collective-permute-start.4 = (f32[8,256]{1,0:T(8,128)S(1)}, f32[8,256]{1,0:T(8,128)S(1)}, u32[]{:S(2)}, u32[]{:S(2)}) collective-permute-start(f32[8,256]{1,0:T(8,128)S(1)} %get-tuple-element.120.rest_0_), channel_id=1, source_target_pairs={{0,2},{1,3},{2,0},{3,1},{4,6},{5,7},{6,4},{7,5},{8,10},{9,11},{10,... | collective-permute-start | bytes 24584 | tf_op jit(solution)/shard_map/ppermute | solution.py:361
  56.6 3.9 %collective-permute-start.7 = (f32[16,33,128]{2,1,0:T(8,128)S(1)}, f32[16,33,128]{2,1,0:T(8,128)S(1)}, u32[]{:S(2)}, u32[]{:S(2)}) collective-permute-start(f32[16,33,128]{2,1,0:T(8,128)S(1)} %get-tuple-element.124), channel_id=1, source_target_pairs={{0,4},{4,0},{1,5},{5,1},{2,6},{6,2},{3,7},{7,3},{8,12},{12,8},{9,1... | collective-permute-start | bytes 811016 | tf_op jit(solution)/shard_map/ppermute | solution.py:356
  59.0 1.7 %collective-permute-start.8 = (f32[16,33,128]{2,1,0:T(8,128)S(1)}, f32[16,33,128]{2,1,0:T(8,128)S(1)}, u32[]{:S(2)}, u32[]{:S(2)}) collective-permute-start(f32[16,33,128]{2,1,0:T(8,128)S(1)} %get-tuple-element.140), channel_id=1, source_target_pairs={{0,4},{4,0},{1,5},{5,1},{2,6},{6,2},{3,7},{7,3},{8,12},{12,8},{9,1... | collective-permute-start | bytes 811016 | tf_op jit(solution)/shard_map/ppermute | solution.py:356
  75.0 5.4 %collective-permute-start.9 = (f32[33,128]{1,0:T(8,128)S(1)}, f32[33,128]{1,0:T(8,128)S(1)}, u32[]{:S(2)}, u32[]{:S(2)}) collective-permute-start(f32[33,128]{1,0:T(8,128)S(1)} %group_total.3), channel_id=1, source_target_pairs={{0,128},{128,0},{1,129},{129,1},{2,130},{130,2},{3,131},{131,3},{4... | collective-permute-start | bytes 50696 | tf_op jit(solution)/shard_map/ppermute | solution.py:356
  80.5 17.2 %copy-start.3 = (bf16[256,1024]{1,0:T(8,128)(2,1)S(1)}, bf16[256,1024]{1,0:T(8,128)(2,1)}, u32[]{:S(2)}) copy-start(bf16[256,1024]{1,0:T(8,128)(2,1)} %keys.5) | copy-start | bytes 1572868
  94.4 4.6 %collective-permute-start.10 = (f32[16,33,128]{2,1,0:T(8,128)S(1)}, f32[16,33,128]{2,1,0:T(8,128)S(1)}, u32[]{:S(2)}, u32[]{:S(2)}) collective-permute-start(f32[16,33,128]{2,1,0:T(8,128)S(1)} %all_to_all.23.wire), channel_id=1, source_target_pairs={{0,4},{4,0},{1,5},{5,1},{2,6},{6,2},{3,7},{7,3},{8,12},{12,8},{9,1... | collective-permute-start | bytes 811016 | tf_op jit(solution)/shard_map/ppermute | solution.py:356

commit v4 on v3

--- a/solution.py
+++ b/solution.py
@@ -71,12 +71,10 @@
     wire[:, ROWS : ROWS + 1, :] = jnp.zeros((wire.shape[0], 1, HEAD_DIM), f32)
 
 
-def get_state(wire, extra, adds, place):
+def get_state(wire, place):
     first = place * BLOCKS
-    blocks = pl.ds(first, BLOCKS)
-    state = wire[blocks, 0:ROWS, :] + jnp.where(adds, extra[blocks, 0:ROWS, :], 0.0)
-    row = wire[first, ROWS : ROWS + 1, :] + jnp.where(adds, extra[first, ROWS : ROWS + 1, :], 0.0)
-    return state.reshape(HEAD_DIM, HEAD_DIM), row
+    state = wire[first : first + BLOCKS, 0:ROWS, :]
+    return state.reshape(HEAD_DIM, HEAD_DIM), wire[first, ROWS : ROWS + 1, :]
 
 
 def send_out(slots, target, slot, here, sem):
@@ -126,10 +124,21 @@
         denom[:, there] = jnp.broadcast_to(total, (tokens, HEAD_DIM))
 
 
-def attention_kernel(own, core, query_feat, numer_in, denom_in, wire, extra, gain, out_grad, *rest):
+def prepare_kernel(core, queries, keys, gain, out_grad, *outs):
+    heads_side = queries.shape[1] // HEAD_DIM // CORES
+    for half, own in enumerate((True, False)):
+        grad_in, query_slope, key_slope = outs[3 * half : 3 * half + 3]
+        for place in range(heads_side):
+            here = head_columns(side_of(core, own), place, heads_side)
+            there = columns(place)
+            grad_in[:, there] = gain[:, here] * out_grad[:, here].astype(f32)
+            query_slope[:, there] = feature_slope(queries[:, here].astype(f32))
+            key_slope[:, there] = feature_slope(keys[:, here].astype(f32))
+
+
+def attention_kernel(own, query_feat, numer_in, denom_in, wire, grad_in, *rest):
     tokens, width = query_feat.shape
     heads_side = width // HEAD_DIM
-    adds = core[0] == 1
     if own:
         attn_out, inverse_out, squares_out, cross_out = rest
         squares = jnp.zeros((tokens, HEAD_DIM), f32)
@@ -139,9 +148,8 @@
         squares = squares_in[...]
         cross = cross_in[...]
     for place in range(heads_side):
-        here = head_columns(side_of(core, own), place, heads_side)
         there = columns(place)
-        state, row = get_state(wire, extra, adds, place)
+        state, row = get_state(wire, place)
         both = jnp.concatenate([state, jnp.broadcast_to(row, state.shape)], axis=0)
         right = jnp.concatenate(split(both), axis=1)
         query = query_feat[:, there]
@@ -149,9 +157,8 @@
         numer = numer_in[:, there] + product[:, :HEAD_DIM]
         inverse = 1.0 / (denom_in[:, there] + product[:, HEAD_DIM:])
         attn = numer * inverse
-        grad_in = gain[:, here] * out_grad[:, here].astype(f32)
         squares = squares + attn * attn
-        cross = cross + attn * grad_in
+        cross = cross + attn * grad_in[:, there]
         attn_out[:, there] = attn
         inverse_out[:, there] = inverse
     if own:
@@ -180,7 +187,7 @@
     return spread[:, :HEAD_DIM], spread[:, HEAD_DIM:]
 
 
-def gradient_kernel(own, core, query_feat, attn_in, inverse_in, gain, out_grad, *rest):
+def gradient_kernel(own, query_feat, attn_in, inverse_in, grad_in, *rest):
     width = query_feat.shape[1]
     heads_side = width // HEAD_DIM
     if own:
@@ -195,12 +202,10 @@
         slope_out[...] = slope
     clear_rows(wire)
     for place in range(heads_side):
-        here = head_columns(side_of(core, own), place, heads_side)
         there = columns(place)
         attn = attn_in[:, there]
         inverse = inverse_in[:, there]
-        grad_in = gain[:, here] * out_grad[:, here].astype(f32)
-        d_attn = scale * grad_in - attn * slope
+        d_attn = scale * grad_in[:, there] - attn * slope
         d_numer = d_attn * inverse
         total = jnp.sum(d_attn * attn, axis=1, keepdims=True)
         d_denom = -total * inverse
@@ -211,73 +216,67 @@
         put_state(wire, place, dot(d_numer.astype(bf16), query, 0, 0), row)
 
 
-def early_backward_kernel(core, gain, scale_in, *refs):
-    halves, normed, parts = (refs[:3], refs[3:6]), refs[6], refs[7:9]
-    normed_slots, _, sems = refs[9:]
-    tokens, width_side = refs[0].shape
-    heads_side = width_side // HEAD_DIM
+def early_backward_kernel(low_own, numer_own, low_other, numer_other, part_own, part_other):
+    tokens = numer_own.shape[0]
+    halves = ((low_own, numer_own, part_own), (low_other, numer_other, part_other))
+    for low, d_numer, part in halves:
+        for place in range(part.shape[1] // HEAD_DIM):
+            there = columns(place)
+            numer_low = d_numer[:, there].astype(bf16)
+            part[:, there] = dot(low[:, columns(place, tokens)], numer_low, 0, 0)
+
+
+def inside_backward_kernel(core, values, gain, scale_in, *refs):
+    halves, refs = (refs[:7], refs[7:14]), refs[14:]
+    normed, query_grad, part_own, part_other, normed_slots, query_slots, sems, mixed_slots = refs
+    parts = (part_own, part_other)
+    tokens, width = values.shape
+    heads_side = width // HEAD_DIM // CORES
+    mask = causal(tokens)
     scale = scale_in[...]
     copies = []
     for half, own in enumerate((True, False)):
-        attn, low, d_numer_in = halves[half]
+        query_feat, key_feat, query_slope, d_numer_in, d_denom_in, attn, wire = halves[half]
         for place in range(heads_side):
             here = head_columns(side_of(core, own), place, heads_side)
             there = columns(place)
             slot = half * heads_side + place
             normed_slots[slot] = (gain[:, here] * attn[:, there] * scale).astype(bf16)
             copies.append(send_out(normed_slots, normed, slot, here, sems.at[0, slot]))
-    for half in range(CORES):
-        attn, low, d_numer_in = halves[half]
-        for place in range(heads_side):
-            there = columns(place)
-            numer_low = d_numer_in[:, there].astype(bf16)
-            parts[half][:, there] = dot(low[:, columns(place, tokens)], numer_low, 0, 0)
-    for copy in copies:
-        copy.wait()
-
-
-def inside_backward_kernel(core, queries, values, *refs):
-    halves, refs = (refs[:6], refs[6:12]), refs[12:]
-    query_grad, parts, (query_slots, _, sems) = refs[0], refs[1:3], refs[3:]
-    tokens, width = queries.shape
-    heads_side = width // HEAD_DIM // CORES
-    adds = core[0] == 1
-    mask = causal(tokens)
-    copies = []
-    for half, own in enumerate((True, False)):
-        query_feat, key_feat, d_numer_in, d_denom_in, wire, extra = halves[half]
-        for place in range(heads_side):
-            here = head_columns(side_of(core, own), place, heads_side)
-            there = columns(place)
-            slot = half * heads_side + place
-            state, row = get_state(wire, extra, adds, place)
+            state, row = get_state(wire, place)
             state_high, state_low = split(state)
             d_denom = d_denom_in[:, there]
             numer_low, numer_rest = split(d_numer_in[:, there])
-            key = key_feat[:, there]
             mixed = dot(numer_low, values[:, here], 1, 1)
             mixed = mixed + jnp.concatenate([d_denom, d_denom], axis=1)
             mixed_low = jnp.where(mask, mixed, 0.0).astype(bf16)
+            mixed_slots[slot] = mixed_low
             left = jnp.concatenate([numer_low, numer_low, numer_rest], axis=1)
             right = jnp.concatenate([state_high, state_low, state_high], axis=0)
-            grad = dot(left, right, 1, 0) + d_denom * row + dot(mixed_low, key, 1, 0)
-            query_raw = queries[:, here].astype(f32)
-            query_slots[slot] = (grad * feature_slope(query_raw)).astype(bf16)
-            copies.append(send_out(query_slots, query_grad, slot, here, sems.at[0, slot]))
+            grad = dot(left, right, 1, 0) + d_denom * row
+            grad = grad + dot(mixed_low, key_feat[:, there], 1, 0)
+            query_slots[slot] = (grad * query_slope[:, there]).astype(bf16)
+            copies.append(send_out(query_slots, query_grad, slot, here, sems.at[1, slot]))
+    for half in range(CORES):
+        query_feat = halves[half][0]
+        for place in range(heads_side):
+            there = columns(place)
+            mixed_low = mixed_slots[half * heads_side + place]
             parts[half][:, there] = dot(mixed_low, query_feat[:, there], 0, 0)
     for copy in copies:
         copy.wait()
 
 
-def outside_backward_kernel(own, core, keys, values, key_feat, key_part, value_part, wire, extra, *rest):
+def outside_backward_kernel(
+    own, core, key_slope, values, key_feat, key_part, value_part, wire, *rest
+):
     key_grad, value_grad, key_slots, value_slots, sems = rest[-5:]
     heads_side = key_feat.shape[1] // HEAD_DIM
-    adds = core[0] == 0
     copies = []
     for place in range(heads_side):
         here = head_columns(side_of(core, own), place, heads_side)
         there = columns(place)
-        state, row = get_state(wire, extra, adds, place)
+        state, row = get_state(wire, place)
         high, low = split(state)
         value = values[:, here]
         key = key_feat[:, there]
@@ -285,8 +284,7 @@
             jnp.concatenate([value, value], axis=1), jnp.concatenate([high, low], axis=0), 1, 0
         )
         grad = grad + row + key_part[:, there]
-        key_raw = keys[:, here].astype(f32)
-        key_slots[place] = (grad * feature_slope(key_raw)).astype(bf16)
+        key_slots[place] = (grad * key_slope[:, there]).astype(bf16)
         copies.append(send_out(key_slots, key_grad, place, here, sems.at[0, place]))
         grad = dot(
             jnp.concatenate([key, key], axis=1), jnp.concatenate([high, low], axis=1), 1, 1
@@ -315,13 +313,31 @@
             total = total + spread[chip]
 
 
+def halves_of(chips, top):
+    size = chips // 2
+    for half in range(2):
+        yield pl.ds(half * size, size), pl.ds(lax.rem(half + top[0], 2) * size, size)
+
+
+def pair_kernel(top, mine, extra, pair):
+    for here, there in halves_of(pair.shape[0], top):
+        pair[here] = mine[there] + extra[there]
+
+
+def finish_kernel(backward, core, top, kept, mine, extra, own, send):
+    later = core[0] == (0 if backward else 1)
+    for here, there in halves_of(own.shape[0], top):
+        own[here] = kept[there] + jnp.where(later, extra[here], 0.0)
+        send[here] = kept[there] + jnp.where(later, 0.0, mine[here])
+
+
 def shaped(shape, dtype):
     return jax.ShapeDtypeStruct(shape, dtype)
 
 
 def call(
-    kernel, name, out_shape, *operands, core=None, flops=0, hbm_in=(), hbm_out=(), slots=0,
-    vmem=16, aliases=None,
+    kernel, name, out_shape, *operands, scalars=(), flops=0, hbm_in=(), hbm_out=(), slots=0,
+    vmem=16, aliases=None, scratch=(),
 ):
     moved = sum(x.size * x.dtype.itemsize for x in operands)
     moved += sum(x.size * x.dtype.itemsize for x in jax.tree.leaves(out_shape))
@@ -332,19 +348,18 @@
 
     in_specs = spaces(len(operands), hbm_in)
     out_specs = spaces(len(jax.tree.leaves(out_shape)), hbm_out)
-    scratch = []
+    scratch_shapes = []
     if slots:
-        scratch = [pltpu.VMEM((slots, BLOCK, HEAD_DIM), bf16)] * 2
-        scratch.append(pltpu.SemaphoreType.DMA((2, slots)))
-    if core is not None:
-        in_specs = [pl.BlockSpec(memory_space=pltpu.SMEM)] + in_specs
-        operands = (core,) + operands
+        scratch_shapes = [pltpu.VMEM((slots, BLOCK, HEAD_DIM), bf16)] * 2
+        scratch_shapes.append(pltpu.SemaphoreType.DMA((2, slots)))
+    in_specs = [pl.BlockSpec(memory_space=pltpu.SMEM) for _ in scalars] + in_specs
+    operands = scalars + operands
     return pl.pallas_call(
         kernel,
         out_shape=out_shape,
         in_specs=in_specs,
         out_specs=tuple(out_specs) if isinstance(out_shape, tuple) else out_specs[0],
-        scratch_shapes=scratch,
+        scratch_shapes=scratch_shapes + list(scratch),
         input_output_aliases=aliases or {},
         compiler_params=pltpu.CompilerParams(vmem_limit_bytes=vmem << 20),
         cost_estimate=pl.CostEstimate(flops=flops, bytes_accessed=moved, transcendentals=0),
@@ -365,20 +380,27 @@
     return lax.optimization_barrier((first, later))
 
 
-def scan_chips(pair, top, backward, inside=None, operands=()):
+def scan_chips(mine, extra, core, top, backward, inside=None, operands=()):
+    wire = shaped(mine.shape, f32)
+    pair = call(pair_kernel, "pair", wire, mine, extra, scalars=(top,))
     spread = lax.all_to_all(pair, "chip", 0, 0)
     total = call(group_total_kernel, "group_total", shaped(spread.shape[1:], f32), spread)
     done = ()
-    if inside is None:
-        other = swap(total, "top")
-    else:
+    if inside is not None:
         total, operands = after(total, *operands)
-        other = swap(total, "top")
+    chips = spread.shape[0]
+    facing = [(chip, chips + (chip + chips // 2) % chips) for chip in range(chips)]
+    other = lax.ppermute(total, ("top", "chip"), facing + [(b, a) for a, b in facing])
+    if inside is not None:
         done = inside(*operands)
     other, spread, done = lax.optimization_barrier((other, spread, done))
     kernel = functools.partial(chip_sums_kernel, backward)
-    sums = call(kernel, "chip_sums", shaped(spread.shape, f32), spread, other, core=top)
-    return lax.all_to_all(sums, "chip", 0, 0), done
+    sums = call(kernel, "chip_sums", wire, spread, other, scalars=(top,))
+    kept = lax.all_to_all(sums, "chip", 0, 0)
+    kernel = functools.partial(finish_kernel, backward)
+    own, send = call(kernel, "finish", (wire, wire), kept, mine, extra, scalars=(core, top))
+    own, (send,) = after(own, send)
+    return own, swap(send, "core"), done
 
 
 def body(queries, key_rows, value_rows, norm_gain, out_grad):
@@ -398,88 +420,93 @@
     stats_shape = shaped((8, tokens), f32)
     unit = tokens * HEAD_DIM * HEAD_DIM * heads
 
-    def side_call(kernel, name, own, *args, **named):
+    def side_call(kernel, name, own, *args, scalars=(core,), **named):
         kernel = functools.partial(kernel, own)
-        return call(kernel, name + ("_own" if own else "_other"), *args, core=core, **named)
+        return call(kernel, name + ("_own" if own else "_other"), *args, scalars=scalars, **named)
 
     key_own, key_other = call(
-        key_features_kernel, "key_features", (half_low, half_low), key_rows, core=core
+        key_features_kernel, "key_features", (half_low, half_low), key_rows, scalars=(core,)
     )
     theirs = side_call(states_kernel, "states", False, wire, key_other, value_rows, flops=unit)
     theirs, (key_own,) = after(theirs, key_own)
     extra = swap(theirs, "core")
     mine = side_call(states_kernel, "states", True, wire, key_own, value_rows, flops=unit)
-    mine, (key_own, queries_in) = after(mine, key_own, queries)
-    extra_got = swap(mine, "core")
     halves = (half_low, square, half, half)
-    inside = side_call(
-        inside_forward_kernel, "inside_forward", True, halves, queries_in, value_rows, key_own,
-        flops=4 * unit,
-    )
-    extra, extra_got, mine, inside = lax.optimization_barrier((extra, extra_got, mine, inside))
-    query_own, low_own, numer, denom = inside
-    kept, _ = scan_chips(mine + extra, top, False)
-    kept, (queries_in, key_other) = after(kept, queries, key_other)
-    got = swap(kept, "core")
+    own_kernels = (queries, key_rows, value_rows, key_own, gain, out_grad)
+
+    def inside_forward_own(queries, keys, values, key_own, gain, out_grad):
+        first = side_call(
+            inside_forward_kernel, "inside_forward", True, halves, queries, values, key_own,
+            flops=4 * unit,
+        )
+        return first, call(
+            prepare_kernel, "prepare", (half,) * 6, queries, keys, gain, out_grad,
+            scalars=(core,), flops=unit,
+        )
+
+    kept, got, inside = scan_chips(
+        mine, extra, core, top, False, inside_forward_own, own_kernels
+    )
+    (query_own, low_own, numer, denom), prepared = inside
+    grad_own, query_slope, key_slope, grad_other, query_slope_other, key_slope_other = prepared
+    kept, (key_other,) = after(kept, key_other)
     query_other, low_other, numer_other, denom_other = side_call(
-        inside_forward_kernel, "inside_forward", False, halves, queries_in, value_rows, key_other,
+        inside_forward_kernel, "inside_forward", False, halves, queries, value_rows, key_other,
         flops=4 * unit,
     )
     attn_own, inverse_own, squares, cross = side_call(
         attention_kernel, "attention", True, (half, half, lanes, lanes),
-        query_own, numer, denom, kept, extra, gain, out_grad, flops=4 * unit,
+        query_own, numer, denom, kept, grad_own, flops=4 * unit, scalars=(),
     )
     attn_other, inverse_other, stats = side_call(
         attention_kernel, "attention", False, (half, half, stats_shape),
-        query_other, numer_other, denom_other, got, extra_got, gain, out_grad, squares, cross,
-        flops=4 * unit,
-    )
-    prefix_own = (kept, extra)
-    prefix_other = (got, extra_got)
+        query_other, numer_other, denom_other, got, grad_other, squares, cross,
+        flops=4 * unit, scalars=(),
+    )
     stats_from = [shifted(stats, "head", step) for step in (2, 1, 3)]
     d_numer_other, d_denom_other, theirs, scale, slope = side_call(
         gradient_kernel, "gradient", False, (half, half, wire, lanes, lanes),
-        query_other, attn_other, inverse_other, gain, out_grad, stats, *stats_from, flops=unit,
+        query_other, attn_other, inverse_other, grad_other, stats, *stats_from,
+        flops=unit, scalars=(),
     )
     theirs, (scale, slope) = after(theirs, scale, slope)
     extra = swap(theirs, "core")
     d_numer_own, d_denom_own, mine = side_call(
         gradient_kernel, "gradient", True, (half, half, wire),
-        query_own, attn_own, inverse_own, gain, out_grad, scale, slope, flops=unit,
-    )
-
-    mine, (scale,) = after(mine, scale)
-    extra_got = swap(mine, "core")
-    normed, value_part, value_part_other = call(
-        early_backward_kernel, "early_backward", (narrow, half, half), gain, scale,
-        attn_own, low_own, d_numer_own, attn_other, low_other, d_numer_other,
-        core=core, flops=4 * unit, hbm_out=(0,), slots=heads,
-    )
-    extra, extra_got, mine, normed, value_part, value_part_other = lax.optimization_barrier(
-        (extra, extra_got, mine, normed, value_part, value_part_other)
+        query_own, attn_own, inverse_own, grad_own, scale, slope, flops=unit, scalars=(),
+    )
+
+    mine, (d_numer_own,) = after(mine, d_numer_own)
+    value_part, value_part_other = call(
+        early_backward_kernel, "early_backward", (half, half),
+        low_own, d_numer_own, low_other, d_numer_other, flops=4 * unit,
+    )
+    extra, mine, value_part, value_part_other = lax.optimization_barrier(
+        (extra, mine, value_part, value_part_other)
     )
 
     def inside_backward(*operands):
         return call(
-            inside_backward_kernel, "inside_backward", (narrow, half, half),
-            *operands, core=core, flops=18 * unit, hbm_out=(0,), slots=heads,
+            inside_backward_kernel, "inside_backward", (narrow, narrow, half, half),
+            *operands, scalars=(core,), flops=18 * unit, hbm_out=(0, 1), slots=heads,
+            scratch=(pltpu.VMEM((heads, tokens, tokens), bf16),),
         )
 
-    operands = (queries, value_rows)
-    operands += (query_own, key_own, d_numer_own, d_denom_own) + prefix_own
-    operands += (query_other, key_other, d_numer_other, d_denom_other) + prefix_other
-    kept, inside = scan_chips(mine + extra, top, True, inside_backward, operands)
-    query_grad, key_part, key_part_other = inside
-    got = swap(kept, "core")
+    operands = (value_rows, gain, scale)
+    operands += (query_own, key_own, query_slope, d_numer_own, d_denom_own, attn_own, kept)
+    operands += (query_other, key_other, query_slope_other, d_numer_other, d_denom_other)
+    operands += (attn_other, got)
+    kept, got, inside = scan_chips(mine, extra, core, top, True, inside_backward, operands)
+    normed, query_grad, key_part, key_part_other = inside
     last = dict(flops=4 * unit, hbm_out=(0, 1), slots=heads_side)
     key_grad, value_grad = side_call(
         outside_backward_kernel, "outside_backward", True, (narrow, narrow),
-        key_rows, value_rows, key_own, key_part, value_part, kept, extra, **last,
+        key_slope, value_rows, key_own, key_part, value_part, kept, **last,
     )
     key_grad, value_grad = side_call(
         outside_backward_kernel, "outside_backward", False, (narrow, narrow),
-        key_rows, value_rows, key_other, key_part_other, value_part_other, got, extra_got,
-        key_grad, value_grad, hbm_in=(7, 8), aliases={8: 0, 9: 1}, **last,
+        key_slope_other, value_rows, key_other, key_part_other, value_part_other, got,
+        key_grad, value_grad, hbm_in=(6, 7), aliases={7: 0, 8: 1}, **last,
     )
     return (normed, query_grad, key_grad, value_grad)
 

time: 101 us -> 98.2 us (0.972)
  starting transfers between devices: 22.8 us -> 21.3 us
    ppermute x8 -> x4, starting transfers between devices: 18.3 us -> 13.1 us  [swap(): return lax.ppermute(array, axis, [(0, 1), (1, 0)])]
    ppermute x0 -> x2, starting transfers between devices: none -> 3.81 us  [scan_chips(): lax.ppermute(total, ('top', 'chip'), facing + [(b, a) for a, b in facing])]
    ppermute x8 -> x4, waiting for transfers between devices: 3.09 us -> 1.57 us  [swap(): return lax.ppermute(array, axis, [(0, 1), (1, 0)])]
    ppermute x0 -> x2, waiting for transfers between devices: none -> 1.37 us  [scan_chips(): lax.ppermute(total, ('top', 'chip'), facing + [(b, a) for a, b in facing])]
    pallas_call x17 -> x22, Pallas kernels: 10.7 us -> 10.1 us  [call(): pl.pallas_call(kernel, out_shape=out_shape, in_specs=in_specs, out_specs=...]
  transfers between devices with their start and end apart: 11 -> 9, of which waited for: 8 -> 7; matrix products, arithmetic and copies ran while one was open for 0% -> 0% of each run, Pallas kernels for 7% -> 7%
where the time goes in v4:
time: 98.2 us; the launch traced here: 98 us
  blocking collectives  59.2 us (60%)
  starting transfers between devices  21.3 us (22%)
  Pallas kernels  10.1 us (10%)
  waiting for transfers between devices  5.3 us (5%)
  local copies, waits for them, and re-layouts  1.11 us (1%)
    all_to_all x2, blocking collectives, scan_chips(): spread = lax.all_to_all(pair, 'chip', 0, 0)  31.6 us
    all_to_all x2, blocking collectives, scan_chips(): kept = lax.all_to_all(sums, 'chip', 0, 0)  27.7 us
    ppermute x4, starting transfers between devices, swap(): return lax.ppermute(array, axis, [(0, 1), (1, 0)])  13.1 us
    pallas_call x22, Pallas kernels, call(): pl.pallas_call(kernel, out_shape=out_shape, in_specs=in_specs, out_specs=...  10.1 us
    ppermute x3, starting transfers between devices, shifted(): lax.ppermute(array, axis, [(i, (i + step) % size) for i in range(size)])  4.4 us
    ppermute x2, starting transfers between devices, scan_chips(): lax.ppermute(total, ('top', 'chip'), facing + [(b, a) for a, b in facing])  3.81 us
    ppermute x3, waiting for transfers between devices, shifted(): lax.ppermute(array, axis, [(i, (i + step) % size) for i in range(size)])  2.36 us
  transfers between devices with their start and end apart: 9, of which 7 were waited for; matrix products, arithmetic and copies ran while one was open for 0% of the time, Pallas kernels for 7%

profile of v4, /device:TPU:1, one launch (start us, length us, event | category | flops | bytes accessed | tf_op | source)
XLA Modules:
  0.0 98.0 jit_solution(15280872031632503715)
XLA Ops:
  0.6 0.0 copy-start
  0.6 0.0 copy-start.2
  0.7 1.1 %copy-done.2 = bf16[256,1024]{1,0:T(8,128)(2,1)S(1)} copy-done((bf16[256,1024]{1,0:T(8,128)(2,1)S(1)}, bf16[256,1024]{1,0:T(8,128)(2,1)}, u32[]{:S(2)}) %copy-start.2) | copy-done | bytes 524312
  1.7 0.3 key_features.1
  2.0 0.0 copy-done
  2.0 0.3 states_other.1
  2.3 3.3 %collective-permute-start = (f32[16,33,128]{2,1,0:T(8,128)S(1)}, f32[16,33,128]{2,1,0:T(8,128)S(1)}, u32[]{:S(2)}, u32[]{:S(2)}) collective-permute-start(f32[16,33,128]{2,1,0:T(8,128)S(1)} %states_other.1), channel_id=1, source_target_pairs={{0,4},{4,0},{1,5},{5,1},{2,6},{6,2},{3,7},{7,3},{8,12},{12,8},{9,1... | collective-permute-start | bytes 811016 | tf_op jit(solution)/shard_map/ppermute | solution.py:371
  5.7 0.3 states_own.1.mine
  6.0 1.0 collective-permute-done.extra
  6.9 0.0 copy-start.3
  7.0 0.0 copy-start.1
  7.0 17.6 %all_to_all.20.spread = f32[16,33,128]{2,1,0:T(8,128)S(1)} all-to-all(f32[16,33,128]{2,1,0:T(8,128)S(1)} %pair.2), channel_id=1, replica_groups=mesh['top'=2,'chip'=16,'core'=2,'head'=4] {'chip'}, dimensions={0} | all-to-all | bytes 540672 | tf_op jit(solution)/shard_map/all_to_all | solution.py:386
  24.6 1.3 %collective-permute-start.1 = (f32[33,128]{1,0:T(8,128)S(1)}, f32[33,128]{1,0:T(8,128)S(1)}, u32[]{:S(2)}, u32[]{:S(2)}) collective-permute-start(f32[33,128]{1,0:T(8,128)S(1)} %group_total.2), channel_id=1, source_target_pairs={{0,192},{8,200},{16,208},{24,216},{32,224},{40,232},{48,240},{56,2... | collective-permute-start | bytes 50696 | tf_op jit(solution)/shard_map/ppermute | solution.py:393
  25.9 0.0 copy-done.3
  25.9 0.0 copy-done.4
  25.9 0.0 copy-done.1
  25.9 0.0 copy-done.5
  25.9 0.5 prepare.1
  26.5 0.7 inside_forward_own.1
  27.2 1.4 %collective-permute-done.1.other = f32[33,128]{1,0:T(8,128)S(1)} collective-permute-done((f32[33,128]{1,0:T(8,128)S(1)}, f32[33,128]{1,0:T(8,128)S(1)}, u32[]{:S(2)}, u32[]{:S(2)}) %collective-permute-start.1) | collective-permute-done | bytes 16928 | tf_op jit(solution)/shard_map/ppermute | solution.py:393
  28.6 12.8 %all_to_all.21.kept = f32[16,33,128]{2,1,0:T(8,128)S(1)} all-to-all(f32[16,33,128]{2,1,0:T(8,128)S(1)} %chip_sums.2), channel_id=1, replica_groups=mesh['top'=2,'chip'=16,'core'=2,'head'=4] {'chip'}, dimensions={0} | all-to-all | bytes 540672 | tf_op jit(solution)/shard_map/all_to_all | solution.py:399
  41.4 0.1 finish.2
  41.5 4.5 %collective-permute-start.2 = (f32[16,33,128]{2,1,0:T(8,128)S(1)}, f32[16,33,128]{2,1,0:T(8,128)S(1)}, u32[]{:S(2)}, u32[]{:S(2)}) collective-permute-start(f32[16,33,128]{2,1,0:T(8,128)S(1)} %get-tuple-element.137), channel_id=1, source_target_pairs={{0,4},{4,0},{1,5},{5,1},{2,6},{6,2},{3,7},{7,3},{8,12},{12,8},{9,1... | collective-permute-start | bytes 811016 | tf_op jit(solution)/shard_map/ppermute | solution.py:371
  46.0 0.7 inside_forward_other.1
  46.7 0.4 attention_own.1
  47.0 0.2 collective-permute-done.2.wire.refs_13_
  47.3 0.5 attention_other.1
  47.8 2.8 %collective-permute-start.5 = (f32[8,256]{1,0:T(8,128)S(1)}, f32[8,256]{1,0:T(8,128)S(1)}, u32[]{:S(2)}, u32[]{:S(2)}) collective-permute-start(f32[8,256]{1,0:T(8,128)S(1)} %get-tuple-element.148.rest_0_), channel_id=1, source_target_pairs={{0,3},{1,0},{2,1},{3,2},{4,7},{5,4},{6,5},{7,6},{8,11},{9,8},{10,9... | collective-permute-start | bytes 24584 | tf_op jit(solution)/shard_map/ppermute | solution.py:376
  50.6 0.0 collective-permute-start.4
  50.6 1.6 %collective-permute-start.3 = (f32[8,256]{1,0:T(8,128)S(1)}, f32[8,256]{1,0:T(8,128)S(1)}, u32[]{:S(2)}, u32[]{:S(2)}) collective-permute-start(f32[8,256]{1,0:T(8,128)S(1)} %get-tuple-element.148.rest_0_), channel_id=1, source_target_pairs={{0,2},{1,3},{2,0},{3,1},{4,6},{5,7},{6,4},{7,5},{8,10},{9,11},{10,... | collective-permute-start | bytes 24584 | tf_op jit(solution)/shard_map/ppermute | solution.py:376
  52.2 0.0 collective-permute-done.5.rest_3_
  52.2 2.1 %collective-permute-done.4.rest_2_ = f32[8,256]{1,0:T(8,128)S(1)} collective-permute-done((f32[8,256]{1,0:T(8,128)S(1)}, f32[8,256]{1,0:T(8,128)S(1)}, u32[]{:S(2)}, u32[]{:S(2)}) %collective-permute-start.4) | collective-permute-done | bytes 8224 | tf_op jit(solution)/shard_map/ppermute | solution.py:376
  54.3 0.3 collective-permute-done.3.rest_1_
  54.6 0.6 gradient_other.1
  55.2 1.9 %collective-permute-start.6 = (f32[16,33,128]{2,1,0:T(8,128)S(1)}, f32[16,33,128]{2,1,0:T(8,128)S(1)}, u32[]{:S(2)}, u32[]{:S(2)}) collective-permute-start(f32[16,33,128]{2,1,0:T(8,128)S(1)} %get-tuple-element.152), channel_id=1, source_target_pairs={{0,4},{4,0},{1,5},{5,1},{2,6},{6,2},{3,7},{7,3},{8,12},{12,8},{9,1... | collective-permute-start | bytes 811016 | tf_op jit(solution)/shard_map/ppermute | solution.py:371
  57.1 0.4 gradient_own.1
  57.6 0.5 early_backward.1
  58.1 0.3 collective-permute-done.6.extra
  58.4 14.0 %all_to_all.22.spread = f32[16,33,128]{2,1,0:T(8,128)S(1)} all-to-all(f32[16,33,128]{2,1,0:T(8,128)S(1)} %pair.3), channel_id=1, replica_groups=mesh['top'=2,'chip'=16,'core'=2,'head'=4] {'chip'}, dimensions={0} | all-to-all | bytes 540672 | tf_op jit(solution)/shard_map/all_to_all | solution.py:386
  72.4 2.5 %collective-permute-start.7 = (f32[33,128]{1,0:T(8,128)S(1)}, f32[33,128]{1,0:T(8,128)S(1)}, u32[]{:S(2)}, u32[]{:S(2)}) collective-permute-start(f32[33,128]{1,0:T(8,128)S(1)} %group_total.3), channel_id=1, source_target_pairs={{0,192},{8,200},{16,208},{24,216},{32,224},{40,232},{48,240},{56,2... | collective-permute-start | bytes 50696 | tf_op jit(solution)/shard_map/ppermute | solution.py:393
  74.9 2.2 %inside_backward.1 = (bf16[256,1024]{1,0:T(8,128)(2,1)}, bf16[256,1024]{1,0:T(8,128)(2,1)}, f32[256,512]{1,0:T(8,128)S(1)}, f32[256,512]{1,0:T(8,128)S(1)}) custom-call(s32[1]{0:T(128)} %bitcast.core, bf16[256,1024]{1,0:T(8,128)(2,1)S(1)} %copy-done, f32[1,1024]{1,0:T(1,128)S(1)} %bitcast.4, f32[256,128]{1,0:T(8,128)S(1)} %get-tuple-element.175.rest_0_.scale_in, ...), custom_call_target="tpu_custom_call" | custom-call | flops 603979776 | bytes 8540160 | tf_op jit(solution)/shard_map/inside_backward/pallas_call | solution.py:357
  77.1 0.0 collective-permute-done.7.other
  77.1 14.9 %all_to_all.23.kept = f32[16,33,128]{2,1,0:T(8,128)S(1)} all-to-all(f32[16,33,128]{2,1,0:T(8,128)S(1)} %chip_sums.3), channel_id=1, replica_groups=mesh['top'=2,'chip'=16,'core'=2,'head'=4] {'chip'}, dimensions={0} | all-to-all | bytes 540672 | tf_op jit(solution)/shard_map/all_to_all | solution.py:399
  92.0 0.1 finish.3
  92.1 3.3 %collective-permute-start.8 = (f32[16,33,128]{2,1,0:T(8,128)S(1)}, f32[16,33,128]{2,1,0:T(8,128)S(1)}, u32[]{:S(2)}, u32[]{:S(2)}) collective-permute-start(f32[16,33,128]{2,1,0:T(8,128)S(1)} %get-tuple-element.201), channel_id=1, source_target_pairs={{0,4},{4,0},{1,5},{5,1},{2,6},{6,2},{3,7},{7,3},{8,12},{12,8},{9,1... | collective-permute-start | bytes 811016 | tf_op jit(solution)/shard_map/ppermute | solution.py:371
  95.4 1.2 %outside_backward_own.1 = (bf16[256,1024]{1,0:T(8,128)(2,1)}, bf16[256,1024]{1,0:T(8,128)(2,1)}) custom-call(s32[1]{0:T(128)} %bitcast.core, f32[256,512]{1,0:T(8,128)S(1)} %get-tuple-element.202.key_slope, bf16[256,1024]{1,0:T(8,128)(2,1)S(1)} %copy-done, bf16[256,512]{1,0:T(8,128)(2,1)S(1)} %get-tuple-element.177.key_feat.refs_1_, ...), custom_call_target="tpu_custom_call" | custom-call | flops 134217728 | bytes 3678208 | tf_op jit(solution)/shard_map/outside_backward_own/pallas_call | solution.py:357
  96.6 0.1 collective-permute-done.8.wire
  96.7 1.1 %outside_backward_other.1 = (bf16[256,1024]{1,0:T(8,128)(2,1)}, bf16[256,1024]{1,0:T(8,128)(2,1)}) custom-call(s32[1]{0:T(128)} %bitcast.core, f32[256,512]{1,0:T(8,128)S(1)} %get-tuple-element.196.key_slope, bf16[256,1024]{1,0:T(8,128)(2,1)S(1)} %copy-done, ...), custom_call_target="tpu_custom_call", output_to_operand_aliasing={{0}: (7, {}), {1}: (8, {})} | custom-call | flops 134217728 | bytes 4726784 | tf_op jit(solution)/shard_map/outside_backward_other/pallas_call | solution.py:357
  (8 shorter events, 0.2 us)
Async XLA Ops:
  0.6 1.4 %copy-start = (bf16[256,1024]{1,0:T(8,128)(2,1)S(1)}, bf16[256,1024]{1,0:T(8,128)(2,1)}, u32[]{:S(2)}) copy-start(bf16[256,1024]{1,0:T(8,128)(2,1)} %values.11) | copy-start | bytes 1572868
  0.6 1.1 %copy-start.2 = (bf16[256,1024]{1,0:T(8,128)(2,1)S(1)}, bf16[256,1024]{1,0:T(8,128)(2,1)}, u32[]{:S(2)}) copy-start(bf16[256,1024]{1,0:T(8,128)(2,1)} %keys.2) | copy-start | bytes 1572868
  2.3 4.6 %collective-permute-start = (f32[16,33,128]{2,1,0:T(8,128)S(1)}, f32[16,33,128]{2,1,0:T(8,128)S(1)}, u32[]{:S(2)}, u32[]{:S(2)}) collective-permute-start(f32[16,33,128]{2,1,0:T(8,128)S(1)} %states_other.1), channel_id=1, source_target_pairs={{0,4},{4,0},{1,5},{5,1},{2,6},{6,2},{3,7},{7,3},{8,12},{12,8},{9,1... | collective-permute-start | bytes 811016 | tf_op jit(solution)/shard_map/ppermute | solution.py:371
  6.9 19.0 %copy-start.3 = (bf16[256,1024]{1,0:T(8,128)(2,1)S(1)}, bf16[256,1024]{1,0:T(8,128)(2,1)}, u32[]{:S(2)}) copy-start(bf16[256,1024]{1,0:T(8,128)(2,1)} %keys.2) | copy-start | bytes 1572868
  6.9 19.0 %copy-start.4 = (bf16[256,1024]{1,0:T(8,128)(2,1)S(1)}, bf16[256,1024]{1,0:T(8,128)(2,1)}, u32[]{:S(2)}) copy-start(bf16[256,1024]{1,0:T(8,128)(2,1)} %out_grad) | copy-start | bytes 1572868
  7.0 19.0 %copy-start.1 = (bf16[256,1024]{1,0:T(8,128)(2,1)S(1)}, bf16[256,1024]{1,0:T(8,128)(2,1)}, u32[]{:S(2)}) copy-start(bf16[256,1024]{1,0:T(8,128)(2,1)} %queries.3) | copy-start | bytes 1572868
  24.6 1.4 %copy-start.5 = (f32[1024]{0:T(1024)S(1)}, f32[1024]{0:T(1024)}, u32[]{:S(2)}) copy-start(f32[1024]{0:T(1024)} %param.8) | copy-start | bytes 12292
  24.6 3.9 %collective-permute-start.1 = (f32[33,128]{1,0:T(8,128)S(1)}, f32[33,128]{1,0:T(8,128)S(1)}, u32[]{:S(2)}, u32[]{:S(2)}) collective-permute-start(f32[33,128]{1,0:T(8,128)S(1)} %group_total.2), channel_id=1, source_target_pairs={{0,192},{8,200},{16,208},{24,216},{32,224},{40,232},{48,240},{56,2... | collective-permute-start | bytes 50696 | tf_op jit(solution)/shard_map/ppermute | solution.py:393
  41.5 5.8 %collective-permute-start.2 = (f32[16,33,128]{2,1,0:T(8,128)S(1)}, f32[16,33,128]{2,1,0:T(8,128)S(1)}, u32[]{:S(2)}, u32[]{:S(2)}) collective-permute-start(f32[16,33,128]{2,1,0:T(8,128)S(1)} %get-tuple-element.137), channel_id=1, source_target_pairs={{0,4},{4,0},{1,5},{5,1},{2,6},{6,2},{3,7},{7,3},{8,12},{12,8},{9,1... | collective-permute-start | bytes 811016 | tf_op jit(solution)/shard_map/ppermute | solution.py:371
  47.8 4.4 %collective-permute-start.5 = (f32[8,256]{1,0:T(8,128)S(1)}, f32[8,256]{1,0:T(8,128)S(1)}, u32[]{:S(2)}, u32[]{:S(2)}) collective-permute-start(f32[8,256]{1,0:T(8,128)S(1)} %get-tuple-element.148.rest_0_), channel_id=1, source_target_pairs={{0,3},{1,0},{2,1},{3,2},{4,7},{5,4},{6,5},{7,6},{8,11},{9,8},{10,9... | collective-permute-start | bytes 24584 | tf_op jit(solution)/shard_map/ppermute | solution.py:376
  50.6 3.7 %collective-permute-start.4 = (f32[8,256]{1,0:T(8,128)S(1)}, f32[8,256]{1,0:T(8,128)S(1)}, u32[]{:S(2)}, u32[]{:S(2)}) collective-permute-start(f32[8,256]{1,0:T(8,128)S(1)} %get-tuple-element.148.rest_0_), channel_id=1, source_target_pairs={{0,1},{1,2},{2,3},{3,0},{4,5},{5,6},{6,7},{7,4},{8,9},{9,10},{10,1... | collective-permute-start | bytes 24584 | tf_op jit(solution)/shard_map/ppermute | solution.py:376
  50.6 4.0 %collective-permute-start.3 = (f32[8,256]{1,0:T(8,128)S(1)}, f32[8,256]{1,0:T(8,128)S(1)}, u32[]{:S(2)}, u32[]{:S(2)}) collective-permute-start(f32[8,256]{1,0:T(8,128)S(1)} %get-tuple-element.148.rest_0_), channel_id=1, source_target_pairs={{0,2},{1,3},{2,0},{3,1},{4,6},{5,7},{6,4},{7,5},{8,10},{9,11},{10,... | collective-permute-start | bytes 24584 | tf_op jit(solution)/shard_map/ppermute | solution.py:376
  55.2 3.1 %collective-permute-start.6 = (f32[16,33,128]{2,1,0:T(8,128)S(1)}, f32[16,33,128]{2,1,0:T(8,128)S(1)}, u32[]{:S(2)}, u32[]{:S(2)}) collective-permute-start(f32[16,33,128]{2,1,0:T(8,128)S(1)} %get-tuple-element.152), channel_id=1, source_target_pairs={{0,4},{4,0},{1,5},{5,1},{2,6},{6,2},{3,7},{7,3},{8,12},{12,8},{9,1... | collective-permute-start | bytes 811016 | tf_op jit(solution)/shard_map/ppermute | solution.py:371
  72.4 4.7 %collective-permute-start.7 = (f32[33,128]{1,0:T(8,128)S(1)}, f32[33,128]{1,0:T(8,128)S(1)}, u32[]{:S(2)}, u32[]{:S(2)}) collective-permute-start(f32[33,128]{1,0:T(8,128)S(1)} %group_total.3), channel_id=1, source_target_pairs={{0,192},{8,200},{16,208},{24,216},{32,224},{40,232},{48,240},{56,2... | collective-permute-start | bytes 50696 | tf_op jit(solution)/shard_map/ppermute | solution.py:393
  92.1 4.6 %collective-permute-start.8 = (f32[16,33,128]{2,1,0:T(8,128)S(1)}, f32[16,33,128]{2,1,0:T(8,128)S(1)}, u32[]{:S(2)}, u32[]{:S(2)}) collective-permute-start(f32[16,33,128]{2,1,0:T(8,128)S(1)} %get-tuple-element.201), channel_id=1, source_target_pairs={{0,4},{4,0},{1,5},{5,1},{2,6},{6,2},{3,7},{7,3},{8,12},{12,8},{9,1... | collective-permute-start | bytes 811016 | tf_op jit(solution)/shard_map/ppermute | solution.py:371

commit v5 on v4

--- a/solution.py
+++ b/solution.py
@@ -295,40 +295,48 @@
         copy.wait()
 
 
+def chunk(place):
+    return pl.ds(place * (ROWS + 1), ROWS + 1)
+
+
 def group_total_kernel(spread, total):
-    value = spread[0]
-    for chip in range(1, spread.shape[0]):
-        value = value + spread[chip]
+    value = spread[chunk(0), :]
+    for chip in range(1, spread.shape[0] // (ROWS + 1)):
+        value = value + spread[chunk(chip), :]
     total[...] = value
 
 
 def chip_sums_kernel(backward, top, spread, other, sums):
-    chips = spread.shape[0]
+    chips = spread.shape[0] // (ROWS + 1)
     inside = top[0] == (0 if backward else TOP - 1)
     total = jnp.where(inside, other[...], 0.0)
     for step in range(chips):
         chip = chips - 1 - step if backward else step
-        sums[chip] = total
+        sums[chunk(chip), :] = total
         if step < chips - 1:
-            total = total + spread[chip]
-
-
-def halves_of(chips, top):
-    size = chips // 2
+            total = total + spread[chunk(chip), :]
+
+
+def pair_kernel(top, mine, extra, pair):
+    size = mine.shape[0] // 2
     for half in range(2):
-        yield pl.ds(half * size, size), pl.ds(lax.rem(half + top[0], 2) * size, size)
-
-
-def pair_kernel(top, mine, extra, pair):
-    for here, there in halves_of(pair.shape[0], top):
-        pair[here] = mine[there] + extra[there]
+        first = lax.rem(half + top[0], 2) * size
+        for place in range(size):
+            value = mine[first + place] + extra[first + place]
+            pair[chunk(half * size + place), :] = value
 
 
 def finish_kernel(backward, core, top, kept, mine, extra, own, send):
+    size = mine.shape[0] // 2
     later = core[0] == (0 if backward else 1)
-    for here, there in halves_of(own.shape[0], top):
-        own[here] = kept[there] + jnp.where(later, extra[here], 0.0)
-        send[here] = kept[there] + jnp.where(later, 0.0, mine[here])
+    for half in range(2):
+        first = pl.multiple_of(lax.rem(half + top[0], 2) * (size * (ROWS + 1)), 8)
+        block = kept[pl.ds(first, size * (ROWS + 1)), :]
+        for place in range(size):
+            here = half * size + place
+            value = block[place * (ROWS + 1) : (place + 1) * (ROWS + 1)]
+            own[here] = value + jnp.where(later, extra[here], 0.0)
+            send[here] = value + jnp.where(later, 0.0, mine[here])
 
 
 def shaped(shape, dtype):
@@ -380,23 +388,29 @@
     return lax.optimization_barrier((first, later))
 
 
+def exchange(flat, chips):
+    chunks = flat.reshape(chips, 1, flat.size // chips)
+    return lax.all_to_all(chunks, "chip", 0, 0).reshape(flat.shape)
+
+
 def scan_chips(mine, extra, core, top, backward, inside=None, operands=()):
     wire = shaped(mine.shape, f32)
-    pair = call(pair_kernel, "pair", wire, mine, extra, scalars=(top,))
-    spread = lax.all_to_all(pair, "chip", 0, 0)
-    total = call(group_total_kernel, "group_total", shaped(spread.shape[1:], f32), spread)
+    chips, rows, lanes = mine.shape
+    flat = shaped((chips * rows, lanes), f32)
+    pair = call(pair_kernel, "pair", flat, mine, extra, scalars=(top,))
+    spread = exchange(pair, chips)
+    total = call(group_total_kernel, "group_total", shaped((rows, lanes), f32), spread)
     done = ()
     if inside is not None:
         total, operands = after(total, *operands)
-    chips = spread.shape[0]
     facing = [(chip, chips + (chip + chips // 2) % chips) for chip in range(chips)]
     other = lax.ppermute(total, ("top", "chip"), facing + [(b, a) for a, b in facing])
     if inside is not None:
         done = inside(*operands)
     other, spread, done = lax.optimization_barrier((other, spread, done))
     kernel = functools.partial(chip_sums_kernel, backward)
-    sums = call(kernel, "chip_sums", wire, spread, other, scalars=(top,))
-    kept = lax.all_to_all(sums, "chip", 0, 0)
+    sums = call(kernel, "chip_sums", flat, spread, other, scalars=(top,))
+    kept = exchange(sums, chips)
     kernel = functools.partial(finish_kernel, backward)
     own, send = call(kernel, "finish", (wire, wire), kept, mine, extra, scalars=(core, top))
     own, (send,) = after(own, send)

time: 98.2 us -> 93.4 us (0.951)
  blocking collectives: 59.2 us -> 54.6 us
    all_to_all x4, blocking collectives: 59.2 us -> 54.6 us  [exchange(): return lax.all_to_all(chunks, 'chip', 0, 0).reshape(flat.shape)]
where the time goes in v5:
time: 93.4 us; the launch traced here: 93.1 us
  blocking collectives  54.6 us (58%)
  starting transfers between devices  21.4 us (23%)
  Pallas kernels  10.1 us (11%)
  waiting for transfers between devices  5.06 us (5%)
  local copies, waits for them, and re-layouts  1.11 us (1%)
  between operations  0.96 us (1%)
    all_to_all x4, blocking collectives, exchange(): return lax.all_to_all(chunks, 'chip', 0, 0).reshape(flat.shape)  54.6 us
    ppermute x4, starting transfers between devices, swap(): return lax.ppermute(array, axis, [(0, 1), (1, 0)])  13.4 us
    pallas_call x22, Pallas kernels, call(): pl.pallas_call(kernel, out_shape=out_shape, in_specs=in_specs, out_specs=...  10.1 us
    ppermute x3, starting transfers between devices, shifted(): lax.ppermute(array, axis, [(i, (i + step) % size) for i in range(size)])  4.4 us
    ppermute x2, starting transfers between devices, scan_chips(): lax.ppermute(total, ('top', 'chip'), facing + [(b, a) for a, b in facing])  3.55 us
    ppermute x3, waiting for transfers between devices, shifted(): lax.ppermute(array, axis, [(i, (i + step) % size) for i in range(size)])  2.36 us
  transfers between devices with their start and end apart: 9, of which 7 were waited for; matrix products, arithmetic and copies ran while one was open for 0% of the time, Pallas kernels for 7%

profile of v5, /device:TPU:1, one launch (start us, length us, event | category | flops | bytes accessed | tf_op | source)
XLA Modules:
  0.0 93.1 jit_solution(2896366223878822158)
XLA Ops:
  0.6 0.0 copy-start
  0.6 0.0 copy-start.2
  0.7 1.1 %copy-done.2 = bf16[256,1024]{1,0:T(8,128)(2,1)S(1)} copy-done((bf16[256,1024]{1,0:T(8,128)(2,1)S(1)}, bf16[256,1024]{1,0:T(8,128)(2,1)}, u32[]{:S(2)}) %copy-start.2) | copy-done | bytes 524312
  1.7 0.3 key_features.1
  2.0 0.0 copy-done
  2.0 0.3 states_other.1
  2.3 3.3 %collective-permute-start = (f32[16,33,128]{2,1,0:T(8,128)S(1)}, f32[16,33,128]{2,1,0:T(8,128)S(1)}, u32[]{:S(2)}, u32[]{:S(2)}) collective-permute-start(f32[16,33,128]{2,1,0:T(8,128)S(1)} %states_other.1), channel_id=1, source_target_pairs={{0,4},{4,0},{1,5},{5,1},{2,6},{6,2},{3,7},{7,3},{8,12},{12,8},{9,1... | collective-permute-start | bytes 811016 | tf_op jit(solution)/shard_map/ppermute | solution.py:379
  5.7 0.3 states_own.1.mine
  6.0 1.0 %collective-permute-done.extra = f32[16,33,128]{2,1,0:T(8,128)S(1)} collective-permute-done((f32[16,33,128]{2,1,0:T(8,128)S(1)}, f32[16,33,128]{2,1,0:T(8,128)S(1)}, u32[]{:S(2)}, u32[]{:S(2)}) %collective-permute-start) | collective-permute-done | bytes 270368 | tf_op jit(solution)/shard_map/ppermute | solution.py:379
  6.9 0.0 copy-start.3
  7.0 0.0 copy-start.1
  7.0 16.6 %all_to_all.20 = f32[16,1,4224]{2,1,0:T(1,128)S(1)} all-to-all(f32[16,1,4224]{2,1,0:T(1,128)S(1)} %bitcast.17), channel_id=1, replica_groups=mesh['top'=2,'chip'=16,'core'=2,'head'=4] {'chip'}, dimensions={0} | all-to-all | bytes 540672 | tf_op jit(solution)/shard_map/all_to_all | solution.py:393
  23.6 1.6 %collective-permute-start.1 = (f32[33,128]{1,0:T(8,128)S(1)}, f32[33,128]{1,0:T(8,128)S(1)}, u32[]{:S(2)}, u32[]{:S(2)}) collective-permute-start(f32[33,128]{1,0:T(8,128)S(1)} %group_total.2), channel_id=1, source_target_pairs={{0,192},{8,200},{16,208},{24,216},{32,224},{40,232},{48,240},{56,2... | collective-permute-start | bytes 50696 | tf_op jit(solution)/shard_map/ppermute | solution.py:407
  25.1 0.0 copy-done.3
  25.1 0.0 copy-done.4
  25.1 0.0 copy-done.1
  25.1 0.0 copy-done.5
  25.1 0.5 prepare.1
  25.7 0.7 inside_forward_own.1
  26.4 1.1 %collective-permute-done.1.other = f32[33,128]{1,0:T(8,128)S(1)} collective-permute-done((f32[33,128]{1,0:T(8,128)S(1)}, f32[33,128]{1,0:T(8,128)S(1)}, u32[]{:S(2)}, u32[]{:S(2)}) %collective-permute-start.1) | collective-permute-done | bytes 16928 | tf_op jit(solution)/shard_map/ppermute | solution.py:407
  27.5 12.0 %all_to_all.21 = f32[16,1,4224]{2,1,0:T(1,128)S(1)} all-to-all(f32[16,1,4224]{2,1,0:T(1,128)S(1)} %bitcast.15), channel_id=1, replica_groups=mesh['top'=2,'chip'=16,'core'=2,'head'=4] {'chip'}, dimensions={0} | all-to-all | bytes 540672 | tf_op jit(solution)/shard_map/all_to_all | solution.py:393
  39.6 0.1 finish.2
  39.7 4.5 %collective-permute-start.2 = (f32[16,33,128]{2,1,0:T(8,128)S(1)}, f32[16,33,128]{2,1,0:T(8,128)S(1)}, u32[]{:S(2)}, u32[]{:S(2)}) collective-permute-start(f32[16,33,128]{2,1,0:T(8,128)S(1)} %get-tuple-element.137), channel_id=1, source_target_pairs={{0,4},{4,0},{1,5},{5,1},{2,6},{6,2},{3,7},{7,3},{8,12},{12,8},{9,1... | collective-permute-start | bytes 811016 | tf_op jit(solution)/shard_map/ppermute | solution.py:379
  44.2 0.7 inside_forward_other.1
  44.9 0.4 attention_own.1
  45.2 0.2 collective-permute-done.2.wire.refs_13_
  45.5 0.5 attention_other.1
  46.0 2.8 %collective-permute-start.5 = (f32[8,256]{1,0:T(8,128)S(1)}, f32[8,256]{1,0:T(8,128)S(1)}, u32[]{:S(2)}, u32[]{:S(2)}) collective-permute-start(f32[8,256]{1,0:T(8,128)S(1)} %get-tuple-element.148.rest_0_), channel_id=1, source_target_pairs={{0,3},{1,0},{2,1},{3,2},{4,7},{5,4},{6,5},{7,6},{8,11},{9,8},{10,9... | collective-permute-start | bytes 24584 | tf_op jit(solution)/shard_map/ppermute | solution.py:384
  48.7 0.0 collective-permute-start.4
  48.8 1.6 %collective-permute-start.3 = (f32[8,256]{1,0:T(8,128)S(1)}, f32[8,256]{1,0:T(8,128)S(1)}, u32[]{:S(2)}, u32[]{:S(2)}) collective-permute-start(f32[8,256]{1,0:T(8,128)S(1)} %get-tuple-element.148.rest_0_), channel_id=1, source_target_pairs={{0,2},{1,3},{2,0},{3,1},{4,6},{5,7},{6,4},{7,5},{8,10},{9,11},{10,... | collective-permute-start | bytes 24584 | tf_op jit(solution)/shard_map/ppermute | solution.py:384
  50.4 0.0 collective-permute-done.5.rest_3_
  50.4 2.1 %collective-permute-done.4.rest_2_ = f32[8,256]{1,0:T(8,128)S(1)} collective-permute-done((f32[8,256]{1,0:T(8,128)S(1)}, f32[8,256]{1,0:T(8,128)S(1)}, u32[]{:S(2)}, u32[]{:S(2)}) %collective-permute-start.4) | collective-permute-done | bytes 8224 | tf_op jit(solution)/shard_map/ppermute | solution.py:384
  52.5 0.3 collective-permute-done.3.rest_1_
  52.8 0.6 gradient_other.1
  53.4 1.9 %collective-permute-start.6 = (f32[16,33,128]{2,1,0:T(8,128)S(1)}, f32[16,33,128]{2,1,0:T(8,128)S(1)}, u32[]{:S(2)}, u32[]{:S(2)}) collective-permute-start(f32[16,33,128]{2,1,0:T(8,128)S(1)} %get-tuple-element.152), channel_id=1, source_target_pairs={{0,4},{4,0},{1,5},{5,1},{2,6},{6,2},{3,7},{7,3},{8,12},{12,8},{9,1... | collective-permute-start | bytes 811016 | tf_op jit(solution)/shard_map/ppermute | solution.py:379
  55.3 0.5 gradient_own.1
  55.8 0.5 early_backward.1
  56.3 0.3 collective-permute-done.6.extra
  56.6 12.9 %all_to_all.22 = f32[16,1,4224]{2,1,0:T(1,128)S(1)} all-to-all(f32[16,1,4224]{2,1,0:T(1,128)S(1)} %bitcast.18), channel_id=1, replica_groups=mesh['top'=2,'chip'=16,'core'=2,'head'=4] {'chip'}, dimensions={0} | all-to-all | bytes 540672 | tf_op jit(solution)/shard_map/all_to_all | solution.py:393
  69.5 2.0 %collective-permute-start.7 = (f32[33,128]{1,0:T(8,128)S(1)}, f32[33,128]{1,0:T(8,128)S(1)}, u32[]{:S(2)}, u32[]{:S(2)}) collective-permute-start(f32[33,128]{1,0:T(8,128)S(1)} %group_total.3), channel_id=1, source_target_pairs={{0,192},{8,200},{16,208},{24,216},{32,224},{40,232},{48,240},{56,2... | collective-permute-start | bytes 50696 | tf_op jit(solution)/shard_map/ppermute | solution.py:407
  71.5 2.2 %inside_backward.1 = (bf16[256,1024]{1,0:T(8,128)(2,1)}, bf16[256,1024]{1,0:T(8,128)(2,1)}, f32[256,512]{1,0:T(8,128)S(1)}, f32[256,512]{1,0:T(8,128)S(1)}) custom-call(s32[1]{0:T(128)} %bitcast.core, bf16[256,1024]{1,0:T(8,128)(2,1)S(1)} %copy-done, f32[1,1024]{1,0:T(1,128)S(1)} %bitcast.22, f32[256,128]{1,0:T(8,128)S(1)} %get-tuple-element.175.rest_0_.scale_in, ...), custom_call_target="tpu_custom_call" | custom-call | flops 603979776 | bytes 8540160 | tf_op jit(solution)/shard_map/inside_backward/pallas_call | solution.py:365
  73.7 0.0 collective-permute-done.7.other
  73.7 13.1 %all_to_all.23 = f32[16,1,4224]{2,1,0:T(1,128)S(1)} all-to-all(f32[16,1,4224]{2,1,0:T(1,128)S(1)} %bitcast.16), channel_id=1, replica_groups=mesh['top'=2,'chip'=16,'core'=2,'head'=4] {'chip'}, dimensions={0} | all-to-all | bytes 540672 | tf_op jit(solution)/shard_map/all_to_all | solution.py:393
  86.8 0.1 finish.3
  86.9 3.7 %collective-permute-start.8 = (f32[16,33,128]{2,1,0:T(8,128)S(1)}, f32[16,33,128]{2,1,0:T(8,128)S(1)}, u32[]{:S(2)}, u32[]{:S(2)}) collective-permute-start(f32[16,33,128]{2,1,0:T(8,128)S(1)} %get-tuple-element.201), channel_id=1, source_target_pairs={{0,4},{4,0},{1,5},{5,1},{2,6},{6,2},{3,7},{7,3},{8,12},{12,8},{9,1... | collective-permute-start | bytes 811016 | tf_op jit(solution)/shard_map/ppermute | solution.py:379
  90.6 1.2 %outside_backward_own.1 = (bf16[256,1024]{1,0:T(8,128)(2,1)}, bf16[256,1024]{1,0:T(8,128)(2,1)}) custom-call(s32[1]{0:T(128)} %bitcast.core, f32[256,512]{1,0:T(8,128)S(1)} %get-tuple-element.202.key_slope, bf16[256,1024]{1,0:T(8,128)(2,1)S(1)} %copy-done, bf16[256,512]{1,0:T(8,128)(2,1)S(1)} %get-tuple-element.177.key_feat.refs_1_, ...), custom_call_target="tpu_custom_call" | custom-call | flops 134217728 | bytes 3678208 | tf_op jit(solution)/shard_map/outside_backward_own/pallas_call | solution.py:365
  91.7 0.1 collective-permute-done.8.wire
  91.8 1.1 %outside_backward_other.1 = (bf16[256,1024]{1,0:T(8,128)(2,1)}, bf16[256,1024]{1,0:T(8,128)(2,1)}) custom-call(s32[1]{0:T(128)} %bitcast.core, f32[256,512]{1,0:T(8,128)S(1)} %get-tuple-element.196.key_slope, bf16[256,1024]{1,0:T(8,128)(2,1)S(1)} %copy-done, ...), custom_call_target="tpu_custom_call", output_to_operand_aliasing={{0}: (7, {}), {1}: (8, {})} | custom-call | flops 134217728 | bytes 4726784 | tf_op jit(solution)/shard_map/outside_backward_other/pallas_call | solution.py:365
  (8 shorter events, 0.2 us)
Async XLA Ops:
  0.6 1.4 %copy-start = (bf16[256,1024]{1,0:T(8,128)(2,1)S(1)}, bf16[256,1024]{1,0:T(8,128)(2,1)}, u32[]{:S(2)}) copy-start(bf16[256,1024]{1,0:T(8,128)(2,1)} %values.11) | copy-start | bytes 1572868
  0.6 1.1 %copy-start.2 = (bf16[256,1024]{1,0:T(8,128)(2,1)S(1)}, bf16[256,1024]{1,0:T(8,128)(2,1)}, u32[]{:S(2)}) copy-start(bf16[256,1024]{1,0:T(8,128)(2,1)} %keys.2) | copy-start | bytes 1572868
  2.3 4.6 %collective-permute-start = (f32[16,33,128]{2,1,0:T(8,128)S(1)}, f32[16,33,128]{2,1,0:T(8,128)S(1)}, u32[]{:S(2)}, u32[]{:S(2)}) collective-permute-start(f32[16,33,128]{2,1,0:T(8,128)S(1)} %states_other.1), channel_id=1, source_target_pairs={{0,4},{4,0},{1,5},{5,1},{2,6},{6,2},{3,7},{7,3},{8,12},{12,8},{9,1... | collective-permute-start | bytes 811016 | tf_op jit(solution)/shard_map/ppermute | solution.py:379
  6.9 18.2 %copy-start.3 = (bf16[256,1024]{1,0:T(8,128)(2,1)S(1)}, bf16[256,1024]{1,0:T(8,128)(2,1)}, u32[]{:S(2)}) copy-start(bf16[256,1024]{1,0:T(8,128)(2,1)} %keys.2) | copy-start | bytes 1572868
  6.9 18.2 %copy-start.4 = (bf16[256,1024]{1,0:T(8,128)(2,1)S(1)}, bf16[256,1024]{1,0:T(8,128)(2,1)}, u32[]{:S(2)}) copy-start(bf16[256,1024]{1,0:T(8,128)(2,1)} %out_grad) | copy-start | bytes 1572868
  7.0 18.2 %copy-start.1 = (bf16[256,1024]{1,0:T(8,128)(2,1)S(1)}, bf16[256,1024]{1,0:T(8,128)(2,1)}, u32[]{:S(2)}) copy-start(bf16[256,1024]{1,0:T(8,128)(2,1)} %queries.3) | copy-start | bytes 1572868
  23.5 1.6 %copy-start.5 = (f32[1024]{0:T(1024)S(1)}, f32[1024]{0:T(1024)}, u32[]{:S(2)}) copy-start(f32[1024]{0:T(1024)} %param.8) | copy-start | bytes 12292
  23.6 3.9 %collective-permute-start.1 = (f32[33,128]{1,0:T(8,128)S(1)}, f32[33,128]{1,0:T(8,128)S(1)}, u32[]{:S(2)}, u32[]{:S(2)}) collective-permute-start(f32[33,128]{1,0:T(8,128)S(1)} %group_total.2), channel_id=1, source_target_pairs={{0,192},{8,200},{16,208},{24,216},{32,224},{40,232},{48,240},{56,2... | collective-permute-start | bytes 50696 | tf_op jit(solution)/shard_map/ppermute | solution.py:407
  39.7 5.8 %collective-permute-start.2 = (f32[16,33,128]{2,1,0:T(8,128)S(1)}, f32[16,33,128]{2,1,0:T(8,128)S(1)}, u32[]{:S(2)}, u32[]{:S(2)}) collective-permute-start(f32[16,33,128]{2,1,0:T(8,128)S(1)} %get-tuple-element.137), channel_id=1, source_target_pairs={{0,4},{4,0},{1,5},{5,1},{2,6},{6,2},{3,7},{7,3},{8,12},{12,8},{9,1... | collective-permute-start | bytes 811016 | tf_op jit(solution)/shard_map/ppermute | solution.py:379
  46.0 4.4 %collective-permute-start.5 = (f32[8,256]{1,0:T(8,128)S(1)}, f32[8,256]{1,0:T(8,128)S(1)}, u32[]{:S(2)}, u32[]{:S(2)}) collective-permute-start(f32[8,256]{1,0:T(8,128)S(1)} %get-tuple-element.148.rest_0_), channel_id=1, source_target_pairs={{0,3},{1,0},{2,1},{3,2},{4,7},{5,4},{6,5},{7,6},{8,11},{9,8},{10,9... | collective-permute-start | bytes 24584 | tf_op jit(solution)/shard_map/ppermute | solution.py:384
  48.7 3.7 %collective-permute-start.4 = (f32[8,256]{1,0:T(8,128)S(1)}, f32[8,256]{1,0:T(8,128)S(1)}, u32[]{:S(2)}, u32[]{:S(2)}) collective-permute-start(f32[8,256]{1,0:T(8,128)S(1)} %get-tuple-element.148.rest_0_), channel_id=1, source_target_pairs={{0,1},{1,2},{2,3},{3,0},{4,5},{5,6},{6,7},{7,4},{8,9},{9,10},{10,1... | collective-permute-start | bytes 24584 | tf_op jit(solution)/shard_map/ppermute | solution.py:384
  48.8 4.0 %collective-permute-start.3 = (f32[8,256]{1,0:T(8,128)S(1)}, f32[8,256]{1,0:T(8,128)S(1)}, u32[]{:S(2)}, u32[]{:S(2)}) collective-permute-start(f32[8,256]{1,0:T(8,128)S(1)} %get-tuple-element.148.rest_0_), channel_id=1, source_target_pairs={{0,2},{1,3},{2,0},{3,1},{4,6},{5,7},{6,4},{7,5},{8,10},{9,11},{10,... | collective-permute-start | bytes 24584 | tf_op jit(solution)/shard_map/ppermute | solution.py:384
  53.4 3.1 %collective-permute-start.6 = (f32[16,33,128]{2,1,0:T(8,128)S(1)}, f32[16,33,128]{2,1,0:T(8,128)S(1)}, u32[]{:S(2)}, u32[]{:S(2)}) collective-permute-start(f32[16,33,128]{2,1,0:T(8,128)S(1)} %get-tuple-element.152), channel_id=1, source_target_pairs={{0,4},{4,0},{1,5},{5,1},{2,6},{6,2},{3,7},{7,3},{8,12},{12,8},{9,1... | collective-permute-start | bytes 811016 | tf_op jit(solution)/shard_map/ppermute | solution.py:379
  69.5 4.2 %collective-permute-start.7 = (f32[33,128]{1,0:T(8,128)S(1)}, f32[33,128]{1,0:T(8,128)S(1)}, u32[]{:S(2)}, u32[]{:S(2)}) collective-permute-start(f32[33,128]{1,0:T(8,128)S(1)} %group_total.3), channel_id=1, source_target_pairs={{0,192},{8,200},{16,208},{24,216},{32,224},{40,232},{48,240},{56,2... | collective-permute-start | bytes 50696 | tf_op jit(solution)/shard_map/ppermute | solution.py:407
  86.9 4.9 %collective-permute-start.8 = (f32[16,33,128]{2,1,0:T(8,128)S(1)}, f32[16,33,128]{2,1,0:T(8,128)S(1)}, u32[]{:S(2)}, u32[]{:S(2)}) collective-permute-start(f32[16,33,128]{2,1,0:T(8,128)S(1)} %get-tuple-element.201), channel_id=1, source_target_pairs={{0,4},{4,0},{1,5},{5,1},{2,6},{6,2},{3,7},{7,3},{8,12},{12,8},{9,1... | collective-permute-start | bytes 811016 | tf_op jit(solution)/shard_map/ppermute | solution.py:379

commit v6 on v5

--- a/solution.py
+++ b/solution.py
@@ -61,20 +61,20 @@
     return pl.ds(place * size, size)
 
 
+def chunk(place, first=0, size=ROWS + 1):
+    return pl.ds(place * (ROWS + 1) + first, size)
+
+
 def put_state(wire, place, state, row):
-    first = place * BLOCKS
-    wire[first : first + BLOCKS, 0:ROWS, :] = state.reshape(BLOCKS, ROWS, HEAD_DIM)
-    wire[first : first + 1, ROWS : ROWS + 1, :] = row.reshape(1, 1, HEAD_DIM)
-
-
-def clear_rows(wire):
-    wire[:, ROWS : ROWS + 1, :] = jnp.zeros((wire.shape[0], 1, HEAD_DIM), f32)
+    for block in range(BLOCKS):
+        here = place * BLOCKS + block
+        wire[chunk(here, 0, ROWS), :] = state[block * ROWS : (block + 1) * ROWS]
+        wire[chunk(here, ROWS, 1), :] = jnp.zeros_like(row) if block else row
 
 
 def get_state(wire, place):
-    first = place * BLOCKS
-    state = wire[first : first + BLOCKS, 0:ROWS, :]
-    return state.reshape(HEAD_DIM, HEAD_DIM), wire[first, ROWS : ROWS + 1, :]
+    blocks = [wire[chunk(place * BLOCKS + block, 0, ROWS), :] for block in range(BLOCKS)]
+    return jnp.concatenate(blocks, axis=0), wire[chunk(place * BLOCKS, ROWS, 1), :]
 
 
 def send_out(slots, target, slot, here, sem):
@@ -89,20 +89,22 @@
     return rows >= cols
 
 
-def key_features_kernel(core, keys, key_own, key_other):
-    heads_side = keys.shape[1] // HEAD_DIM // CORES
-    for target, own in ((key_other, False), (key_own, True)):
-        for place in range(heads_side):
-            here = head_columns(side_of(core, own), place, heads_side)
-            target[:, columns(place)] = feature(keys[:, here].astype(f32)).astype(bf16)
-
-
-def states_kernel(own, core, key_feat, values, wire):
-    heads_side = key_feat.shape[1] // HEAD_DIM
-    clear_rows(wire)
+def key_features_kernel(core, keys, key_out):
+    heads_side = key_out.shape[1] // HEAD_DIM
+    for place in range(heads_side):
+        here = head_columns(side_of(core, False), place, heads_side)
+        key_out[:, columns(place)] = feature(keys[:, here].astype(f32)).astype(bf16)
+
+
+def states_kernel(own, core, keys, values, wire, *key_out):
+    heads_side = keys.shape[1] // HEAD_DIM // (CORES if own else 1)
     for place in range(heads_side):
         here = head_columns(side_of(core, own), place, heads_side)
-        key = key_feat[:, columns(place)]
+        if own:
+            key = feature(keys[:, here].astype(f32)).astype(bf16)
+            key_out[0][:, columns(place)] = key
+        else:
+            key = keys[:, columns(place)]
         row = jnp.sum(key.astype(f32), axis=0, keepdims=True)
         put_state(wire, place, dot(values[:, here], key, 0, 0), row)
 
@@ -200,7 +202,6 @@
         scale, slope = token_scales(total, HEADS * HEAD_DIM)
         scale_out[...] = scale
         slope_out[...] = slope
-    clear_rows(wire)
     for place in range(heads_side):
         there = columns(place)
         attn = attn_in[:, there]
@@ -295,10 +296,6 @@
         copy.wait()
 
 
-def chunk(place):
-    return pl.ds(place * (ROWS + 1), ROWS + 1)
-
-
 def group_total_kernel(spread, total):
     value = spread[chunk(0), :]
     for chip in range(1, spread.shape[0] // (ROWS + 1)):
@@ -317,26 +314,23 @@
             total = total + spread[chunk(chip), :]
 
 
+def halves_of(rows, top):
+    size = rows // 2
+    for half in range(2):
+        there = pl.multiple_of(lax.rem(half + top[0], 2) * size, 8)
+        yield pl.ds(half * size, size), pl.ds(there, size)
+
+
 def pair_kernel(top, mine, extra, pair):
-    size = mine.shape[0] // 2
-    for half in range(2):
-        first = lax.rem(half + top[0], 2) * size
-        for place in range(size):
-            value = mine[first + place] + extra[first + place]
-            pair[chunk(half * size + place), :] = value
+    for here, there in halves_of(pair.shape[0], top):
+        pair[here, :] = mine[there, :] + extra[there, :]
 
 
 def finish_kernel(backward, core, top, kept, mine, extra, own, send):
-    size = mine.shape[0] // 2
     later = core[0] == (0 if backward else 1)
-    for half in range(2):
-        first = pl.multiple_of(lax.rem(half + top[0], 2) * (size * (ROWS + 1)), 8)
-        block = kept[pl.ds(first, size * (ROWS + 1)), :]
-        for place in range(size):
-            here = half * size + place
-            value = block[place * (ROWS + 1) : (place + 1) * (ROWS + 1)]
-            own[here] = value + jnp.where(later, extra[here], 0.0)
-            send[here] = value + jnp.where(later, 0.0, mine[here])
+    for here, there in halves_of(own.shape[0], top):
+        own[here, :] = kept[there, :] + jnp.where(later, extra[here, :], 0.0)
+        send[here, :] = kept[there, :] + jnp.where(later, 0.0, mine[here, :])
 
 
 def shaped(shape, dtype):
@@ -379,9 +373,9 @@
     return lax.ppermute(array, axis, [(0, 1), (1, 0)])
 
 
-def shifted(array, axis, step):
-    size = lax.axis_size(axis)
-    return lax.ppermute(array, axis, [(i, (i + step) % size) for i in range(size)])
+def swap_pairs(array, axis, order):
+    pairs = [(a, b) for a, b in zip(order[::2], order[1::2])]
+    return lax.ppermute(array, axis, pairs + [(b, a) for a, b in pairs])
 
 
 def after(first, *later):
@@ -395,11 +389,10 @@
 
 def scan_chips(mine, extra, core, top, backward, inside=None, operands=()):
     wire = shaped(mine.shape, f32)
-    chips, rows, lanes = mine.shape
-    flat = shaped((chips * rows, lanes), f32)
-    pair = call(pair_kernel, "pair", flat, mine, extra, scalars=(top,))
+    chips = lax.axis_size("chip")
+    pair = call(pair_kernel, "pair", wire, mine, extra, scalars=(top,))
     spread = exchange(pair, chips)
-    total = call(group_total_kernel, "group_total", shaped((rows, lanes), f32), spread)
+    total = call(group_total_kernel, "group_total", shaped((ROWS + 1, HEAD_DIM), f32), spread)
     done = ()
     if inside is not None:
         total, operands = after(total, *operands)
@@ -409,7 +402,7 @@
         done = inside(*operands)
     other, spread, done = lax.optimization_barrier((other, spread, done))
     kernel = functools.partial(chip_sums_kernel, backward)
-    sums = call(kernel, "chip_sums", flat, spread, other, scalars=(top,))
+    sums = call(kernel, "chip_sums", wire, spread, other, scalars=(top,))
     kept = exchange(sums, chips)
     kernel = functools.partial(finish_kernel, backward)
     own, send = call(kernel, "finish", (wire, wire), kept, mine, extra, scalars=(core, top))
@@ -425,7 +418,7 @@
     top = lax.axis_index("top").astype(jnp.int32).reshape(1)
     core, top = lax.optimization_barrier((core, top))
     gain = norm_gain.reshape(1, width)
-    wire = shaped((lax.axis_size("chip"), ROWS + 1, HEAD_DIM), f32)
+    wire = shaped((lax.axis_size("chip") * (ROWS + 1), HEAD_DIM), f32)
     narrow = shaped((tokens, width), bf16)
     half_low = shaped((tokens, width // CORES), bf16)
     half = shaped((tokens, width // CORES), f32)
@@ -438,13 +431,15 @@
         kernel = functools.partial(kernel, own)
         return call(kernel, name + ("_own" if own else "_other"), *args, scalars=scalars, **named)
 
-    key_own, key_other = call(
-        key_features_kernel, "key_features", (half_low, half_low), key_rows, scalars=(core,)
+    key_other = call(
+        key_features_kernel, "key_features", half_low, key_rows, scalars=(core,)
     )
     theirs = side_call(states_kernel, "states", False, wire, key_other, value_rows, flops=unit)
-    theirs, (key_own,) = after(theirs, key_own)
+    theirs, (keys, values) = after(theirs, key_rows, value_rows)
     extra = swap(theirs, "core")
-    mine = side_call(states_kernel, "states", True, wire, key_own, value_rows, flops=unit)
+    mine, key_own = side_call(
+        states_kernel, "states", True, (wire, half_low), keys, values, flops=unit
+    )
     halves = (half_low, square, half, half)
     own_kernels = (queries, key_rows, value_rows, key_own, gain, out_grad)
 
@@ -477,7 +472,10 @@
         query_other, numer_other, denom_other, got, grad_other, squares, cross,
         flops=4 * unit, scalars=(),
     )
-    stats_from = [shifted(stats, "head", step) for step in (2, 1, 3)]
+    stats_from = [
+        swap_pairs(stats, "head", order)
+        for order in ((0, 1, 2, 3), (1, 2, 3, 0), (0, 2, 1, 3))
+    ]
     d_numer_other, d_denom_other, theirs, scale, slope = side_call(
         gradient_kernel, "gradient", False, (half, half, wire, lanes, lanes),
         query_other, attn_other, inverse_other, grad_other, stats, *stats_from,

time: 93.4 us -> 92.4 us (0.989)
  transfers between devices with their start and end apart: 9 -> 9, of which waited for: 7 -> 6; matrix products, arithmetic and copies ran while one was open for 0% -> 0% of each run, Pallas kernels for 7% -> 8%
where the time goes in v6:
time: 92.4 us; the launch traced here: 92.2 us
  blocking collectives  54.6 us (59%)
  starting transfers between devices  20.5 us (22%)
  Pallas kernels  9.98 us (11%)
  waiting for transfers between devices  5.21 us (6%)
  local copies, waits for them, and re-layouts  1.11 us (1%)
    all_to_all x4, blocking collectives, exchange(): return lax.all_to_all(chunks, 'chip', 0, 0).reshape(flat.shape)  54.6 us
    ppermute x4, starting transfers between devices, swap(): return lax.ppermute(array, axis, [(0, 1), (1, 0)])  13.4 us
    pallas_call x22, Pallas kernels, call(): pl.pallas_call(kernel, out_shape=out_shape, in_specs=in_specs, out_specs=...  9.98 us
    ppermute x3, starting transfers between devices, swap_pairs(): return lax.ppermute(array, axis, pairs + [(b, a) for a, b in pairs])  3.71 us
    ppermute x2, starting transfers between devices, scan_chips(): lax.ppermute(total, ('top', 'chip'), facing + [(b, a) for a, b in facing])  3.36 us
    ppermute x3, waiting for transfers between devices, swap_pairs(): return lax.ppermute(array, axis, pairs + [(b, a) for a, b in pairs])  2.94 us
  transfers between devices with their start and end apart: 9, of which 6 were waited for; matrix products, arithmetic and copies ran while one was open for 0% of the time, Pallas kernels for 8%

profile of v6, /device:TPU:1, one launch (start us, length us, event | category | flops | bytes accessed | tf_op | source)
XLA Modules:
  0.0 92.2 jit_solution(8297964808507828924)
XLA Ops:
  0.6 0.0 copy-start
  0.6 0.0 copy-start.2
  0.7 1.1 %copy-done.2 = bf16[256,1024]{1,0:T(8,128)(2,1)S(1)} copy-done((bf16[256,1024]{1,0:T(8,128)(2,1)S(1)}, bf16[256,1024]{1,0:T(8,128)(2,1)}, u32[]{:S(2)}) %copy-start.2) | copy-done | bytes 524312
  1.7 0.1 key_features.1.keys.key_feat.refs_8_
  1.9 0.0 copy-done
  1.9 0.3 states_other.1
  2.2 3.3 %collective-permute-start = (f32[528,128]{1,0:T(8,128)S(1)}, f32[528,128]{1,0:T(8,128)S(1)}, u32[]{:S(2)}, u32[]{:S(2)}) collective-permute-start(f32[528,128]{1,0:T(8,128)S(1)} %states_other.1), channel_id=1, source_target_pairs={{0,4},{4,0},{1,5},{5,1},{2,6},{6,2},{3,7},{7,3},{8,12},{12,8},{9,1... | collective-permute-start | bytes 811016 | tf_op jit(solution)/shard_map/ppermute | solution.py:373
  5.5 0.4 states_own.1
  5.9 0.8 collective-permute-done.extra
  6.7 0.0 copy-start.3
  6.7 0.0 copy-start.1
  6.7 16.6 %all_to_all.20 = f32[16,1,4224]{2,1,0:T(1,128)S(1)} all-to-all(f32[16,1,4224]{2,1,0:T(1,128)S(1)} %bitcast.19), channel_id=1, replica_groups=mesh['top'=2,'chip'=16,'core'=2,'head'=4] {'chip'}, dimensions={0} | all-to-all | bytes 540672 | tf_op jit(solution)/shard_map/all_to_all | solution.py:387
  23.3 1.6 %collective-permute-start.1 = (f32[33,128]{1,0:T(8,128)S(1)}, f32[33,128]{1,0:T(8,128)S(1)}, u32[]{:S(2)}, u32[]{:S(2)}) collective-permute-start(f32[33,128]{1,0:T(8,128)S(1)} %group_total.2), channel_id=1, source_target_pairs={{0,192},{8,200},{16,208},{24,216},{32,224},{40,232},{48,240},{56,2... | collective-permute-start | bytes 50696 | tf_op jit(solution)/shard_map/ppermute | solution.py:400
  24.9 0.0 copy-done.3
  24.9 0.0 copy-done.4
  24.9 0.0 copy-done.1
  24.9 0.0 copy-done.5
  24.9 0.5 prepare.1
  25.5 0.7 inside_forward_own.1
  26.1 1.1 %collective-permute-done.1.other = f32[33,128]{1,0:T(8,128)S(1)} collective-permute-done((f32[33,128]{1,0:T(8,128)S(1)}, f32[33,128]{1,0:T(8,128)S(1)}, u32[]{:S(2)}, u32[]{:S(2)}) %collective-permute-start.1) | collective-permute-done | bytes 16928 | tf_op jit(solution)/shard_map/ppermute | solution.py:400
  27.3 12.0 %all_to_all.21 = f32[16,1,4224]{2,1,0:T(1,128)S(1)} all-to-all(f32[16,1,4224]{2,1,0:T(1,128)S(1)} %bitcast.17), channel_id=1, replica_groups=mesh['top'=2,'chip'=16,'core'=2,'head'=4] {'chip'}, dimensions={0} | all-to-all | bytes 540672 | tf_op jit(solution)/shard_map/all_to_all | solution.py:387
  39.4 0.1 finish.2
  39.4 4.5 %collective-permute-start.2 = (f32[528,128]{1,0:T(8,128)S(1)}, f32[528,128]{1,0:T(8,128)S(1)}, u32[]{:S(2)}, u32[]{:S(2)}) collective-permute-start(f32[528,128]{1,0:T(8,128)S(1)} %get-tuple-element.139), channel_id=1, source_target_pairs={{0,4},{4,0},{1,5},{5,1},{2,6},{6,2},{3,7},{7,3},{8,12},{12,8},{9,1... | collective-permute-start | bytes 811016 | tf_op jit(solution)/shard_map/ppermute | solution.py:373
  44.0 0.7 inside_forward_other.1
  44.6 0.4 attention_own.1
  45.0 0.1 collective-permute-done.2.wire.refs_13_
  45.1 0.5 attention_other.1
  45.7 2.9 %collective-permute-start.5 = (f32[8,256]{1,0:T(8,128)S(1)}, f32[8,256]{1,0:T(8,128)S(1)}, u32[]{:S(2)}, u32[]{:S(2)}) collective-permute-start(f32[8,256]{1,0:T(8,128)S(1)} %get-tuple-element.150.rest_0_), channel_id=1, source_target_pairs={{0,2},{1,3},{2,0},{3,1},{4,6},{5,7},{6,4},{7,5},{8,10},{9,11},{10,... | collective-permute-start | bytes 24584 | tf_op jit(solution)/shard_map/ppermute | solution.py:378
  48.6 0.8 collective-permute-start.4
  49.4 0.0 collective-permute-start.3
  49.4 0.3 collective-permute-done.5.rest_3_
  49.7 2.6 %collective-permute-done.4.rest_2_ = f32[8,256]{1,0:T(8,128)S(1)} collective-permute-done((f32[8,256]{1,0:T(8,128)S(1)}, f32[8,256]{1,0:T(8,128)S(1)}, u32[]{:S(2)}, u32[]{:S(2)}) %collective-permute-start.4) | collective-permute-done | bytes 8224 | tf_op jit(solution)/shard_map/ppermute | solution.py:378
  52.3 0.0 collective-permute-done.3.rest_1_
  52.3 0.6 gradient_other.1
  53.0 1.9 %collective-permute-start.6 = (f32[528,128]{1,0:T(8,128)S(1)}, f32[528,128]{1,0:T(8,128)S(1)}, u32[]{:S(2)}, u32[]{:S(2)}) collective-permute-start(f32[528,128]{1,0:T(8,128)S(1)} %get-tuple-element.154), channel_id=1, source_target_pairs={{0,4},{4,0},{1,5},{5,1},{2,6},{6,2},{3,7},{7,3},{8,12},{12,8},{9,1... | collective-permute-start | bytes 811016 | tf_op jit(solution)/shard_map/ppermute | solution.py:373
  54.8 0.5 gradient_own.1
  55.3 0.5 early_backward.1
  55.8 0.2 collective-permute-done.6.extra
  56.1 12.9 %all_to_all.22 = f32[16,1,4224]{2,1,0:T(1,128)S(1)} all-to-all(f32[16,1,4224]{2,1,0:T(1,128)S(1)} %bitcast.20), channel_id=1, replica_groups=mesh['top'=2,'chip'=16,'core'=2,'head'=4] {'chip'}, dimensions={0} | all-to-all | bytes 540672 | tf_op jit(solution)/shard_map/all_to_all | solution.py:387
  69.0 1.8 %collective-permute-start.7 = (f32[33,128]{1,0:T(8,128)S(1)}, f32[33,128]{1,0:T(8,128)S(1)}, u32[]{:S(2)}, u32[]{:S(2)}) collective-permute-start(f32[33,128]{1,0:T(8,128)S(1)} %group_total.3), channel_id=1, source_target_pairs={{0,192},{8,200},{16,208},{24,216},{32,224},{40,232},{48,240},{56,2... | collective-permute-start | bytes 50696 | tf_op jit(solution)/shard_map/ppermute | solution.py:400
  70.8 2.2 %inside_backward.1 = (bf16[256,1024]{1,0:T(8,128)(2,1)}, bf16[256,1024]{1,0:T(8,128)(2,1)}, f32[256,512]{1,0:T(8,128)S(1)}, f32[256,512]{1,0:T(8,128)S(1)}) custom-call(s32[1]{0:T(128)} %bitcast.core, bf16[256,1024]{1,0:T(8,128)(2,1)S(1)} %copy-done, f32[1,1024]{1,0:T(1,128)S(1)} %bitcast.22, f32[256,128]{1,0:T(8,128)S(1)} %get-tuple-element.177.rest_0_.scale_in, ...), custom_call_target="tpu_custom_call" | custom-call | flops 603979776 | bytes 8540160 | tf_op jit(solution)/shard_map/inside_backward/pallas_call | solution.py:359
  73.0 0.0 collective-permute-done.7.other
  73.0 13.1 %all_to_all.23 = f32[16,1,4224]{2,1,0:T(1,128)S(1)} all-to-all(f32[16,1,4224]{2,1,0:T(1,128)S(1)} %bitcast.18), channel_id=1, replica_groups=mesh['top'=2,'chip'=16,'core'=2,'head'=4] {'chip'}, dimensions={0} | all-to-all | bytes 540672 | tf_op jit(solution)/shard_map/all_to_all | solution.py:387
  86.1 0.1 finish.3
  86.2 3.7 %collective-permute-start.8 = (f32[528,128]{1,0:T(8,128)S(1)}, f32[528,128]{1,0:T(8,128)S(1)}, u32[]{:S(2)}, u32[]{:S(2)}) collective-permute-start(f32[528,128]{1,0:T(8,128)S(1)} %get-tuple-element.203), channel_id=1, source_target_pairs={{0,4},{4,0},{1,5},{5,1},{2,6},{6,2},{3,7},{7,3},{8,12},{12,8},{9,1... | collective-permute-start | bytes 811016 | tf_op jit(solution)/shard_map/ppermute | solution.py:373
  89.8 1.2 %outside_backward_own.1 = (bf16[256,1024]{1,0:T(8,128)(2,1)}, bf16[256,1024]{1,0:T(8,128)(2,1)}) custom-call(s32[1]{0:T(128)} %bitcast.core, f32[256,512]{1,0:T(8,128)S(1)} %get-tuple-element.204.key_slope, bf16[256,1024]{1,0:T(8,128)(2,1)S(1)} %copy-done, bf16[256,512]{1,0:T(8,128)(2,1)S(1)} %get-tuple-element.179.key_feat.refs_1_, ...), custom_call_target="tpu_custom_call" | custom-call | flops 134217728 | bytes 3678208 | tf_op jit(solution)/shard_map/outside_backward_own/pallas_call | solution.py:359
  91.0 0.0 collective-permute-done.8.wire
  91.0 1.1 %outside_backward_other.1 = (bf16[256,1024]{1,0:T(8,128)(2,1)}, bf16[256,1024]{1,0:T(8,128)(2,1)}) custom-call(s32[1]{0:T(128)} %bitcast.core, f32[256,512]{1,0:T(8,128)S(1)} %get-tuple-element.198.key_slope, bf16[256,1024]{1,0:T(8,128)(2,1)S(1)} %copy-done, ...), custom_call_target="tpu_custom_call", output_to_operand_aliasing={{0}: (7, {}), {1}: (8, {})} | custom-call | flops 134217728 | bytes 4726784 | tf_op jit(solution)/shard_map/outside_backward_other/pallas_call | solution.py:359
  (8 shorter events, 0.2 us)
Async XLA Ops:
  0.6 1.3 %copy-start = (bf16[256,1024]{1,0:T(8,128)(2,1)S(1)}, bf16[256,1024]{1,0:T(8,128)(2,1)}, u32[]{:S(2)}) copy-start(bf16[256,1024]{1,0:T(8,128)(2,1)} %values.10) | copy-start | bytes 1572868
  0.6 1.1 %copy-start.2 = (bf16[256,1024]{1,0:T(8,128)(2,1)S(1)}, bf16[256,1024]{1,0:T(8,128)(2,1)}, u32[]{:S(2)}) copy-start(bf16[256,1024]{1,0:T(8,128)(2,1)} %keys.3) | copy-start | bytes 1572868
  2.2 4.5 %collective-permute-start = (f32[528,128]{1,0:T(8,128)S(1)}, f32[528,128]{1,0:T(8,128)S(1)}, u32[]{:S(2)}, u32[]{:S(2)}) collective-permute-start(f32[528,128]{1,0:T(8,128)S(1)} %states_other.1), channel_id=1, source_target_pairs={{0,4},{4,0},{1,5},{5,1},{2,6},{6,2},{3,7},{7,3},{8,12},{12,8},{9,1... | collective-permute-start | bytes 811016 | tf_op jit(solution)/shard_map/ppermute | solution.py:373
  6.7 18.2 %copy-start.3 = (bf16[256,1024]{1,0:T(8,128)(2,1)S(1)}, bf16[256,1024]{1,0:T(8,128)(2,1)}, u32[]{:S(2)}) copy-start(bf16[256,1024]{1,0:T(8,128)(2,1)} %keys.3) | copy-start | bytes 1572868
  6.7 18.2 %copy-start.4 = (bf16[256,1024]{1,0:T(8,128)(2,1)S(1)}, bf16[256,1024]{1,0:T(8,128)(2,1)}, u32[]{:S(2)}) copy-start(bf16[256,1024]{1,0:T(8,128)(2,1)} %out_grad) | copy-start | bytes 1572868
  6.7 18.2 %copy-start.1 = (bf16[256,1024]{1,0:T(8,128)(2,1)S(1)}, bf16[256,1024]{1,0:T(8,128)(2,1)}, u32[]{:S(2)}) copy-start(bf16[256,1024]{1,0:T(8,128)(2,1)} %queries.3) | copy-start | bytes 1572868
  23.3 1.6 %copy-start.5 = (f32[1024]{0:T(1024)S(1)}, f32[1024]{0:T(1024)}, u32[]{:S(2)}) copy-start(f32[1024]{0:T(1024)} %param.8) | copy-start | bytes 12292
  23.3 3.9 %collective-permute-start.1 = (f32[33,128]{1,0:T(8,128)S(1)}, f32[33,128]{1,0:T(8,128)S(1)}, u32[]{:S(2)}, u32[]{:S(2)}) collective-permute-start(f32[33,128]{1,0:T(8,128)S(1)} %group_total.2), channel_id=1, source_target_pairs={{0,192},{8,200},{16,208},{24,216},{32,224},{40,232},{48,240},{56,2... | collective-permute-start | bytes 50696 | tf_op jit(solution)/shard_map/ppermute | solution.py:400
  39.4 5.7 %collective-permute-start.2 = (f32[528,128]{1,0:T(8,128)S(1)}, f32[528,128]{1,0:T(8,128)S(1)}, u32[]{:S(2)}, u32[]{:S(2)}) collective-permute-start(f32[528,128]{1,0:T(8,128)S(1)} %get-tuple-element.139), channel_id=1, source_target_pairs={{0,4},{4,0},{1,5},{5,1},{2,6},{6,2},{3,7},{7,3},{8,12},{12,8},{9,1... | collective-permute-start | bytes 811016 | tf_op jit(solution)/shard_map/ppermute | solution.py:373
  45.7 4.0 %collective-permute-start.5 = (f32[8,256]{1,0:T(8,128)S(1)}, f32[8,256]{1,0:T(8,128)S(1)}, u32[]{:S(2)}, u32[]{:S(2)}) collective-permute-start(f32[8,256]{1,0:T(8,128)S(1)} %get-tuple-element.150.rest_0_), channel_id=1, source_target_pairs={{0,2},{1,3},{2,0},{3,1},{4,6},{5,7},{6,4},{7,5},{8,10},{9,11},{10,... | collective-permute-start | bytes 24584 | tf_op jit(solution)/shard_map/ppermute | solution.py:378
  48.6 3.7 %collective-permute-start.4 = (f32[8,256]{1,0:T(8,128)S(1)}, f32[8,256]{1,0:T(8,128)S(1)}, u32[]{:S(2)}, u32[]{:S(2)}) collective-permute-start(f32[8,256]{1,0:T(8,128)S(1)} %get-tuple-element.150.rest_0_), channel_id=1, source_target_pairs={{1,2},{3,0},{2,1},{0,3},{5,6},{7,4},{6,5},{4,7},{9,10},{11,8},{10,... | collective-permute-start | bytes 24584 | tf_op jit(solution)/shard_map/ppermute | solution.py:378
  49.4 2.9 %collective-permute-start.3 = (f32[8,256]{1,0:T(8,128)S(1)}, f32[8,256]{1,0:T(8,128)S(1)}, u32[]{:S(2)}, u32[]{:S(2)}) collective-permute-start(f32[8,256]{1,0:T(8,128)S(1)} %get-tuple-element.150.rest_0_), channel_id=1, source_target_pairs={{0,1},{2,3},{1,0},{3,2},{4,5},{6,7},{5,4},{7,6},{8,9},{10,11},{9,8... | collective-permute-start | bytes 24584 | tf_op jit(solution)/shard_map/ppermute | solution.py:378
  53.0 3.1 %collective-permute-start.6 = (f32[528,128]{1,0:T(8,128)S(1)}, f32[528,128]{1,0:T(8,128)S(1)}, u32[]{:S(2)}, u32[]{:S(2)}) collective-permute-start(f32[528,128]{1,0:T(8,128)S(1)} %get-tuple-element.154), channel_id=1, source_target_pairs={{0,4},{4,0},{1,5},{5,1},{2,6},{6,2},{3,7},{7,3},{8,12},{12,8},{9,1... | collective-permute-start | bytes 811016 | tf_op jit(solution)/shard_map/ppermute | solution.py:373
  69.0 4.0 %collective-permute-start.7 = (f32[33,128]{1,0:T(8,128)S(1)}, f32[33,128]{1,0:T(8,128)S(1)}, u32[]{:S(2)}, u32[]{:S(2)}) collective-permute-start(f32[33,128]{1,0:T(8,128)S(1)} %group_total.3), channel_id=1, source_target_pairs={{0,192},{8,200},{16,208},{24,216},{32,224},{40,232},{48,240},{56,2... | collective-permute-start | bytes 50696 | tf_op jit(solution)/shard_map/ppermute | solution.py:400
  86.2 4.8 %collective-permute-start.8 = (f32[528,128]{1,0:T(8,128)S(1)}, f32[528,128]{1,0:T(8,128)S(1)}, u32[]{:S(2)}, u32[]{:S(2)}) collective-permute-start(f32[528,128]{1,0:T(8,128)S(1)} %get-tuple-element.203), channel_id=1, source_target_pairs={{0,4},{4,0},{1,5},{5,1},{2,6},{6,2},{3,7},{7,3},{8,12},{12,8},{9,1... | collective-permute-start | bytes 811016 | tf_op jit(solution)/shard_map/ppermute | solution.py:373

commit v7 on v6

--- a/solution.py
+++ b/solution.py
@@ -14,6 +14,7 @@
 TOP = 2
 ROWS = 32
 BLOCK = 256
+GANG = 2
 BLOCKS = HEAD_DIM // ROWS
 
 f32 = jnp.float32
@@ -77,10 +78,18 @@
     return jnp.concatenate(blocks, axis=0), wire[chunk(place * BLOCKS, ROWS, 1), :]
 
 
-def send_out(slots, target, slot, here, sem):
-    copy = pltpu.make_async_copy(slots.at[slot], target.at[:, here], sem)
+def put_out(slots, target, sems, slot, side, heads_side, value):
+    place = slot % GANG
+    slots[slot // GANG, :, columns(place)] = value
+    if place != GANG - 1:
+        return []
+    first = (side * heads_side + slot % heads_side - place) * HEAD_DIM
+    here = pl.ds(pl.multiple_of(first, HEAD_DIM), GANG * HEAD_DIM)
+    copy = pltpu.make_async_copy(
+        slots.at[slot // GANG], target.at[:, here], sems.at[slot // GANG]
+    )
     copy.start()
-    return copy
+    return [copy]
 
 
 def causal(tokens):
@@ -238,12 +247,13 @@
     copies = []
     for half, own in enumerate((True, False)):
         query_feat, key_feat, query_slope, d_numer_in, d_denom_in, attn, wire = halves[half]
+        side = side_of(core, own)
         for place in range(heads_side):
             here = head_columns(side_of(core, own), place, heads_side)
             there = columns(place)
             slot = half * heads_side + place
-            normed_slots[slot] = (gain[:, here] * attn[:, there] * scale).astype(bf16)
-            copies.append(send_out(normed_slots, normed, slot, here, sems.at[0, slot]))
+            out = (gain[:, here] * attn[:, there] * scale).astype(bf16)
+            copies += put_out(normed_slots, normed, sems.at[0], slot, side, heads_side, out)
             state, row = get_state(wire, place)
             state_high, state_low = split(state)
             d_denom = d_denom_in[:, there]
@@ -256,8 +266,8 @@
             right = jnp.concatenate([state_high, state_low, state_high], axis=0)
             grad = dot(left, right, 1, 0) + d_denom * row
             grad = grad + dot(mixed_low, key_feat[:, there], 1, 0)
-            query_slots[slot] = (grad * query_slope[:, there]).astype(bf16)
-            copies.append(send_out(query_slots, query_grad, slot, here, sems.at[1, slot]))
+            out = (grad * query_slope[:, there]).astype(bf16)
+            copies += put_out(query_slots, query_grad, sems.at[1], slot, side, heads_side, out)
     for half in range(CORES):
         query_feat = halves[half][0]
         for place in range(heads_side):
@@ -272,6 +282,7 @@
     own, core, key_slope, values, key_feat, key_part, value_part, wire, *rest
 ):
     key_grad, value_grad, key_slots, value_slots, sems = rest[-5:]
+    side = side_of(core, own)
     heads_side = key_feat.shape[1] // HEAD_DIM
     copies = []
     for place in range(heads_side):
@@ -285,13 +296,13 @@
             jnp.concatenate([value, value], axis=1), jnp.concatenate([high, low], axis=0), 1, 0
         )
         grad = grad + row + key_part[:, there]
-        key_slots[place] = (grad * key_slope[:, there]).astype(bf16)
-        copies.append(send_out(key_slots, key_grad, place, here, sems.at[0, place]))
+        out = (grad * key_slope[:, there]).astype(bf16)
+        copies += put_out(key_slots, key_grad, sems.at[0], place, side, heads_side, out)
         grad = dot(
             jnp.concatenate([key, key], axis=1), jnp.concatenate([high, low], axis=1), 1, 1
         )
-        value_slots[place] = (grad + value_part[:, there]).astype(bf16)
-        copies.append(send_out(value_slots, value_grad, place, here, sems.at[1, place]))
+        out = (grad + value_part[:, there]).astype(bf16)
+        copies += put_out(value_slots, value_grad, sems.at[1], place, side, heads_side, out)
     for copy in copies:
         copy.wait()
 
@@ -352,8 +363,8 @@
     out_specs = spaces(len(jax.tree.leaves(out_shape)), hbm_out)
     scratch_shapes = []
     if slots:
-        scratch_shapes = [pltpu.VMEM((slots, BLOCK, HEAD_DIM), bf16)] * 2
-        scratch_shapes.append(pltpu.SemaphoreType.DMA((2, slots)))
+        scratch_shapes = [pltpu.VMEM((slots // GANG, BLOCK, GANG * HEAD_DIM), bf16)] * 2
+        scratch_shapes.append(pltpu.SemaphoreType.DMA((2, slots // GANG)))
     in_specs = [pl.BlockSpec(memory_space=pltpu.SMEM) for _ in scalars] + in_specs
     operands = scalars + operands
     return pl.pallas_call(
@@ -441,28 +452,28 @@
         states_kernel, "states", True, (wire, half_low), keys, values, flops=unit
     )
     halves = (half_low, square, half, half)
-    own_kernels = (queries, key_rows, value_rows, key_own, gain, out_grad)
-
-    def inside_forward_own(queries, keys, values, key_own, gain, out_grad):
+    own_kernels = (queries, key_rows, value_rows, key_own, key_other, gain, out_grad)
+
+    def inside_forward_both(queries, keys, values, key_own, key_other, gain, out_grad):
         first = side_call(
             inside_forward_kernel, "inside_forward", True, halves, queries, values, key_own,
             flops=4 * unit,
         )
-        return first, call(
+        second = side_call(
+            inside_forward_kernel, "inside_forward", False, halves, queries, values, key_other,
+            flops=4 * unit,
+        )
+        return first, second, call(
             prepare_kernel, "prepare", (half,) * 6, queries, keys, gain, out_grad,
             scalars=(core,), flops=unit,
         )
 
     kept, got, inside = scan_chips(
-        mine, extra, core, top, False, inside_forward_own, own_kernels
-    )
-    (query_own, low_own, numer, denom), prepared = inside
+        mine, extra, core, top, False, inside_forward_both, own_kernels
+    )
+    (query_own, low_own, numer, denom), second, prepared = inside
+    query_other, low_other, numer_other, denom_other = second
     grad_own, query_slope, key_slope, grad_other, query_slope_other, key_slope_other = prepared
-    kept, (key_other,) = after(kept, key_other)
-    query_other, low_other, numer_other, denom_other = side_call(
-        inside_forward_kernel, "inside_forward", False, halves, queries, value_rows, key_other,
-        flops=4 * unit,
-    )
     attn_own, inverse_own, squares, cross = side_call(
         attention_kernel, "attention", True, (half, half, lanes, lanes),
         query_own, numer, denom, kept, grad_own, flops=4 * unit, scalars=(),

time: 92.4 us -> 92.4 us (level)
  transfers between devices with their start and end apart: 9 -> 9, of which waited for: 6 -> 6; matrix products, arithmetic and copies ran while one was open for 0% -> 0% of each run, Pallas kernels for 8% -> 7%
where the time goes in v7:
time: 92.4 us; the launch traced here: 92.1 us
  blocking collectives  55.3 us (60%)
  starting transfers between devices  19.8 us (21%)
  Pallas kernels  9.94 us (11%)
  waiting for transfers between devices  5.17 us (6%)
  local copies, waits for them, and re-layouts  1.12 us (1%)
    all_to_all x4, blocking collectives, exchange(): return lax.all_to_all(chunks, 'chip', 0, 0).reshape(flat.shape)  55.3 us
    ppermute x4, starting transfers between devices, swap(): return lax.ppermute(array, axis, [(0, 1), (1, 0)])  12.7 us
    pallas_call x22, Pallas kernels, call(): pl.pallas_call(kernel, out_shape=out_shape, in_specs=in_specs, out_specs=...  9.94 us
    ppermute x3, starting transfers between devices, swap_pairs(): return lax.ppermute(array, axis, pairs + [(b, a) for a, b in pairs])  3.71 us
    ppermute x2, starting transfers between devices, scan_chips(): lax.ppermute(total, ('top', 'chip'), facing + [(b, a) for a, b in facing])  3.36 us
    ppermute x3, waiting for transfers between devices, swap_pairs(): return lax.ppermute(array, axis, pairs + [(b, a) for a, b in pairs])  2.93 us
  transfers between devices with their start and end apart: 9, of which 6 were waited for; matrix products, arithmetic and copies ran while one was open for 0% of the time, Pallas kernels for 7%

profile of v7, /device:TPU:1, one launch (start us, length us, event | category | flops | bytes accessed | tf_op | source)
XLA Modules:
  0.0 92.1 jit_solution(11930269711426662483)
XLA Ops:
  0.6 0.0 copy-start
  0.6 0.0 copy-start.2
  0.7 1.1 %copy-done.2 = bf16[256,1024]{1,0:T(8,128)(2,1)S(1)} copy-done((bf16[256,1024]{1,0:T(8,128)(2,1)S(1)}, bf16[256,1024]{1,0:T(8,128)(2,1)}, u32[]{:S(2)}) %copy-start.2) | copy-done | bytes 524312
  1.7 0.1 key_features.1.keys.key_feat.refs_8_
  1.9 0.3 states_other.1
  2.2 3.3 %collective-permute-start = (f32[528,128]{1,0:T(8,128)S(1)}, f32[528,128]{1,0:T(8,128)S(1)}, u32[]{:S(2)}, u32[]{:S(2)}) collective-permute-start(f32[528,128]{1,0:T(8,128)S(1)} %states_other.1), channel_id=1, source_target_pairs={{0,4},{4,0},{1,5},{5,1},{2,6},{6,2},{3,7},{7,3},{8,12},{12,8},{9,1... | collective-permute-start | bytes 811016 | tf_op jit(solution)/shard_map/ppermute | solution.py:384
  5.5 0.4 states_own.1
  5.9 0.8 collective-permute-done.extra
  6.7 0.0 copy-start.1
  6.7 16.6 %all_to_all.20 = f32[16,1,4224]{2,1,0:T(1,128)S(1)} all-to-all(f32[16,1,4224]{2,1,0:T(1,128)S(1)} %bitcast.19), channel_id=1, replica_groups=mesh['top'=2,'chip'=16,'core'=2,'head'=4] {'chip'}, dimensions={0} | all-to-all | bytes 540672 | tf_op jit(solution)/shard_map/all_to_all | solution.py:398
  23.3 0.0 copy-start.3
  23.4 0.0 copy-start.4
  23.4 0.0 copy-start.5
  23.4 1.6 %collective-permute-start.1 = (f32[33,128]{1,0:T(8,128)S(1)}, f32[33,128]{1,0:T(8,128)S(1)}, u32[]{:S(2)}, u32[]{:S(2)}) collective-permute-start(f32[33,128]{1,0:T(8,128)S(1)} %group_total.2), channel_id=1, source_target_pairs={{0,192},{8,200},{16,208},{24,216},{32,224},{40,232},{48,240},{56,2... | collective-permute-start | bytes 50696 | tf_op jit(solution)/shard_map/ppermute | solution.py:411
  24.9 0.7 inside_forward_own.1
  25.6 0.0 copy-done.3
  25.6 0.0 copy-done.4
  25.6 0.0 copy-done.5
  25.6 0.5 prepare.1
  26.2 0.7 inside_forward_other.1
  26.9 0.5 collective-permute-done.1.other
  27.3 12.8 %all_to_all.21 = f32[16,1,4224]{2,1,0:T(1,128)S(1)} all-to-all(f32[16,1,4224]{2,1,0:T(1,128)S(1)} %bitcast.17), channel_id=1, replica_groups=mesh['top'=2,'chip'=16,'core'=2,'head'=4] {'chip'}, dimensions={0} | all-to-all | bytes 540672 | tf_op jit(solution)/shard_map/all_to_all | solution.py:398
  40.1 0.1 finish.2
  40.2 3.8 %collective-permute-start.2 = (f32[528,128]{1,0:T(8,128)S(1)}, f32[528,128]{1,0:T(8,128)S(1)}, u32[]{:S(2)}, u32[]{:S(2)}) collective-permute-start(f32[528,128]{1,0:T(8,128)S(1)} %get-tuple-element.145), channel_id=1, source_target_pairs={{0,4},{4,0},{1,5},{5,1},{2,6},{6,2},{3,7},{7,3},{8,12},{12,8},{9,1... | collective-permute-start | bytes 811016 | tf_op jit(solution)/shard_map/ppermute | solution.py:384
  44.0 0.4 attention_own.1
  44.4 0.8 collective-permute-done.2.wire.refs_13_
  45.2 0.5 attention_other.1
  45.7 2.9 %collective-permute-start.5 = (f32[8,256]{1,0:T(8,128)S(1)}, f32[8,256]{1,0:T(8,128)S(1)}, u32[]{:S(2)}, u32[]{:S(2)}) collective-permute-start(f32[8,256]{1,0:T(8,128)S(1)} %get-tuple-element.156.rest_0_), channel_id=1, source_target_pairs={{0,2},{1,3},{2,0},{3,1},{4,6},{5,7},{6,4},{7,5},{8,10},{9,11},{10,... | collective-permute-start | bytes 24584 | tf_op jit(solution)/shard_map/ppermute | solution.py:389
  48.6 0.8 collective-permute-start.4
  49.4 0.0 collective-permute-start.3
  49.4 0.3 collective-permute-done.5.rest_3_
  49.7 2.6 %collective-permute-done.4.rest_2_ = f32[8,256]{1,0:T(8,128)S(1)} collective-permute-done((f32[8,256]{1,0:T(8,128)S(1)}, f32[8,256]{1,0:T(8,128)S(1)}, u32[]{:S(2)}, u32[]{:S(2)}) %collective-permute-start.4) | collective-permute-done | bytes 8224 | tf_op jit(solution)/shard_map/ppermute | solution.py:389
  52.4 0.0 collective-permute-done.3.rest_1_
  52.4 0.6 gradient_other.1
  53.0 1.9 %collective-permute-start.6 = (f32[528,128]{1,0:T(8,128)S(1)}, f32[528,128]{1,0:T(8,128)S(1)}, u32[]{:S(2)}, u32[]{:S(2)}) collective-permute-start(f32[528,128]{1,0:T(8,128)S(1)} %get-tuple-element.160), channel_id=1, source_target_pairs={{0,4},{4,0},{1,5},{5,1},{2,6},{6,2},{3,7},{7,3},{8,12},{12,8},{9,1... | collective-permute-start | bytes 811016 | tf_op jit(solution)/shard_map/ppermute | solution.py:384
  54.9 0.5 gradient_own.1
  55.3 0.5 early_backward.1
  55.8 0.2 collective-permute-done.6.extra
  56.1 12.9 %all_to_all.22 = f32[16,1,4224]{2,1,0:T(1,128)S(1)} all-to-all(f32[16,1,4224]{2,1,0:T(1,128)S(1)} %bitcast.20), channel_id=1, replica_groups=mesh['top'=2,'chip'=16,'core'=2,'head'=4] {'chip'}, dimensions={0} | all-to-all | bytes 540672 | tf_op jit(solution)/shard_map/all_to_all | solution.py:398
  69.0 1.8 %collective-permute-start.7 = (f32[33,128]{1,0:T(8,128)S(1)}, f32[33,128]{1,0:T(8,128)S(1)}, u32[]{:S(2)}, u32[]{:S(2)}) collective-permute-start(f32[33,128]{1,0:T(8,128)S(1)} %group_total.3), channel_id=1, source_target_pairs={{0,192},{8,200},{16,208},{24,216},{32,224},{40,232},{48,240},{56,2... | collective-permute-start | bytes 50696 | tf_op jit(solution)/shard_map/ppermute | solution.py:411
  70.8 2.1 %inside_backward.1 = (bf16[256,1024]{1,0:T(8,128)(2,1)}, bf16[256,1024]{1,0:T(8,128)(2,1)}, f32[256,512]{1,0:T(8,128)S(1)}, f32[256,512]{1,0:T(8,128)S(1)}) custom-call(s32[1]{0:T(128)} %bitcast.core, bf16[256,1024]{1,0:T(8,128)(2,1)S(1)} %copy-done, f32[1,1024]{1,0:T(1,128)S(1)} %bitcast.22, f32[256,128]{1,0:T(8,128)S(1)} %get-tuple-element.183.rest_0_.scale_in, ...), custom_call_target="tpu_custom_call" | custom-call | flops 603979776 | bytes 8540160 | tf_op jit(solution)/shard_map/inside_backward/pallas_call | solution.py:370
  72.9 0.0 collective-permute-done.7.other
  73.0 13.1 %all_to_all.23 = f32[16,1,4224]{2,1,0:T(1,128)S(1)} all-to-all(f32[16,1,4224]{2,1,0:T(1,128)S(1)} %bitcast.18), channel_id=1, replica_groups=mesh['top'=2,'chip'=16,'core'=2,'head'=4] {'chip'}, dimensions={0} | all-to-all | bytes 540672 | tf_op jit(solution)/shard_map/all_to_all | solution.py:398
  86.0 0.1 finish.3
  86.1 3.7 %collective-permute-start.8 = (f32[528,128]{1,0:T(8,128)S(1)}, f32[528,128]{1,0:T(8,128)S(1)}, u32[]{:S(2)}, u32[]{:S(2)}) collective-permute-start(f32[528,128]{1,0:T(8,128)S(1)} %get-tuple-element.209), channel_id=1, source_target_pairs={{0,4},{4,0},{1,5},{5,1},{2,6},{6,2},{3,7},{7,3},{8,12},{12,8},{9,1... | collective-permute-start | bytes 811016 | tf_op jit(solution)/shard_map/ppermute | solution.py:384
  89.8 1.2 %outside_backward_own.1 = (bf16[256,1024]{1,0:T(8,128)(2,1)}, bf16[256,1024]{1,0:T(8,128)(2,1)}) custom-call(s32[1]{0:T(128)} %bitcast.core, f32[256,512]{1,0:T(8,128)S(1)} %get-tuple-element.210.key_slope, bf16[256,1024]{1,0:T(8,128)(2,1)S(1)} %copy-done, bf16[256,512]{1,0:T(8,128)(2,1)S(1)} %get-tuple-element.185.key_feat.refs_1_, ...), custom_call_target="tpu_custom_call" | custom-call | flops 134217728 | bytes 3678208 | tf_op jit(solution)/shard_map/outside_backward_own/pallas_call | solution.py:370
  91.0 0.0 collective-permute-done.8.wire
  91.0 1.2 %outside_backward_other.1 = (bf16[256,1024]{1,0:T(8,128)(2,1)}, bf16[256,1024]{1,0:T(8,128)(2,1)}) custom-call(s32[1]{0:T(128)} %bitcast.core, f32[256,512]{1,0:T(8,128)S(1)} %get-tuple-element.204.key_slope, bf16[256,1024]{1,0:T(8,128)(2,1)S(1)} %copy-done, ...), custom_call_target="tpu_custom_call", output_to_operand_aliasing={{0}: (7, {}), {1}: (8, {})} | custom-call | flops 134217728 | bytes 4726784 | tf_op jit(solution)/shard_map/outside_backward_other/pallas_call | solution.py:370
  (8 shorter events, 0.2 us)
Async XLA Ops:
  0.6 1.3 %copy-start = (bf16[256,1024]{1,0:T(8,128)(2,1)S(1)}, bf16[256,1024]{1,0:T(8,128)(2,1)}, u32[]{:S(2)}) copy-start(bf16[256,1024]{1,0:T(8,128)(2,1)} %values.9) | copy-start | bytes 1572868
  0.6 1.1 %copy-start.2 = (bf16[256,1024]{1,0:T(8,128)(2,1)S(1)}, bf16[256,1024]{1,0:T(8,128)(2,1)}, u32[]{:S(2)}) copy-start(bf16[256,1024]{1,0:T(8,128)(2,1)} %keys.3) | copy-start | bytes 1572868
  2.2 4.5 %collective-permute-start = (f32[528,128]{1,0:T(8,128)S(1)}, f32[528,128]{1,0:T(8,128)S(1)}, u32[]{:S(2)}, u32[]{:S(2)}) collective-permute-start(f32[528,128]{1,0:T(8,128)S(1)} %states_other.1), channel_id=1, source_target_pairs={{0,4},{4,0},{1,5},{5,1},{2,6},{6,2},{3,7},{7,3},{8,12},{12,8},{9,1... | collective-permute-start | bytes 811016 | tf_op jit(solution)/shard_map/ppermute | solution.py:384
  6.7 18.2 %copy-start.1 = (bf16[256,1024]{1,0:T(8,128)(2,1)S(1)}, bf16[256,1024]{1,0:T(8,128)(2,1)}, u32[]{:S(2)}) copy-start(bf16[256,1024]{1,0:T(8,128)(2,1)} %queries.2) | copy-start | bytes 1572868
  23.3 2.3 %copy-start.3 = (bf16[256,1024]{1,0:T(8,128)(2,1)S(1)}, bf16[256,1024]{1,0:T(8,128)(2,1)}, u32[]{:S(2)}) copy-start(bf16[256,1024]{1,0:T(8,128)(2,1)} %keys.3) | copy-start | bytes 1572868
  23.4 2.3 %copy-start.4 = (bf16[256,1024]{1,0:T(8,128)(2,1)S(1)}, bf16[256,1024]{1,0:T(8,128)(2,1)}, u32[]{:S(2)}) copy-start(bf16[256,1024]{1,0:T(8,128)(2,1)} %out_grad) | copy-start | bytes 1572868
  23.4 2.3 %copy-start.5 = (f32[1024]{0:T(1024)S(1)}, f32[1024]{0:T(1024)}, u32[]{:S(2)}) copy-start(f32[1024]{0:T(1024)} %param.8) | copy-start | bytes 12292
  23.4 3.9 %collective-permute-start.1 = (f32[33,128]{1,0:T(8,128)S(1)}, f32[33,128]{1,0:T(8,128)S(1)}, u32[]{:S(2)}, u32[]{:S(2)}) collective-permute-start(f32[33,128]{1,0:T(8,128)S(1)} %group_total.2), channel_id=1, source_target_pairs={{0,192},{8,200},{16,208},{24,216},{32,224},{40,232},{48,240},{56,2... | collective-permute-start | bytes 50696 | tf_op jit(solution)/shard_map/ppermute | solution.py:411
  40.2 5.0 %collective-permute-start.2 = (f32[528,128]{1,0:T(8,128)S(1)}, f32[528,128]{1,0:T(8,128)S(1)}, u32[]{:S(2)}, u32[]{:S(2)}) collective-permute-start(f32[528,128]{1,0:T(8,128)S(1)} %get-tuple-element.145), channel_id=1, source_target_pairs={{0,4},{4,0},{1,5},{5,1},{2,6},{6,2},{3,7},{7,3},{8,12},{12,8},{9,1... | collective-permute-start | bytes 811016 | tf_op jit(solution)/shard_map/ppermute | solution.py:384
  45.7 4.0 %collective-permute-start.5 = (f32[8,256]{1,0:T(8,128)S(1)}, f32[8,256]{1,0:T(8,128)S(1)}, u32[]{:S(2)}, u32[]{:S(2)}) collective-permute-start(f32[8,256]{1,0:T(8,128)S(1)} %get-tuple-element.156.rest_0_), channel_id=1, source_target_pairs={{0,2},{1,3},{2,0},{3,1},{4,6},{5,7},{6,4},{7,5},{8,10},{9,11},{10,... | collective-permute-start | bytes 24584 | tf_op jit(solution)/shard_map/ppermute | solution.py:389
  48.6 3.7 %collective-permute-start.4 = (f32[8,256]{1,0:T(8,128)S(1)}, f32[8,256]{1,0:T(8,128)S(1)}, u32[]{:S(2)}, u32[]{:S(2)}) collective-permute-start(f32[8,256]{1,0:T(8,128)S(1)} %get-tuple-element.156.rest_0_), channel_id=1, source_target_pairs={{1,2},{3,0},{2,1},{0,3},{5,6},{7,4},{6,5},{4,7},{9,10},{11,8},{10,... | collective-permute-start | bytes 24584 | tf_op jit(solution)/shard_map/ppermute | solution.py:389
  49.4 2.9 %collective-permute-start.3 = (f32[8,256]{1,0:T(8,128)S(1)}, f32[8,256]{1,0:T(8,128)S(1)}, u32[]{:S(2)}, u32[]{:S(2)}) collective-permute-start(f32[8,256]{1,0:T(8,128)S(1)} %get-tuple-element.156.rest_0_), channel_id=1, source_target_pairs={{0,1},{2,3},{1,0},{3,2},{4,5},{6,7},{5,4},{7,6},{8,9},{10,11},{9,8... | collective-permute-start | bytes 24584 | tf_op jit(solution)/shard_map/ppermute | solution.py:389
  53.0 3.1 %collective-permute-start.6 = (f32[528,128]{1,0:T(8,128)S(1)}, f32[528,128]{1,0:T(8,128)S(1)}, u32[]{:S(2)}, u32[]{:S(2)}) collective-permute-start(f32[528,128]{1,0:T(8,128)S(1)} %get-tuple-element.160), channel_id=1, source_target_pairs={{0,4},{4,0},{1,5},{5,1},{2,6},{6,2},{3,7},{7,3},{8,12},{12,8},{9,1... | collective-permute-start | bytes 811016 | tf_op jit(solution)/shard_map/ppermute | solution.py:384
  69.0 3.9 %collective-permute-start.7 = (f32[33,128]{1,0:T(8,128)S(1)}, f32[33,128]{1,0:T(8,128)S(1)}, u32[]{:S(2)}, u32[]{:S(2)}) collective-permute-start(f32[33,128]{1,0:T(8,128)S(1)} %group_total.3), channel_id=1, source_target_pairs={{0,192},{8,200},{16,208},{24,216},{32,224},{40,232},{48,240},{56,2... | collective-permute-start | bytes 50696 | tf_op jit(solution)/shard_map/ppermute | solution.py:411
  86.1 4.8 %collective-permute-start.8 = (f32[528,128]{1,0:T(8,128)S(1)}, f32[528,128]{1,0:T(8,128)S(1)}, u32[]{:S(2)}, u32[]{:S(2)}) collective-permute-start(f32[528,128]{1,0:T(8,128)S(1)} %get-tuple-element.209), channel_id=1, source_target_pairs={{0,4},{4,0},{1,5},{5,1},{2,6},{6,2},{3,7},{7,3},{8,12},{12,8},{9,1... | collective-permute-start | bytes 811016 | tf_op jit(solution)/shard_map/ppermute | solution.py:384

commit v8 on v7

--- a/solution.py
+++ b/solution.py
@@ -452,28 +452,28 @@
         states_kernel, "states", True, (wire, half_low), keys, values, flops=unit
     )
     halves = (half_low, square, half, half)
-    own_kernels = (queries, key_rows, value_rows, key_own, key_other, gain, out_grad)
-
-    def inside_forward_both(queries, keys, values, key_own, key_other, gain, out_grad):
+    own_kernels = (queries, key_rows, value_rows, key_own, gain, out_grad)
+
+    def inside_forward_own(queries, keys, values, key_own, gain, out_grad):
         first = side_call(
             inside_forward_kernel, "inside_forward", True, halves, queries, values, key_own,
             flops=4 * unit,
         )
-        second = side_call(
-            inside_forward_kernel, "inside_forward", False, halves, queries, values, key_other,
-            flops=4 * unit,
-        )
-        return first, second, call(
+        return first, call(
             prepare_kernel, "prepare", (half,) * 6, queries, keys, gain, out_grad,
             scalars=(core,), flops=unit,
         )
 
     kept, got, inside = scan_chips(
-        mine, extra, core, top, False, inside_forward_both, own_kernels
-    )
-    (query_own, low_own, numer, denom), second, prepared = inside
-    query_other, low_other, numer_other, denom_other = second
+        mine, extra, core, top, False, inside_forward_own, own_kernels
+    )
+    (query_own, low_own, numer, denom), prepared = inside
     grad_own, query_slope, key_slope, grad_other, query_slope_other, key_slope_other = prepared
+    kept, (key_other,) = after(kept, key_other)
+    query_other, low_other, numer_other, denom_other = side_call(
+        inside_forward_kernel, "inside_forward", False, halves, queries, value_rows, key_other,
+        flops=4 * unit,
+    )
     attn_own, inverse_own, squares, cross = side_call(
         attention_kernel, "attention", True, (half, half, lanes, lanes),
         query_own, numer, denom, kept, grad_own, flops=4 * unit, scalars=(),

time: 92.4 us -> 92.4 us (level)
  no operation moved by 1% of the time
where the time goes in v8:
time: 92.4 us; the launch traced here: 92.1 us
  blocking collectives  54.6 us (59%)
  starting transfers between devices  20.5 us (22%)
  Pallas kernels  9.96 us (11%)
  waiting for transfers between devices  5.2 us (6%)
  local copies, waits for them, and re-layouts  1.11 us (1%)
    all_to_all x4, blocking collectives, exchange(): return lax.all_to_all(chunks, 'chip', 0, 0).reshape(flat.shape)  54.6 us
    ppermute x4, starting transfers between devices, swap(): return lax.ppermute(array, axis, [(0, 1), (1, 0)])  13.4 us
    pallas_call x22, Pallas kernels, call(): pl.pallas_call(kernel, out_shape=out_shape, in_specs=in_specs, out_specs=...  9.96 us
    ppermute x3, starting transfers between devices, swap_pairs(): return lax.ppermute(array, axis, pairs + [(b, a) for a, b in pairs])  3.71 us
    ppermute x2, starting transfers between devices, scan_chips(): lax.ppermute(total, ('top', 'chip'), facing + [(b, a) for a, b in facing])  3.36 us
    ppermute x3, waiting for transfers between devices, swap_pairs(): return lax.ppermute(array, axis, pairs + [(b, a) for a, b in pairs])  2.94 us
  transfers between devices with their start and end apart: 9, of which 6 were waited for; matrix products, arithmetic and copies ran while one was open for 0% of the time, Pallas kernels for 7%

profile of v8, /device:TPU:1, one launch (start us, length us, event | category | flops | bytes accessed | tf_op | source)
XLA Modules:
  0.0 92.1 jit_solution(12299692216176931755)
XLA Ops:
  0.6 0.0 copy-start
  0.6 0.0 copy-start.2
  0.7 1.1 %copy-done.2 = bf16[256,1024]{1,0:T(8,128)(2,1)S(1)} copy-done((bf16[256,1024]{1,0:T(8,128)(2,1)S(1)}, bf16[256,1024]{1,0:T(8,128)(2,1)}, u32[]{:S(2)}) %copy-start.2) | copy-done | bytes 524312
  1.7 0.1 key_features.1.keys.key_feat.refs_8_
  1.9 0.0 copy-done
  1.9 0.3 states_other.1
  2.2 3.3 %collective-permute-start = (f32[528,128]{1,0:T(8,128)S(1)}, f32[528,128]{1,0:T(8,128)S(1)}, u32[]{:S(2)}, u32[]{:S(2)}) collective-permute-start(f32[528,128]{1,0:T(8,128)S(1)} %states_other.1), channel_id=1, source_target_pairs={{0,4},{4,0},{1,5},{5,1},{2,6},{6,2},{3,7},{7,3},{8,12},{12,8},{9,1... | collective-permute-start | bytes 811016 | tf_op jit(solution)/shard_map/ppermute | solution.py:384
  5.5 0.4 states_own.1
  5.9 0.8 collective-permute-done.extra
  6.7 0.0 copy-start.3
  6.7 0.0 copy-start.1
  6.7 16.6 %all_to_all.20 = f32[16,1,4224]{2,1,0:T(1,128)S(1)} all-to-all(f32[16,1,4224]{2,1,0:T(1,128)S(1)} %bitcast.19), channel_id=1, replica_groups=mesh['top'=2,'chip'=16,'core'=2,'head'=4] {'chip'}, dimensions={0} | all-to-all | bytes 540672 | tf_op jit(solution)/shard_map/all_to_all | solution.py:398
  23.3 1.6 %collective-permute-start.1 = (f32[33,128]{1,0:T(8,128)S(1)}, f32[33,128]{1,0:T(8,128)S(1)}, u32[]{:S(2)}, u32[]{:S(2)}) collective-permute-start(f32[33,128]{1,0:T(8,128)S(1)} %group_total.2), channel_id=1, source_target_pairs={{0,192},{8,200},{16,208},{24,216},{32,224},{40,232},{48,240},{56,2... | collective-permute-start | bytes 50696 | tf_op jit(solution)/shard_map/ppermute | solution.py:411
  24.9 0.0 copy-done.3
  24.9 0.0 copy-done.4
  24.9 0.0 copy-done.1
  24.9 0.0 copy-done.5
  24.9 0.5 prepare.1
  25.5 0.7 inside_forward_own.1
  26.1 1.1 %collective-permute-done.1.other = f32[33,128]{1,0:T(8,128)S(1)} collective-permute-done((f32[33,128]{1,0:T(8,128)S(1)}, f32[33,128]{1,0:T(8,128)S(1)}, u32[]{:S(2)}, u32[]{:S(2)}) %collective-permute-start.1) | collective-permute-done | bytes 16928 | tf_op jit(solution)/shard_map/ppermute | solution.py:411
  27.3 12.0 %all_to_all.21 = f32[16,1,4224]{2,1,0:T(1,128)S(1)} all-to-all(f32[16,1,4224]{2,1,0:T(1,128)S(1)} %bitcast.17), channel_id=1, replica_groups=mesh['top'=2,'chip'=16,'core'=2,'head'=4] {'chip'}, dimensions={0} | all-to-all | bytes 540672 | tf_op jit(solution)/shard_map/all_to_all | solution.py:398
  39.4 0.1 finish.2
  39.4 4.5 %collective-permute-start.2 = (f32[528,128]{1,0:T(8,128)S(1)}, f32[528,128]{1,0:T(8,128)S(1)}, u32[]{:S(2)}, u32[]{:S(2)}) collective-permute-start(f32[528,128]{1,0:T(8,128)S(1)} %get-tuple-element.139), channel_id=1, source_target_pairs={{0,4},{4,0},{1,5},{5,1},{2,6},{6,2},{3,7},{7,3},{8,12},{12,8},{9,1... | collective-permute-start | bytes 811016 | tf_op jit(solution)/shard_map/ppermute | solution.py:384
  44.0 0.7 inside_forward_other.1
  44.6 0.4 attention_own.1
  45.0 0.1 collective-permute-done.2.wire.refs_13_
  45.1 0.5 attention_other.1
  45.7 2.9 %collective-permute-start.5 = (f32[8,256]{1,0:T(8,128)S(1)}, f32[8,256]{1,0:T(8,128)S(1)}, u32[]{:S(2)}, u32[]{:S(2)}) collective-permute-start(f32[8,256]{1,0:T(8,128)S(1)} %get-tuple-element.150.rest_0_), channel_id=1, source_target_pairs={{0,2},{1,3},{2,0},{3,1},{4,6},{5,7},{6,4},{7,5},{8,10},{9,11},{10,... | collective-permute-start | bytes 24584 | tf_op jit(solution)/shard_map/ppermute | solution.py:389
  48.6 0.8 collective-permute-start.4
  49.4 0.0 collective-permute-start.3
  49.4 0.3 collective-permute-done.5.rest_3_
  49.7 2.6 %collective-permute-done.4.rest_2_ = f32[8,256]{1,0:T(8,128)S(1)} collective-permute-done((f32[8,256]{1,0:T(8,128)S(1)}, f32[8,256]{1,0:T(8,128)S(1)}, u32[]{:S(2)}, u32[]{:S(2)}) %collective-permute-start.4) | collective-permute-done | bytes 8224 | tf_op jit(solution)/shard_map/ppermute | solution.py:389
  52.3 0.0 collective-permute-done.3.rest_1_
  52.3 0.6 gradient_other.1
  53.0 1.9 %collective-permute-start.6 = (f32[528,128]{1,0:T(8,128)S(1)}, f32[528,128]{1,0:T(8,128)S(1)}, u32[]{:S(2)}, u32[]{:S(2)}) collective-permute-start(f32[528,128]{1,0:T(8,128)S(1)} %get-tuple-element.154), channel_id=1, source_target_pairs={{0,4},{4,0},{1,5},{5,1},{2,6},{6,2},{3,7},{7,3},{8,12},{12,8},{9,1... | collective-permute-start | bytes 811016 | tf_op jit(solution)/shard_map/ppermute | solution.py:384
  54.8 0.5 gradient_own.1
  55.3 0.5 early_backward.1
  55.8 0.2 collective-permute-done.6.extra
  56.1 12.9 %all_to_all.22 = f32[16,1,4224]{2,1,0:T(1,128)S(1)} all-to-all(f32[16,1,4224]{2,1,0:T(1,128)S(1)} %bitcast.20), channel_id=1, replica_groups=mesh['top'=2,'chip'=16,'core'=2,'head'=4] {'chip'}, dimensions={0} | all-to-all | bytes 540672 | tf_op jit(solution)/shard_map/all_to_all | solution.py:398
  69.0 1.8 %collective-permute-start.7 = (f32[33,128]{1,0:T(8,128)S(1)}, f32[33,128]{1,0:T(8,128)S(1)}, u32[]{:S(2)}, u32[]{:S(2)}) collective-permute-start(f32[33,128]{1,0:T(8,128)S(1)} %group_total.3), channel_id=1, source_target_pairs={{0,192},{8,200},{16,208},{24,216},{32,224},{40,232},{48,240},{56,2... | collective-permute-start | bytes 50696 | tf_op jit(solution)/shard_map/ppermute | solution.py:411
  70.8 2.2 %inside_backward.1 = (bf16[256,1024]{1,0:T(8,128)(2,1)}, bf16[256,1024]{1,0:T(8,128)(2,1)}, f32[256,512]{1,0:T(8,128)S(1)}, f32[256,512]{1,0:T(8,128)S(1)}) custom-call(s32[1]{0:T(128)} %bitcast.core, bf16[256,1024]{1,0:T(8,128)(2,1)S(1)} %copy-done, f32[1,1024]{1,0:T(1,128)S(1)} %bitcast.22, f32[256,128]{1,0:T(8,128)S(1)} %get-tuple-element.177.rest_0_.scale_in, ...), custom_call_target="tpu_custom_call" | custom-call | flops 603979776 | bytes 8540160 | tf_op jit(solution)/shard_map/inside_backward/pallas_call | solution.py:370
  72.9 0.0 collective-permute-done.7.other
  73.0 13.1 %all_to_all.23 = f32[16,1,4224]{2,1,0:T(1,128)S(1)} all-to-all(f32[16,1,4224]{2,1,0:T(1,128)S(1)} %bitcast.18), channel_id=1, replica_groups=mesh['top'=2,'chip'=16,'core'=2,'head'=4] {'chip'}, dimensions={0} | all-to-all | bytes 540672 | tf_op jit(solution)/shard_map/all_to_all | solution.py:398
  86.1 0.1 finish.3
  86.1 3.7 %collective-permute-start.8 = (f32[528,128]{1,0:T(8,128)S(1)}, f32[528,128]{1,0:T(8,128)S(1)}, u32[]{:S(2)}, u32[]{:S(2)}) collective-permute-start(f32[528,128]{1,0:T(8,128)S(1)} %get-tuple-element.203), channel_id=1, source_target_pairs={{0,4},{4,0},{1,5},{5,1},{2,6},{6,2},{3,7},{7,3},{8,12},{12,8},{9,1... | collective-permute-start | bytes 811016 | tf_op jit(solution)/shard_map/ppermute | solution.py:384
  89.8 1.2 %outside_backward_own.1 = (bf16[256,1024]{1,0:T(8,128)(2,1)}, bf16[256,1024]{1,0:T(8,128)(2,1)}) custom-call(s32[1]{0:T(128)} %bitcast.core, f32[256,512]{1,0:T(8,128)S(1)} %get-tuple-element.204.key_slope, bf16[256,1024]{1,0:T(8,128)(2,1)S(1)} %copy-done, bf16[256,512]{1,0:T(8,128)(2,1)S(1)} %get-tuple-element.179.key_feat.refs_1_, ...), custom_call_target="tpu_custom_call" | custom-call | flops 134217728 | bytes 3678208 | tf_op jit(solution)/shard_map/outside_backward_own/pallas_call | solution.py:370
  91.0 0.0 collective-permute-done.8.wire
  91.0 1.2 %outside_backward_other.1 = (bf16[256,1024]{1,0:T(8,128)(2,1)}, bf16[256,1024]{1,0:T(8,128)(2,1)}) custom-call(s32[1]{0:T(128)} %bitcast.core, f32[256,512]{1,0:T(8,128)S(1)} %get-tuple-element.198.key_slope, bf16[256,1024]{1,0:T(8,128)(2,1)S(1)} %copy-done, ...), custom_call_target="tpu_custom_call", output_to_operand_aliasing={{0}: (7, {}), {1}: (8, {})} | custom-call | flops 134217728 | bytes 4726784 | tf_op jit(solution)/shard_map/outside_backward_other/pallas_call | solution.py:370
  (8 shorter events, 0.2 us)
Async XLA Ops:
  0.6 1.3 %copy-start = (bf16[256,1024]{1,0:T(8,128)(2,1)S(1)}, bf16[256,1024]{1,0:T(8,128)(2,1)}, u32[]{:S(2)}) copy-start(bf16[256,1024]{1,0:T(8,128)(2,1)} %values.10) | copy-start | bytes 1572868
  0.6 1.1 %copy-start.2 = (bf16[256,1024]{1,0:T(8,128)(2,1)S(1)}, bf16[256,1024]{1,0:T(8,128)(2,1)}, u32[]{:S(2)}) copy-start(bf16[256,1024]{1,0:T(8,128)(2,1)} %keys.3) | copy-start | bytes 1572868
  2.2 4.5 %collective-permute-start = (f32[528,128]{1,0:T(8,128)S(1)}, f32[528,128]{1,0:T(8,128)S(1)}, u32[]{:S(2)}, u32[]{:S(2)}) collective-permute-start(f32[528,128]{1,0:T(8,128)S(1)} %states_other.1), channel_id=1, source_target_pairs={{0,4},{4,0},{1,5},{5,1},{2,6},{6,2},{3,7},{7,3},{8,12},{12,8},{9,1... | collective-permute-start | bytes 811016 | tf_op jit(solution)/shard_map/ppermute | solution.py:384
  6.7 18.2 %copy-start.3 = (bf16[256,1024]{1,0:T(8,128)(2,1)S(1)}, bf16[256,1024]{1,0:T(8,128)(2,1)}, u32[]{:S(2)}) copy-start(bf16[256,1024]{1,0:T(8,128)(2,1)} %keys.3) | copy-start | bytes 1572868
  6.7 18.2 %copy-start.4 = (bf16[256,1024]{1,0:T(8,128)(2,1)S(1)}, bf16[256,1024]{1,0:T(8,128)(2,1)}, u32[]{:S(2)}) copy-start(bf16[256,1024]{1,0:T(8,128)(2,1)} %out_grad) | copy-start | bytes 1572868
  6.7 18.2 %copy-start.1 = (bf16[256,1024]{1,0:T(8,128)(2,1)S(1)}, bf16[256,1024]{1,0:T(8,128)(2,1)}, u32[]{:S(2)}) copy-start(bf16[256,1024]{1,0:T(8,128)(2,1)} %queries.3) | copy-start | bytes 1572868
  23.3 1.6 %copy-start.5 = (f32[1024]{0:T(1024)S(1)}, f32[1024]{0:T(1024)}, u32[]{:S(2)}) copy-start(f32[1024]{0:T(1024)} %param.8) | copy-start | bytes 12292
  23.3 3.9 %collective-permute-start.1 = (f32[33,128]{1,0:T(8,128)S(1)}, f32[33,128]{1,0:T(8,128)S(1)}, u32[]{:S(2)}, u32[]{:S(2)}) collective-permute-start(f32[33,128]{1,0:T(8,128)S(1)} %group_total.2), channel_id=1, source_target_pairs={{0,192},{8,200},{16,208},{24,216},{32,224},{40,232},{48,240},{56,2... | collective-permute-start | bytes 50696 | tf_op jit(solution)/shard_map/ppermute | solution.py:411
  39.4 5.7 %collective-permute-start.2 = (f32[528,128]{1,0:T(8,128)S(1)}, f32[528,128]{1,0:T(8,128)S(1)}, u32[]{:S(2)}, u32[]{:S(2)}) collective-permute-start(f32[528,128]{1,0:T(8,128)S(1)} %get-tuple-element.139), channel_id=1, source_target_pairs={{0,4},{4,0},{1,5},{5,1},{2,6},{6,2},{3,7},{7,3},{8,12},{12,8},{9,1... | collective-permute-start | bytes 811016 | tf_op jit(solution)/shard_map/ppermute | solution.py:384
  45.7 4.0 %collective-permute-start.5 = (f32[8,256]{1,0:T(8,128)S(1)}, f32[8,256]{1,0:T(8,128)S(1)}, u32[]{:S(2)}, u32[]{:S(2)}) collective-permute-start(f32[8,256]{1,0:T(8,128)S(1)} %get-tuple-element.150.rest_0_), channel_id=1, source_target_pairs={{0,2},{1,3},{2,0},{3,1},{4,6},{5,7},{6,4},{7,5},{8,10},{9,11},{10,... | collective-permute-start | bytes 24584 | tf_op jit(solution)/shard_map/ppermute | solution.py:389
  48.6 3.7 %collective-permute-start.4 = (f32[8,256]{1,0:T(8,128)S(1)}, f32[8,256]{1,0:T(8,128)S(1)}, u32[]{:S(2)}, u32[]{:S(2)}) collective-permute-start(f32[8,256]{1,0:T(8,128)S(1)} %get-tuple-element.150.rest_0_), channel_id=1, source_target_pairs={{1,2},{3,0},{2,1},{0,3},{5,6},{7,4},{6,5},{4,7},{9,10},{11,8},{10,... | collective-permute-start | bytes 24584 | tf_op jit(solution)/shard_map/ppermute | solution.py:389
  49.4 2.9 %collective-permute-start.3 = (f32[8,256]{1,0:T(8,128)S(1)}, f32[8,256]{1,0:T(8,128)S(1)}, u32[]{:S(2)}, u32[]{:S(2)}) collective-permute-start(f32[8,256]{1,0:T(8,128)S(1)} %get-tuple-element.150.rest_0_), channel_id=1, source_target_pairs={{0,1},{2,3},{1,0},{3,2},{4,5},{6,7},{5,4},{7,6},{8,9},{10,11},{9,8... | collective-permute-start | bytes 24584 | tf_op jit(solution)/shard_map/ppermute | solution.py:389
  53.0 3.1 %collective-permute-start.6 = (f32[528,128]{1,0:T(8,128)S(1)}, f32[528,128]{1,0:T(8,128)S(1)}, u32[]{:S(2)}, u32[]{:S(2)}) collective-permute-start(f32[528,128]{1,0:T(8,128)S(1)} %get-tuple-element.154), channel_id=1, source_target_pairs={{0,4},{4,0},{1,5},{5,1},{2,6},{6,2},{3,7},{7,3},{8,12},{12,8},{9,1... | collective-permute-start | bytes 811016 | tf_op jit(solution)/shard_map/ppermute | solution.py:384
  69.0 4.0 %collective-permute-start.7 = (f32[33,128]{1,0:T(8,128)S(1)}, f32[33,128]{1,0:T(8,128)S(1)}, u32[]{:S(2)}, u32[]{:S(2)}) collective-permute-start(f32[33,128]{1,0:T(8,128)S(1)} %group_total.3), channel_id=1, source_target_pairs={{0,192},{8,200},{16,208},{24,216},{32,224},{40,232},{48,240},{56,2... | collective-permute-start | bytes 50696 | tf_op jit(solution)/shard_map/ppermute | solution.py:411
  86.1 4.8 %collective-permute-start.8 = (f32[528,128]{1,0:T(8,128)S(1)}, f32[528,128]{1,0:T(8,128)S(1)}, u32[]{:S(2)}, u32[]{:S(2)}) collective-permute-start(f32[528,128]{1,0:T(8,128)S(1)} %get-tuple-element.203), channel_id=1, source_target_pairs={{0,4},{4,0},{1,5},{5,1},{2,6},{6,2},{3,7},{7,3},{8,12},{12,8},{9,1... | collective-permute-start | bytes 811016 | tf_op jit(solution)/shard_map/ppermute | solution.py:384
